TPU v7x, 32 devices: a whole 2x2x4 slice. The times are simulated.
32 devices in a mesh: dp: 8 (over z, y), tensor: 4 (over x, core).
Axes of the slice: x: 2, y: 2, z: 4, core: 2. Of those that a mesh axis runs over, the one named last changes fastest.
Arguments:
- res_in: bfloat16 [5120, 2048], P(('dp', 'tensor')), may hold values from -30 to 30
- out_grad: bfloat16 [5120, 2048], P(('dp', 'tensor')), may hold values from -6 to 6
- seg_ids: int32 [8, 640], P('dp'), may hold values from 0 to 2, never falling along the last dimension, each value on 1 to 512 neighbouring positions
- tok_counts: int32 [8], P('dp'), may hold values from 320 to 640, as said below
- slot_table: int32 [8, 4, 640], P('dp'), may hold values from -1 to 639, as said below
- slot_gates: float32 [8, 4, 640], P('dp'), may hold values from 0.1 to 1
- attn_gain: bfloat16 [2048], P(('dp', 'tensor')), may hold values from 0.099609375 to 1.8984375
- latent_gain: bfloat16 [512], P(('dp', 'tensor')), may hold values from 0.099609375 to 1.8984375
- ffn_gain: bfloat16 [2048], P(('dp', 'tensor')), may hold values from 0.099609375 to 1.8984375
- w_latent: bfloat16 [2048, 576], P(('dp', 'tensor')), may hold values from -0.125 to 0.125
- w_query: bfloat16 [2048, 3072], P('dp', 'tensor'), may hold values from -0.125 to 0.125
- w_keyval: bfloat16 [512, 4096], P('dp', 'tensor'), may hold values from -0.25 to 0.25
- w_output: bfloat16 [2048, 2048], P('tensor', 'dp'), may hold values from -1 to 1
- w_expert_in: bfloat16 [4, 2, 2048, 1408], P(None, None, 'dp', 'tensor'), may hold values from -0.125 to 0.125
- w_expert_out: bfloat16 [4, 1408, 2048], P(None, 'tensor', 'dp'), may hold values from -0.15625 to 0.15625
- w_shared_in: bfloat16 [2, 2048, 2816], P(None, 'dp', 'tensor'), may hold values from -0.125 to 0.125
- w_shared_out: bfloat16 [2816, 2048], P('tensor', 'dp'), may hold values from -0.109375 to 0.109375
Outputs:
- res_out: bfloat16 [5120, 2048], P(('dp', 'tensor'))
- res_grad: float32 [5120, 2048], P(('dp', 'tensor'))
- attn_gain_grad: float32 [2048], P(('dp', 'tensor'))
- latent_gain_grad: float32 [512], P(('dp', 'tensor'))
- ffn_gain_grad: float32 [2048], P(('dp', 'tensor'))
- w_latent_grad: float32 [2048, 576], P(('dp', 'tensor'))
- w_query_grad: float32 [2048, 3072], P('dp', 'tensor')
- w_keyval_grad: float32 [512, 4096], P('dp', 'tensor')
- w_output_grad: float32 [2048, 2048], P('tensor', 'dp')
- w_expert_in_grad: float32 [4, 2, 2048, 1408], P(None, None, 'dp', 'tensor')
- w_expert_out_grad: float32 [4, 1408, 2048], P(None, 'tensor', 'dp')
- w_shared_in_grad: float32 [2, 2048, 2816], P(None, 'dp', 'tensor')
- w_shared_out_grad: float32 [2816, 2048], P('tensor', 'dp')
Inputs may be any that keep to these rules, and one draw needn't show every extreme that they name: `tok_counts`: token slots at or after a group's count are padding; some group is full. `slot_table`: row e of a group lists in increasing order the tokens of that group routed to expert e, then -1 to the end. Every token below its group's count is routed to exactly 3 experts, padding to none; in every group one expert receives all counted tokens.
All inputs are finite; a program needn't handle non-finite values.
Results may differ from a plain program's by a relative error of at most 0.019.
Values may be sent and summed in bfloat16 or wider, within the bound.
A program may use at most 256 MiB of HBM per device.

v0:
```python
import jax
import jax.numpy as jnp
from jax import lax
from jax.sharding import PartitionSpec as P

D = 2048
H = 16
HD = 128
RD = 64
VD = 128
KR = 512
TOK = 640


NORM_EPS = 1e-06
ROPE_BASE = 50000.0


def rms_factor(values):
    return lax.rsqrt(jnp.mean(values * values, axis=-1, keepdims=True) + NORM_EPS)


def norm_back(grad_out, values, factor, gain_vec):
    scaled = grad_out * gain_vec
    inner_sum = jnp.mean(scaled * values, axis=-1, keepdims=True)
    return (
        factor * (scaled - values * factor * factor * inner_sum),
        jnp.sum(grad_out * values * factor, axis=0),
    )


def rotary_tables(positions):
    half_width = RD // 2
    inv_freq = ROPE_BASE ** (-jnp.arange(half_width, dtype=jnp.float32) / half_width)
    angles = positions.astype(jnp.float32)[:, None] * inv_freq[None, :]
    return (jnp.cos(angles), jnp.sin(angles))


def rotate(values, cosine_table, sine_table):
    half_width = values.shape[-1] // 2
    first_half = values[..., :half_width]
    second_half = values[..., half_width:]
    return jnp.concatenate(
        [
            first_half * cosine_table - second_half * sine_table,
            second_half * cosine_table + first_half * sine_table,
        ],
        axis=-1,
    )


def silu_parts(gate_pre):
    sigma_gate = jax.nn.sigmoid(gate_pre)
    return (gate_pre * sigma_gate, sigma_gate * (1.0 + gate_pre * (1.0 - sigma_gate)))


def gather_attention(w_query, w_keyval, w_output):
    return (
        lax.all_gather(w_query, "dp", axis=0, tiled=True),
        lax.all_gather(w_keyval, "dp", axis=0, tiled=True),
        lax.all_gather(w_output, "dp", axis=1, tiled=True),
    )


def gather_experts(w_expert_in, w_expert_out, w_shared_in, w_shared_out):
    return (
        lax.all_gather(w_expert_in, "dp", axis=2, tiled=True),
        lax.all_gather(w_expert_out, "dp", axis=2, tiled=True),
        lax.all_gather(w_shared_in, "dp", axis=1, tiled=True),
        lax.all_gather(w_shared_out, "dp", axis=1, tiled=True),
    )


def body(
    res_in,
    out_grad,
    seg_ids,
    tok_counts,
    slot_table,
    slot_gates,
    attn_gain,
    latent_gain,
    ffn_gain,
    w_latent,
    w_query,
    w_keyval,
    w_output,
    w_expert_in,
    w_expert_out,
    w_shared_in,
    w_shared_out,
):
    f32 = jnp.float32
    bf16 = jnp.bfloat16
    n_tensor = lax.axis_size("tensor")
    local_rows = res_in.shape[0]
    row_start = lax.axis_index("tensor") * local_rows
    local_heads = H // n_tensor
    score_scale = (HD + RD) ** (-0.5)
    latent_full, attn_gain_full, latent_gain_full, ffn_gain_full = (
        lax.all_gather(w_latent, ("dp", "tensor"), axis=0, tiled=True),
        lax.all_gather(attn_gain, ("dp", "tensor"), axis=0, tiled=True),
        lax.all_gather(latent_gain, ("dp", "tensor"), axis=0, tiled=True),
        lax.all_gather(ffn_gain, ("dp", "tensor"), axis=0, tiled=True),
    )
    query_full, keyval_full, output_full = gather_attention(w_query, w_keyval, w_output)
    segment_row = seg_ids[0]
    token_ids = jnp.arange(TOK, dtype=jnp.int32)
    positions = token_ids - jnp.sum(
        (segment_row[None, :] < segment_row[:, None]).astype(jnp.int32), axis=1
    )
    cos_all, sin_all = rotary_tables(positions)
    cos_local = lax.dynamic_slice_in_dim(cos_all, row_start, local_rows, 0)
    sin_local = lax.dynamic_slice_in_dim(sin_all, row_start, local_rows, 0)
    local_ids = row_start + jnp.arange(local_rows, dtype=jnp.int32)
    valid_rows = (local_ids < tok_counts[0]).astype(f32)[:, None]
    allowed = (segment_row[:, None] == segment_row[None, :]) & (
        token_ids[None, :] <= token_ids[:, None]
    )
    resid_in = res_in.astype(f32)
    in_factor = rms_factor(resid_in)
    normed_in = (resid_in * in_factor * attn_gain_full).astype(bf16)
    latent_raw = jnp.dot(normed_in, latent_full, preferred_element_type=f32)
    latent_c = latent_raw[:, :KR]
    latent_factor = rms_factor(latent_c)
    latent_norm = (latent_c * latent_factor * latent_gain_full).astype(bf16)
    rope_key = rotate(latent_raw[:, KR:], cos_local, sin_local).astype(bf16)
    normed_all, latent_all = (
        lax.all_gather(normed_in, "tensor", axis=0, tiled=True),
        lax.all_gather(
            jnp.concatenate([latent_norm, rope_key], axis=1), "tensor", axis=0, tiled=True
        ),
    )
    latent_all_norm = latent_all[:, :KR]
    rope_all = latent_all[:, KR:]
    query_raw = jnp.dot(normed_all, query_full, preferred_element_type=f32).reshape(
        TOK, local_heads, HD + RD
    )
    query_final = jnp.concatenate(
        [
            query_raw[..., :HD],
            rotate(query_raw[..., HD:], cos_all[:, None, :], sin_all[:, None, :]),
        ],
        axis=-1,
    ).astype(bf16)
    keyval = (
        jnp.dot(latent_all_norm, keyval_full, preferred_element_type=f32)
        .astype(bf16)
        .reshape(TOK, local_heads, HD + VD)
    )
    key_nope = keyval[..., :HD]
    values_all = keyval[..., HD:]

    def attention_scores():
        raw_scores = jnp.einsum(
            "qhd,khd->hqk", query_final[..., :HD], key_nope, preferred_element_type=f32
        )
        raw_scores = raw_scores + jnp.einsum(
            "qhr,kr->hqk", query_final[..., HD:], rope_all, preferred_element_type=f32
        )
        return jnp.where(allowed[None], raw_scores * score_scale, -1e30)

    scores = attention_scores()
    top_score = jnp.max(scores, axis=-1, keepdims=True)
    log_total = top_score + jnp.log(jnp.sum(jnp.exp(scores - top_score), axis=-1, keepdims=True))
    probs_all = jnp.exp(scores - log_total)
    probs_low = probs_all.astype(bf16)
    attn_mix = (
        jnp.einsum("hqk,khd->qhd", probs_low, values_all, preferred_element_type=f32)
        .astype(bf16)
        .reshape(TOK, local_heads * VD)
    )
    attn_part = jnp.dot(attn_mix, output_full, preferred_element_type=f32)
    attn_out = lax.psum_scatter(attn_part, "tensor", scatter_dimension=0, tiled=True)
    mid_resid = resid_in + valid_rows * attn_out
    mid_factor = rms_factor(mid_resid)
    normed_mid = (mid_resid * mid_factor * ffn_gain_full).astype(bf16)
    expert_in_full, expert_out_full, shared_in_full, shared_out_full = gather_experts(
        w_expert_in, w_expert_out, w_shared_in, w_shared_out
    )
    mid_all = lax.all_gather(normed_mid, "tensor", axis=0, tiled=True)
    shared_gate = jnp.dot(mid_all, shared_in_full[0], preferred_element_type=f32)
    shared_up = jnp.dot(mid_all, shared_in_full[1], preferred_element_type=f32)
    shared_silu, shared_slope = silu_parts(shared_gate)
    shared_hidden = (shared_silu * shared_up).astype(bf16)
    ffn_part = jnp.dot(shared_hidden, shared_out_full, preferred_element_type=f32)
    group_slots = slot_table[0]
    slot_used = group_slots >= 0
    slot_rows = jnp.where(slot_used, group_slots, 0)
    slot_weight = jnp.where(slot_used, slot_gates[0], 0.0)
    target = jnp.where(slot_used, group_slots, TOK).reshape(-1)
    expert_rows = mid_all[slot_rows]
    expert_gate = jnp.einsum(
        "etd,edf->etf", expert_rows, expert_in_full[:, 0], preferred_element_type=f32
    )
    expert_up = jnp.einsum(
        "etd,edf->etf", expert_rows, expert_in_full[:, 1], preferred_element_type=f32
    )
    expert_silu, expert_slope = silu_parts(expert_gate)
    expert_hidden = (expert_silu * expert_up).astype(bf16)
    expert_out = jnp.einsum(
        "etf,efd->etd", expert_hidden, expert_out_full, preferred_element_type=f32
    )
    ffn_part = ffn_part.at[target].add(
        (expert_out * slot_weight[..., None]).reshape(-1, D), mode="drop"
    )
    ffn_out = lax.psum_scatter(
        ffn_part.astype(jnp.bfloat16), "tensor", scatter_dimension=0, tiled=True
    ).astype(jnp.float32)
    res_out = (mid_resid + valid_rows * ffn_out).astype(bf16)
    grad_in = out_grad.astype(f32)
    ffn_grad = (valid_rows * grad_in).astype(bf16)
    ffn_grad_all = lax.all_gather(ffn_grad, "tensor", axis=0, tiled=True)
    expert_in_full, expert_out_full, shared_in_full, shared_out_full = gather_experts(
        w_expert_in, w_expert_out, w_shared_in, w_shared_out
    )
    shared_hidden_grad = jnp.einsum(
        "td,fd->tf", ffn_grad_all, shared_out_full, preferred_element_type=f32
    )
    shared_pair_grad = jnp.stack(
        [
            (shared_hidden_grad * shared_up * shared_slope).astype(bf16),
            (shared_hidden_grad * shared_silu).astype(bf16),
        ],
        axis=0,
    )
    shared_out_wgrad = jnp.einsum(
        "tf,td->fd", shared_hidden, ffn_grad_all, preferred_element_type=f32
    )
    shared_in_wgrad = jnp.einsum(
        "td,ktf->kdf", mid_all, shared_pair_grad, preferred_element_type=f32
    )
    mid_all_grad = jnp.einsum(
        "ktf,kdf->td", shared_pair_grad, shared_in_full, preferred_element_type=f32
    )
    expert_out_grad = (ffn_grad_all[slot_rows].astype(f32) * slot_weight[..., None]).astype(bf16)
    expert_hidden_grad = jnp.einsum(
        "etd,efd->etf", expert_out_grad, expert_out_full, preferred_element_type=f32
    )
    expert_pair_grad = jnp.stack(
        [
            (expert_hidden_grad * expert_up * expert_slope).astype(bf16),
            (expert_hidden_grad * expert_silu).astype(bf16),
        ],
        axis=1,
    )
    expert_out_wgrad = jnp.einsum(
        "etf,etd->efd", expert_hidden, expert_out_grad, preferred_element_type=f32
    )
    expert_in_wgrad = jnp.einsum(
        "etd,ektf->ekdf", expert_rows, expert_pair_grad, preferred_element_type=f32
    )
    rows_back = jnp.einsum(
        "ektf,ekdf->etd", expert_pair_grad, expert_in_full, preferred_element_type=f32
    )
    mid_all_grad = mid_all_grad.at[target].add(rows_back.reshape(-1, D), mode="drop")
    expert_in_owned, expert_out_owned, shared_in_owned, shared_out_owned = (
        lax.psum_scatter(
            expert_in_wgrad.astype(jnp.bfloat16), "dp", scatter_dimension=2, tiled=True
        ).astype(jnp.float32),
        lax.psum_scatter(
            expert_out_wgrad.astype(jnp.bfloat16), "dp", scatter_dimension=2, tiled=True
        ).astype(jnp.float32),
        lax.psum_scatter(
            shared_in_wgrad.astype(jnp.bfloat16), "dp", scatter_dimension=1, tiled=True
        ).astype(jnp.float32),
        lax.psum_scatter(
            shared_out_wgrad.astype(jnp.bfloat16), "dp", scatter_dimension=1, tiled=True
        ).astype(jnp.float32),
    )
    mid_grad_local = lax.psum_scatter(mid_all_grad, "tensor", scatter_dimension=0, tiled=True)
    mid_back, ffn_gain_part = norm_back(mid_grad_local, mid_resid, mid_factor, ffn_gain_full)
    mid_grad = grad_in + mid_back
    attn_grad = (valid_rows * mid_grad).astype(bf16)
    attn_grad_all = lax.all_gather(attn_grad, "tensor", axis=0, tiled=True)
    query_full, keyval_full, output_full = gather_attention(w_query, w_keyval, w_output)
    output_wgrad = jnp.einsum("tv,td->vd", attn_mix, attn_grad_all, preferred_element_type=f32)
    mix_grad = (
        jnp.einsum("td,vd->tv", attn_grad_all, output_full, preferred_element_type=f32)
        .astype(bf16)
        .reshape(TOK, local_heads, VD)
    )
    scores = attention_scores()
    probs_all = jnp.exp(scores - log_total)
    probs_low = probs_all.astype(bf16)
    probs_grad = jnp.einsum("qhd,khd->hqk", mix_grad, values_all, preferred_element_type=f32)
    value_grad = jnp.einsum("hqk,qhd->khd", probs_low, mix_grad, preferred_element_type=f32)
    scores_grad = (
        probs_all * (probs_grad - jnp.sum(probs_all * probs_grad, axis=-1, keepdims=True))
    ).astype(bf16)
    query_nope_grad = (
        jnp.einsum("hqk,khd->qhd", scores_grad, key_nope, preferred_element_type=f32) * score_scale
    )
    query_rope_grad = (
        jnp.einsum("hqk,kr->qhr", scores_grad, rope_all, preferred_element_type=f32) * score_scale
    )
    key_nope_grad = (
        jnp.einsum("hqk,qhd->khd", scores_grad, query_final[..., :HD], preferred_element_type=f32)
        * score_scale
    )
    rope_key_grad = (
        jnp.einsum("hqk,qhr->kr", scores_grad, query_final[..., HD:], preferred_element_type=f32)
        * score_scale
    )
    query_grad = (
        jnp.concatenate(
            [query_nope_grad, rotate(query_rope_grad, cos_all[:, None, :], -sin_all[:, None, :])],
            axis=-1,
        )
        .astype(bf16)
        .reshape(TOK, local_heads * (HD + RD))
    )
    keyval_grad = (
        jnp.concatenate([key_nope_grad, value_grad], axis=-1)
        .astype(bf16)
        .reshape(TOK, local_heads * (HD + VD))
    )
    query_wgrad = jnp.einsum("td,tq->dq", normed_all, query_grad, preferred_element_type=f32)
    keyval_wgrad = jnp.einsum("tc,tk->ck", latent_all_norm, keyval_grad, preferred_element_type=f32)
    normed_part = jnp.einsum("tq,dq->td", query_grad, query_full, preferred_element_type=f32)
    latent_part = jnp.concatenate(
        [
            jnp.einsum("tk,ck->tc", keyval_grad, keyval_full, preferred_element_type=f32),
            rope_key_grad,
        ],
        axis=1,
    )
    normed_grad_local, latent_grad_local = (
        lax.psum_scatter(normed_part, "tensor", scatter_dimension=0, tiled=True),
        lax.psum_scatter(latent_part, "tensor", scatter_dimension=0, tiled=True),
    )
    query_owned, keyval_owned, output_owned = (
        lax.psum_scatter(
            query_wgrad.astype(jnp.bfloat16), "dp", scatter_dimension=0, tiled=True
        ).astype(jnp.float32),
        lax.psum_scatter(
            keyval_wgrad.astype(jnp.bfloat16), "dp", scatter_dimension=0, tiled=True
        ).astype(jnp.float32),
        lax.psum_scatter(
            output_wgrad.astype(jnp.bfloat16), "dp", scatter_dimension=1, tiled=True
        ).astype(jnp.float32),
    )
    latent_c_grad, latent_gain_part = norm_back(
        latent_grad_local[:, :KR], latent_c, latent_factor, latent_gain_full
    )
    rope_raw_grad = rotate(latent_grad_local[:, KR:], cos_local, -sin_local)
    latent_raw_grad = jnp.concatenate([latent_c_grad, rope_raw_grad], axis=1).astype(bf16)
    latent_wgrad = jnp.einsum("td,tk->dk", normed_in, latent_raw_grad, preferred_element_type=f32)
    normed_grad = normed_grad_local + jnp.einsum(
        "tk,dk->td", latent_raw_grad, latent_full, preferred_element_type=f32
    )
    in_back, attn_gain_part = norm_back(normed_grad, resid_in, in_factor, attn_gain_full)
    res_grad = mid_grad + in_back
    latent_owned, attn_gain_grad, latent_gain_grad, ffn_gain_grad = (
        lax.psum_scatter(latent_wgrad, ("dp", "tensor"), scatter_dimension=0, tiled=True),
        lax.psum_scatter(attn_gain_part, ("dp", "tensor"), scatter_dimension=0, tiled=True),
        lax.psum_scatter(latent_gain_part, ("dp", "tensor"), scatter_dimension=0, tiled=True),
        lax.psum_scatter(ffn_gain_part, ("dp", "tensor"), scatter_dimension=0, tiled=True),
    )
    return (
        res_out,
        res_grad,
        attn_gain_grad,
        latent_gain_grad,
        ffn_gain_grad,
        latent_owned,
        query_owned,
        keyval_owned,
        output_owned,
        expert_in_owned,
        expert_out_owned,
        shared_in_owned,
        shared_out_owned,
    )


def solution(mesh):
    placed = (
        P(("dp", "tensor"), None),
        P(("dp", "tensor"), None),
        P("dp", None),
        P("dp"),
        P("dp", None, None),
        P("dp", None, None),
        P(("dp", "tensor")),
        P(("dp", "tensor")),
        P(("dp", "tensor")),
        P(("dp", "tensor"), None),
        P("dp", "tensor"),
        P("dp", "tensor"),
        P("tensor", "dp"),
        P(None, None, "dp", "tensor"),
        P(None, "tensor", "dp"),
        P(None, "dp", "tensor"),
        P("tensor", "dp"),
    )
    return jax.shard_map(
        body,
        mesh=mesh,
        in_specs=placed,
        out_specs=(
            P(("dp", "tensor"), None),
            P(("dp", "tensor"), None),
            P(("dp", "tensor")),
            P(("dp", "tensor")),
            P(("dp", "tensor")),
            P(("dp", "tensor"), None),
            P("dp", "tensor"),
            P("dp", "tensor"),
            P("tensor", "dp"),
            P(None, None, "dp", "tensor"),
            P(None, "tensor", "dp"),
            P(None, "dp", "tensor"),
            P("tensor", "dp"),
        ),
        check_vma=False,
    )
```

profile of v0, /device:TPU:0, one launch (start us, length us, event | category | flops | bytes accessed | tf_op | source)
XLA Modules:
  0.0 1957.5 jit_solution(11171231999007672449)
XLA Ops:
  11.3 42.3 %all-reduce.7 = (bf16[2048]{0:T(1024)(128)(2,1)S(1)}, bf16[512]{0:T(512)(128)(2,1)S(1)}, bf16[2048]{0:T(1024)(128)(2,1)S(1)}) all-reduce(bf16[2048]{0:T(1024)(128)(2,1)S(1)} %dynamic-update-slice, bf16[512]{0:T(512)(128)(2,1)S(1)} %dynamic-update-slice.1, ...), channel_id=1, replica_groups=mesh['dp'=8,'tensor'=4] {'dp','tensor'}, use_global_device_ids=true, to_apply=%add | all-reduce | flops 4608 | bytes 18432
  84.1 28.7 %all-gather.15.cloned.1.call-done = bf16[512,1024]{1,0:T(8,128)(2,1)} async-done(((bf16[64,1024]{1,0:T(8,128)(2,1)}), bf16[512,1024]{1,0:T(8,128)(2,1)}) %all-gather.15.cloned.1.call-update) | async-done | bytes 1048592 | tf_op jit(solution)/shard_map/all_gather | solution.py:60
  139.3 62.5 %all-gather.19.cloned.1.call-done = bf16[2048,768]{1,0:T(8,128)(2,1)} async-done(((bf16[256,768]{1,0:T(8,128)(2,1)}), bf16[2048,768]{1,0:T(8,128)(2,1)}) %all-gather.19.cloned.1.call-update) | async-done | bytes 3145744 | tf_op jit(solution)/shard_map/all_gather | solution.py:59
  215.9 37.5 %all-gather.21.cloned.1.call-done = bf16[512,2048]{1,0:T(8,128)(2,1)} async-done(((bf16[512,256]{1,0:T(8,128)(2,1)}), bf16[512,2048]{1,0:T(8,128)(2,1)}) %all-gather.21.cloned.1.call-update) | async-done | bytes 2097168 | tf_op jit(solution)/shard_map/all_gather | solution.py:61
  260.1 48.6 %reduce-scatter.16.cloned.1.call-done = f32[160,2048]{1,0:T(8,128)} async-done(((f32[640,2048]{1,0:T(8,128)}), f32[160,2048]{1,0:T(8,128)}) %reduce-scatter.16.cloned.1.call-update) | async-done | bytes 1310736 | tf_op jit(solution)/shard_map/reduce_scatter | solution.py:174
  339.1 22.3 %gather_fusion = bf16[2560,2048]{1,0:T(8,128)(2,1)} fusion(bf16[640,2048]{1,0:T(8,128)(2,1)} %all-gather.23.cloned.1.call-done, s32[3072]{0:T(1024)S(1)} %pad_clamp_fusion), kind=kCustom, calls=%fused_computation | custom fusion | bytes 20981760 | tf_op jit(solution)/shard_map/gather | solution.py:192
  389.2 73.6 %all-gather.25.cloned.1.call-done = bf16[2,2048,704]{1,2,0:T(8,128)(2,1)} async-done(((bf16[2,256,704]{1,2,0:T(8,128)(2,1)}), bf16[2,2048,704]{1,2,0:T(8,128)(2,1)}) %all-gather.25.cloned.1.call-update) | async-done | bytes 5767184 | tf_op jit(solution)/shard_map/all_gather | solution.py:69
  472.1 50.9 %all-gather.27.cloned.1.call-done = bf16[704,2048]{1,0:T(8,128)(2,1)} async-done(((bf16[704,256]{1,0:T(8,128)(2,1)}), bf16[704,2048]{1,0:T(8,128)(2,1)}) %all-gather.27.cloned.1.call-update) | async-done | bytes 2883600 | tf_op jit(solution)/shard_map/all_gather | solution.py:70
  541.2 75.9 %all-gather.31.cloned.1.call-done = bf16[4,352,2048]{2,1,0:T(8,128)(2,1)} async-done(((bf16[4,352,256]{2,1,0:T(8,128)(2,1)}), bf16[4,352,2048]{2,1,0:T(8,128)(2,1)}) %all-gather.31.cloned.1.call-update) | async-done | bytes 5767184 | tf_op jit(solution)/shard_map/all_gather | solution.py:68
  629.7 152.1 %all-gather.29.cloned.1.call-done = bf16[4,2,2048,352]{2,3,0,1:T(8,128)(2,1)} async-done(((bf16[4,2,256,352]{2,3,0,1:T(8,128)(2,1)}), bf16[4,2,2048,352]{2,3,0,1:T(8,128)(2,1)}) %all-gather.29.cloned.1.call-update) | async-done | bytes 11534352 | tf_op jit(solution)/shard_map/all_gather | solution.py:67
  822.6 38.3 %scatter_fusion.1 = f32[640,2048]{1,0:T(8,128)} fusion(f32[640,2048]{1,0:T(8,128)} %convolution_bitcast_fusion, s32[2560]{0:T(1024)S(1)} %fusion.52, f32[2560,2048]{1,0:T(8,128)} %bitcast.133), kind=kCustom, calls=%fused_computation.3 | custom fusion | flops 5242880 | bytes 62924800 | tf_op jit(solution)/shard_map/scatter-add | solution.py:256
  878.6 38.7 %scatter_fusion = f32[640,2048]{1,0:T(8,128)} fusion(f32[640,2048]{1,0:T(8,128)} %fusion.67, s32[2560]{0:T(1024)S(1)} %fusion.52, f32[2560,2048]{1,0:T(8,128)} %bitcast.132), kind=kCustom, calls=%fused_computation.2 | custom fusion | flops 5242880 | bytes 62924800 | tf_op jit(solution)/shard_map/scatter-add | solution.py:204
  924.8 30.2 %reduce-scatter.18.cloned.1.call-done = bf16[160,2048]{1,0:T(8,128)(2,1)} async-done(((bf16[640,2048]{1,0:T(8,128)(2,1)}), bf16[160,2048]{1,0:T(8,128)(2,1)}) %reduce-scatter.18.cloned.1.call-update) | async-done | bytes 655376 | tf_op jit(solution)/shard_map/reduce_scatter | solution.py:207
  958.1 25.5 %all-gather.35.cloned.1.call-done = bf16[640,2048]{1,0:T(8,128)(2,1)} async-done(((bf16[160,2048]{1,0:T(8,128)(2,1)}), bf16[640,2048]{1,0:T(8,128)(2,1)}) %all-gather.35.cloned.1.call-update) | async-done | bytes 2621456 | tf_op jit(solution)/shard_map/all_gather | solution.py:275
  1083.5 29.9 %reduce-scatter.38.cloned.1.call-done = bf16[704,256]{1,0:T(8,128)(2,1)} async-done(((bf16[704,2048]{1,0:T(8,128)(2,1)}), bf16[704,256]{1,0:T(8,128)(2,1)}) %reduce-scatter.38.cloned.1.call-update) | async-done | bytes 360464 | tf_op jit(solution)/shard_map/reduce_scatter | solution.py:267
  1115.3 111.2 %reduce-scatter.36.cloned.1.call-done = bf16[2,256,704]{1,2,0:T(8,128)(2,1)} async-done(((bf16[2,2048,704]{1,2,0:T(8,128)(2,1)}), bf16[2,256,704]{1,2,0:T(8,128)(2,1)}) %reduce-scatter.36.cloned.1.call-update) | async-done | bytes 720912 | tf_op jit(solution)/shard_map/reduce_scatter | solution.py:264
  1228.8 111.5 %reduce-scatter.34.cloned.1.call-done = bf16[4,352,256]{2,1,0:T(8,128)(2,1)} async-done(((bf16[4,352,2048]{2,1,0:T(8,128)(2,1)}), bf16[4,352,256]{2,1,0:T(8,128)(2,1)}) %reduce-scatter.34.cloned.1.call-update) | async-done | bytes 720912 | tf_op jit(solution)/shard_map/reduce_scatter | solution.py:261
  1342.6 64.1 %reduce-scatter.28.cloned.1.call-done = bf16[64,1024]{1,0:T(8,128)(2,1)} async-done(((bf16[512,1024]{1,0:T(8,128)(2,1)}), bf16[64,1024]{1,0:T(8,128)(2,1)}) %reduce-scatter.28.cloned.1.call-update) | async-done | bytes 131088 | tf_op jit(solution)/shard_map/reduce_scatter | solution.py:336
  1408.3 69.4 %reduce-scatter.30.cloned.1.call-done = bf16[512,256]{1,0:T(8,128)(2,1)} async-done(((bf16[512,2048]{1,0:T(8,128)(2,1)}), bf16[512,256]{1,0:T(8,128)(2,1)}) %reduce-scatter.30.cloned.1.call-update) | async-done | bytes 262160 | tf_op jit(solution)/shard_map/reduce_scatter | solution.py:339
  1479.5 75.9 %reduce-scatter.26.cloned.1.call-done = bf16[256,768]{1,0:T(8,128)(2,1)} async-done(((bf16[2048,768]{1,0:T(8,128)(2,1)}), bf16[256,768]{1,0:T(8,128)(2,1)}) %reduce-scatter.26.cloned.1.call-update) | async-done | bytes 393232 | tf_op jit(solution)/shard_map/reduce_scatter | solution.py:333
  1557.4 194.4 %reduce-scatter.32.cloned.1.call-done = bf16[4,2,256,352]{2,3,1,0:T(8,128)(2,1)} async-done(((bf16[4,2,2048,352]{2,3,1,0:T(8,128)(2,1)}), bf16[4,2,256,352]{2,3,1,0:T(8,128)(2,1)}) %reduce-scatter.32.cloned.1.call-update) | async-done | bytes 1441808 | tf_op jit(solution)/shard_map/reduce_scatter | solution.py:258
  1754.9 49.8 %reduce-scatter.22.cloned.1.call-done = f32[160,2048]{1,0:T(8,128)} async-done(((f32[640,2048]{1,0:T(8,128)}), f32[160,2048]{1,0:T(8,128)}) %reduce-scatter.22.cloned.1.call-update) | async-done | bytes 1310736 | tf_op jit(solution)/shard_map/reduce_scatter | solution.py:329
  1809.7 40.5 %all-reduce.6 = (f32[2048]{0:T(1024)S(1)}, f32[512]{0:T(512)S(1)}, f32[2048]{0:T(1024)S(1)}) all-reduce(f32[2048]{0:T(1024)} %get-tuple-element.15, f32[512]{0:T(512)} %get-tuple-element.17, f32[2048]{0:T(1024)S(1)} %get-tuple-element.13), channel_id=7, replica_groups=mesh['dp'=8,'tensor'=4] {'dp','tensor'}, use_global_device_ids=true, to_apply=%region_18.19.clone | all-reduce | flops 4608 | bytes 36864
  1856.1 94.6 %reduce-scatter.24.cloned.1.call-done = f32[64,576]{1,0:T(8,128)} async-done(((f32[2048,576]{1,0:T(8,128)}), f32[64,576]{1,0:T(8,128)}) %reduce-scatter.24.cloned.1.call-update) | async-done | bytes 147472 | tf_op jit(solution)/shard_map/reduce_scatter | solution.py:355
  (317 shorter events, 373.1 us)
Async XLA Ops:
  7.2 64.4 %all-gather.13.cloned.1.call-start = ((), (), s32[]{:S(2)}) async-start(), calls=%async_computation.13 | async-start | bytes 2703360 | tf_op jit(solution)/shard_map/all_gather | solution.py:101
  7.9 104.9 %all-gather.15.cloned.1.call-start = ((), (), s32[]{:S(2)}) async-start(), calls=%async_computation.14 | async-start | bytes 1179648 | tf_op jit(solution)/shard_map/all_gather | solution.py:60
  8.7 130.6 %all-gather.17.cloned.1.call-start = ((), (), s32[]{:S(2)}) async-start(), calls=%async_computation.15 | async-start | bytes 3276800 | tf_op jit(solution)/shard_map/all_gather | solution.py:129
  57.6 144.2 %all-gather.19.cloned.1.call-start = ((), (), s32[]{:S(2)}) async-start(), calls=%async_computation.16 | async-start | bytes 3538944 | tf_op jit(solution)/shard_map/all_gather | solution.py:59
  58.2 195.2 %all-gather.21.cloned.1.call-start = ((), (), s32[]{:S(2)}) async-start(), calls=%async_computation.17 | async-start | bytes 2359296 | tf_op jit(solution)/shard_map/all_gather | solution.py:61
  58.8 249.9 %reduce-scatter.16.cloned.1.call-start = ((), (), s32[]{:S(2)}) async-start(), calls=%async_computation.18 | async-start | bytes 6553600 | tf_op jit(solution)/shard_map/reduce_scatter | solution.py:174
  258.9 80.1 %all-gather.23.cloned.1.call-start = ((), (), s32[]{:S(2)}) async-start(), calls=%async_computation.19 | async-start | bytes 3276800 | tf_op jit(solution)/shard_map/all_gather | solution.py:181
  314.1 148.7 %all-gather.25.cloned.1.call-start = ((), (), s32[]{:S(2)}) async-start(), calls=%async_computation.20 | async-start | bytes 6488064 | tf_op jit(solution)/shard_map/all_gather | solution.py:69
  314.8 208.2 %all-gather.27.cloned.1.call-start = ((), (), s32[]{:S(2)}) async-start(), calls=%async_computation.21 | async-start | bytes 3244032 | tf_op jit(solution)/shard_map/all_gather | solution.py:70
  315.4 301.7 %all-gather.31.cloned.1.call-start = ((), (), s32[]{:S(2)}) async-start(), calls=%async_computation.23 | async-start | bytes 6488064 | tf_op jit(solution)/shard_map/all_gather | solution.py:68
  316.2 465.6 %all-gather.29.cloned.1.call-start = ((), (), s32[]{:S(2)}) async-start(), calls=%async_computation.22 | async-start | bytes 12976128 | tf_op jit(solution)/shard_map/all_gather | solution.py:67
  317.5 604.4 %reduce-scatter.20.cloned.1.call-start = ((), (), s32[]{:S(2)}) async-start(), calls=%async_computation.26 | async-start | bytes 6553600 | tf_op jit(solution)/shard_map/reduce_scatter | solution.py:271
  860.9 94.1 %reduce-scatter.18.cloned.1.call-start = ((), (), s32[]{:S(2)}) async-start(), calls=%async_computation.24 | async-start | bytes 3276800 | tf_op jit(solution)/shard_map/reduce_scatter | solution.py:207
  921.7 61.8 %all-gather.35.cloned.1.call-start = ((), (), s32[]{:S(2)}) async-start(), calls=%async_computation.27 | async-start | bytes 3276800 | tf_op jit(solution)/shard_map/all_gather | solution.py:275
  957.9 117.0 %reduce-scatter.40.cloned.1.call-start = ((), (), s32[]{:S(2)}) async-start(), calls=%async_computation.37 | async-start | bytes 2048000 | tf_op jit(solution)/shard_map/reduce_scatter | solution.py:330
  1008.3 105.1 %reduce-scatter.38.cloned.1.call-start = ((), (), s32[]{:S(2)}) async-start(), calls=%async_computation.36 | async-start | bytes 3244032 | tf_op jit(solution)/shard_map/reduce_scatter | solution.py:267
  1012.4 214.1 %reduce-scatter.36.cloned.1.call-start = ((), (), s32[]{:S(2)}) async-start(), calls=%async_computation.35 | async-start | bytes 6488064 | tf_op jit(solution)/shard_map/reduce_scatter | solution.py:264
  1022.3 317.9 %reduce-scatter.34.cloned.1.call-start = ((), (), s32[]{:S(2)}) async-start(), calls=%async_computation.34 | async-start | bytes 6488064 | tf_op jit(solution)/shard_map/reduce_scatter | solution.py:261
  1034.9 371.8 %reduce-scatter.28.cloned.1.call-start = ((), (), s32[]{:S(2)}) async-start(), calls=%async_computation.31 | async-start | bytes 1179648 | tf_op jit(solution)/shard_map/reduce_scatter | solution.py:336
  1038.6 439.2 %reduce-scatter.30.cloned.1.call-start = ((), (), s32[]{:S(2)}) async-start(), calls=%async_computation.32 | async-start | bytes 2359296 | tf_op jit(solution)/shard_map/reduce_scatter | solution.py:339
  1043.9 511.6 %reduce-scatter.26.cloned.1.call-start = ((), (), s32[]{:S(2)}) async-start(), calls=%async_computation.30 | async-start | bytes 3538944 | tf_op jit(solution)/shard_map/reduce_scatter | solution.py:333
  1051.6 700.1 %reduce-scatter.32.cloned.1.call-start = ((), (), s32[]{:S(2)}) async-start(), calls=%async_computation.33 | async-start | bytes 12976128 | tf_op jit(solution)/shard_map/reduce_scatter | solution.py:258
  1068.0 736.8 %reduce-scatter.22.cloned.1.call-start = ((), (), s32[]{:S(2)}) async-start(), calls=%async_computation.28 | async-start | bytes 6553600 | tf_op jit(solution)/shard_map/reduce_scatter | solution.py:329
  1074.8 875.9 %reduce-scatter.24.cloned.1.call-start = ((), (), s32[]{:S(2)}) async-start(), calls=%async_computation.29 | async-start | bytes 5406720 | tf_op jit(solution)/shard_map/reduce_scatter | solution.py:355
  (74 other events, 2570.5 us)
Sparse Core Ops, SparseCore 0:
  10.9 60.6 all-gather.12
  73.7 39.0 all-gather.14
  141.3 60.4 all-gather.18
  203.7 49.6 all-gather.20
  259.1 49.5 reduce-scatter.15
  313.5 25.5 all-gather.22
  341.3 25.5 all-gather.32
  369.1 93.5 all-gather.24
  464.8 58.1 all-gather.26
  525.3 91.7 all-gather.30
  619.8 161.9 all-gather.28
  861.1 49.5 reduce-scatter.19
  921.9 33.1 reduce-scatter.17
  958.0 25.5 all-gather.34
  1008.5 28.5 reduce-scatter.39
  1041.1 72.3 reduce-scatter.37
  1116.9 109.5 reduce-scatter.35
  1230.2 110.0 reduce-scatter.33
  1343.5 63.1 reduce-scatter.27
  1410.7 67.0 reduce-scatter.29
  1481.8 73.6 reduce-scatter.25
  1559.5 192.2 reduce-scatter.31
  1754.3 50.4 reduce-scatter.21
  1807.7 143.0 reduce-scatter.23
  (1 shorter events, 24.2 us)
where the time goes:
time: 1960 us
  waiting for transfers between devices  1450 us (74%)
  matrix products  204 us (10%)
  other arithmetic  122 us (6%)
  blocking collectives  91.7 us (5%)
  local copies, waits for them, and re-layouts  72.9 us (4%)
    reduce_scatter x1, waiting for transfers between devices, body(): lax.psum_scatter(expert_in_wgrad.astype(jnp.bfloat16), 'dp', scatter_dime...  194 us
    all_gather x1, waiting for transfers between devices, gather_experts(): lax.all_gather(w_expert_in, 'dp', axis=2, tiled=True)  152 us
    reduce_scatter x1, waiting for transfers between devices, body(): lax.psum_scatter(expert_out_wgrad.astype(jnp.bfloat16), 'dp', scatter_dim...  111 us
    reduce_scatter x1, waiting for transfers between devices, body(): lax.psum_scatter(shared_in_wgrad.astype(jnp.bfloat16), 'dp', scatter_dime...  111 us
    reduce_scatter x1, waiting for transfers between devices, body(): lax.psum_scatter(latent_wgrad, ('dp', 'tensor'), scatter_dimension=0, til...  94.6 us
    unnamed x2, blocking collectives  82.7 us
    all_gather x1, waiting for transfers between devices, gather_experts(): lax.all_gather(w_expert_out, 'dp', axis=2, tiled=True)  75.9 us
    reduce_scatter x1, waiting for transfers between devices, body(): lax.psum_scatter(query_wgrad.astype(jnp.bfloat16), 'dp', scatter_dimensio...  75.9 us
  transfers between devices with their start and end apart: 25, of which 23 were waited for; matrix products, arithmetic and copies ran while one was open for 14% of the time, Pallas kernels for 0%

commit v1 on v0

v1 whole, which is shorter than its diff:
```python
import jax
import jax.numpy as jnp
from jax import lax
from jax.sharding import PartitionSpec as P

D = 2048
H = 16
HD = 128
RD = 64
VD = 128
KR = 512
TOK = 640
EXPERTS = 4


NORM_EPS = 1e-06
ROPE_BASE = 50000.0


def rms_factor(values):
    return lax.rsqrt(jnp.mean(values * values, axis=-1, keepdims=True) + NORM_EPS)


def norm_back(grad_out, values, factor, gain_vec):
    scaled = grad_out * gain_vec
    inner_sum = jnp.mean(scaled * values, axis=-1, keepdims=True)
    return (
        factor * (scaled - values * factor * factor * inner_sum),
        jnp.sum(grad_out * values * factor, axis=0),
    )


def rotary_tables(positions):
    half_width = RD // 2
    inv_freq = ROPE_BASE ** (-jnp.arange(half_width, dtype=jnp.float32) / half_width)
    angles = positions.astype(jnp.float32)[:, None] * inv_freq[None, :]
    return (jnp.cos(angles), jnp.sin(angles))


def rotate(values, cosine_table, sine_table):
    half_width = values.shape[-1] // 2
    first_half = values[..., :half_width]
    second_half = values[..., half_width:]
    return jnp.concatenate(
        [
            first_half * cosine_table - second_half * sine_table,
            second_half * cosine_table + first_half * sine_table,
        ],
        axis=-1,
    )


def silu_parts(gate_pre):
    sigma_gate = jax.nn.sigmoid(gate_pre)
    return (gate_pre * sigma_gate, sigma_gate * (1.0 + gate_pre * (1.0 - sigma_gate)))


def flip_pairs(count, bit):
    return [(i, i ^ (1 << bit)) for i in range(count)]


def swap_dp(values, bit):
    return lax.ppermute(values, "dp", flip_pairs(lax.axis_size("dp"), bit))


def swap_tensor(values, bit):
    return lax.ppermute(values, "tensor", flip_pairs(lax.axis_size("tensor"), bit))


def dp_bits():
    top = lax.axis_size("dp").bit_length() - 1
    return [1] + list(range(top - 1, 1, -1)) + [0]


def slot_order(bits):
    order = [0]
    for bit in bits:
        order = order + [j ^ (1 << bit) for j in order]
    return order


def select_blocks(blocks, index):
    step = 1
    while step < len(blocks):
        hit = (index & step) != 0
        blocks = [jnp.where(hit, blocks[i ^ step], blocks[i]) for i in range(len(blocks))]
        step *= 2
    return blocks


def to_slots(values, index, bits, axis):
    count = 1 << len(bits)
    blocks = select_blocks(jnp.split(values, count, axis=axis), index)
    return jnp.concatenate([blocks[j] for j in slot_order(bits)], axis=axis)


def from_slots(values, index, bits, axis):
    order = slot_order(bits)
    slots = jnp.split(values, len(order), axis=axis)
    blocks = [slots[order.index(i)] for i in range(len(order))]
    return jnp.concatenate(select_blocks(blocks, index), axis=axis)


def gather_dp(values, bits):
    for bit in bits:
        values = jnp.concatenate([values, swap_dp(values, bit)], axis=0)
    return values


def gather_tensor(values):
    for bit in (1, 0):
        values = jnp.concatenate([values, swap_tensor(values, bit)], axis=0)
    return values


def scatter_dp(values, bits, axis):
    values = values.astype(jnp.float32)
    for bit in reversed(bits):
        keep, give = jnp.split(values, 2, axis=axis)
        values = keep + swap_dp(give.astype(jnp.bfloat16), bit).astype(jnp.float32)
    return values


def scatter_tensor(values):
    for bit in (0, 1):
        keep, give = jnp.split(values, 2, axis=0)
        values = keep + swap_tensor(give.astype(jnp.bfloat16), bit).astype(jnp.float32)
    return values


def partner_columns(values):
    count = lax.axis_size("dp")
    slots = jnp.split(values, count, axis=-1)
    return jnp.concatenate([slots[k ^ 1] for k in range(count)], axis=-1)


def gather_pair(values, bit):
    over = swap_dp(partner_columns(values), bit)
    own = jnp.concatenate([values, over, swap_tensor(values, 1), swap_tensor(over, 1)], axis=0)
    return jnp.concatenate([own, swap_tensor(own, 0)], axis=0)


def scatter_pair(values, bit):
    values = scatter_tensor(values)
    keep, give = jnp.split(values, 2, axis=0)
    return keep + swap_dp(partner_columns(give).astype(jnp.bfloat16), bit).astype(jnp.float32)


def dot(a, b, contract):
    return lax.dot_general(a, b, (contract, ((), ())), preferred_element_type=jnp.float32)


def body(
    res_in,
    out_grad,
    seg_ids,
    tok_counts,
    slot_table,
    slot_gates,
    attn_gain,
    latent_gain,
    ffn_gain,
    w_latent,
    w_query,
    w_keyval,
    w_output,
    w_expert_in,
    w_expert_out,
    w_shared_in,
    w_shared_out,
):
    f32 = jnp.float32
    bf16 = jnp.bfloat16
    n_tensor = lax.axis_size("tensor")
    n_dp = lax.axis_size("dp")
    dp = lax.axis_index("dp")
    tensor = lax.axis_index("tensor")
    bits = dp_bits()
    merge = bits[0]
    half = (dp >> merge) & 1
    rows = res_in.shape[0]
    local_heads = H // n_tensor
    score_scale = (HD + RD) ** (-0.5)

    res_local = to_slots(res_in, dp, bits, 1)
    res_all = gather_tensor(res_local)
    tensor_slots = slot_order([1, 0])
    token_ids = jnp.concatenate(
        [(tensor ^ j) * rows + jnp.arange(rows, dtype=jnp.int32) for j in tensor_slots]
    )
    segment_canon = seg_ids[0]
    segment_row = jnp.concatenate(
        [lax.dynamic_slice_in_dim(segment_canon, (tensor ^ j) * rows, rows) for j in tensor_slots]
    )
    valid_all = (token_ids < tok_counts[0]).astype(f32)
    valid_rows = valid_all[:rows, None]
    group_gate = jnp.sum(
        jnp.where(slot_table[0][:, :, None] == token_ids[None, None, :], slot_gates[0][:, :, None], 0.0),
        axis=1,
    )
    grad_in = to_slots(out_grad, dp, bits, 1).astype(f32)
    ffn_grad = (valid_rows * grad_in).astype(bf16)

    pack_rows = w_latent.shape[0]
    gain_row = jnp.concatenate([attn_gain, ffn_gain, latent_gain])
    gain_row = jnp.pad(gain_row, (0, w_latent.shape[1] - gain_row.shape[0]))
    pack = jnp.concatenate([w_latent, jnp.broadcast_to(gain_row, (16, w_latent.shape[1]))], axis=0)
    pack = gather_dp(pack[None], bits)
    pack = gather_tensor(pack[None])
    pack_blocks = [pack[tensor_slots.index(j)] for j in range(n_tensor)]
    pack = jnp.stack(select_blocks(pack_blocks, tensor), axis=1)
    latent_full = pack[:, :, :pack_rows].reshape(D, KR + RD)
    gains = pack[:, :, pack_rows]
    gain_width, latent_width = D // (n_dp * n_tensor), KR // (n_dp * n_tensor)
    attn_gain_full = gains[..., :gain_width].reshape(D)
    ffn_gain_full = gains[..., gain_width : 2 * gain_width].reshape(D)
    latent_gain_full = from_slots(
        gains[..., 2 * gain_width : 2 * gain_width + latent_width].reshape(KR), dp, bits, 0
    )
    query_full = gather_dp(w_query, bits)
    keyval_full = from_slots(gather_dp(w_keyval, bits), dp, bits, 0)
    output_full = gather_dp(w_output[None], bits)
    output_full = jnp.concatenate([output_full[k] for k in range(n_dp)], axis=1)

    n_half = EXPERTS // 2
    expert_units = jnp.concatenate(
        [
            w_expert_in.transpose(0, 1, 3, 2).reshape(EXPERTS, -1, w_expert_in.shape[2]),
            w_expert_out,
        ],
        axis=1,
    )
    width = w_expert_out.shape[1]
    shared_t = w_shared_in.transpose(0, 2, 1)
    units = []
    for side in range(2):
        cut = slice(side * width, (side + 1) * width)
        shared_unit = jnp.concatenate([shared_t[0, cut], shared_t[1, cut], w_shared_out[cut]], axis=0)
        units.append(jnp.concatenate([expert_units[side * n_half : (side + 1) * n_half], shared_unit[None]], axis=0))
    first = half == 0
    own_units = jnp.where(first, units[0], units[1])
    other_units = jnp.where(first, units[1], units[0])
    pieces = []
    for p in range(n_half + 1):
        piece = jnp.stack([own_units[p], swap_dp(other_units[p], merge)], axis=0)
        piece = gather_dp(piece, bits[1:])
        pieces.append(jnp.concatenate([piece[k] for k in range(n_dp)], axis=1))

    positions = token_ids - jnp.sum(
        (segment_canon[None, :] < segment_row[:, None]).astype(jnp.int32), axis=1
    )
    cos_all, sin_all = rotary_tables(positions)
    allowed = (segment_row[:, None] == segment_row[None, :]) & (
        token_ids[None, :] <= token_ids[:, None]
    )
    resid_all = res_all.astype(f32)
    in_factor = rms_factor(resid_all)
    normed_all = (resid_all * in_factor * attn_gain_full).astype(bf16)
    latent_raw = jnp.dot(normed_all, latent_full, preferred_element_type=f32)
    latent_c = latent_raw[:, :KR]
    latent_factor = rms_factor(latent_c)
    latent_norm = (latent_c * latent_factor * latent_gain_full).astype(bf16)
    rope_all = rotate(latent_raw[:, KR:], cos_all, sin_all).astype(bf16)
    query_raw = jnp.dot(normed_all, query_full, preferred_element_type=f32).reshape(
        TOK, local_heads, HD + RD
    )
    query_final = jnp.concatenate(
        [
            query_raw[..., :HD],
            rotate(query_raw[..., HD:], cos_all[:, None, :], sin_all[:, None, :]),
        ],
        axis=-1,
    ).astype(bf16)
    keyval = (
        jnp.dot(latent_norm, keyval_full, preferred_element_type=f32)
        .astype(bf16)
        .reshape(TOK, local_heads, HD + VD)
    )
    key_nope = keyval[..., :HD]
    values_all = keyval[..., HD:]
    raw_scores = jnp.einsum(
        "qhd,khd->hqk", query_final[..., :HD], key_nope, preferred_element_type=f32
    )
    raw_scores = raw_scores + jnp.einsum(
        "qhr,kr->hqk", query_final[..., HD:], rope_all, preferred_element_type=f32
    )
    scores = jnp.where(allowed[None], raw_scores * score_scale, -1e30)
    top_score = jnp.max(scores, axis=-1, keepdims=True)
    exp_scores = jnp.exp(scores - top_score)
    probs_all = exp_scores / jnp.sum(exp_scores, axis=-1, keepdims=True)
    probs_low = probs_all.astype(bf16)
    attn_mix = (
        jnp.einsum("hqk,khd->qhd", probs_low, values_all, preferred_element_type=f32)
        .astype(bf16)
        .reshape(TOK, local_heads * VD)
    )
    attn_part = jnp.dot(attn_mix, output_full, preferred_element_type=f32)
    attn_out = scatter_tensor(attn_part)
    resid_in = res_local.astype(f32)
    mid_resid = resid_in + valid_rows * attn_out
    mid_factor = rms_factor(mid_resid)
    normed_mid = (mid_resid * mid_factor * ffn_gain_full).astype(bf16)

    mid_pair = gather_pair(normed_mid, merge)
    grad_pair = gather_pair(ffn_grad, merge)
    other_gate = swap_dp(group_gate, merge)
    pair_gate = jnp.concatenate(
        [
            gate[:, k * rows : (k + 1) * rows]
            for k in ((0, 0), (1, 0), (0, 1), (1, 1), (0, 2), (1, 2), (0, 3), (1, 3))
            for gate, k in (((group_gate, other_gate)[k[0]], k[1]),)
        ],
        axis=1,
    )
    pair_gate = jnp.where(first, pair_gate[:n_half], pair_gate[n_half:])
    mid_pair_grad = None
    hidden_parts, out_parts, unit_grads = [], [], []
    for p, piece in enumerate(pieces):
        gate_up = dot(piece[: 2 * width], mid_pair, ((1,), (1,)))
        gate_pre, up = gate_up[:width], gate_up[width:]
        silu, slope = silu_parts(gate_pre)
        hidden_grad = dot(piece[2 * width :], grad_pair, ((1,), (1,)))
        hidden = silu * up
        if p < n_half:
            hidden = hidden * pair_gate[p][None]
            hidden_grad = hidden_grad * pair_gate[p][None]
        hidden = hidden.astype(bf16)
        pre_grad = jnp.concatenate(
            [(hidden_grad * up * slope).astype(bf16), (hidden_grad * silu).astype(bf16)], axis=0
        )
        back = dot(pre_grad, piece[: 2 * width], ((0,), (0,)))
        mid_pair_grad = back if mid_pair_grad is None else mid_pair_grad + back
        hidden_parts.append(hidden)
        out_parts.append(piece[2 * width :])
        in_wgrad = dot(pre_grad, mid_pair, ((1,), (0,)))
        out_wgrad = dot(hidden, grad_pair, ((1,), (0,)))
        unit_grads.append(jnp.concatenate([in_wgrad, out_wgrad], axis=0).astype(bf16))
    ffn_part = dot(
        jnp.concatenate(hidden_parts, axis=0), jnp.concatenate(out_parts, axis=0), ((0,), (0,))
    )
    ffn_out = scatter_pair(ffn_part, merge)
    res_out = (mid_resid + valid_rows * ffn_out).astype(bf16)
    mid_grad_local = scatter_pair(mid_pair_grad, merge)

    mid_back, ffn_gain_part = norm_back(mid_grad_local, mid_resid, mid_factor, ffn_gain_full)
    mid_grad = grad_in + mid_back
    attn_grad = (valid_rows * mid_grad).astype(bf16)
    attn_grad_all = gather_tensor(attn_grad)
    output_wgrad = dot(attn_mix, attn_grad_all, ((0,), (0,)))
    mix_grad = (
        dot(attn_grad_all, output_full, ((1,), (1,))).astype(bf16).reshape(TOK, local_heads, VD)
    )
    probs_grad = jnp.einsum("qhd,khd->hqk", mix_grad, values_all, preferred_element_type=f32)
    value_grad = jnp.einsum("hqk,qhd->khd", probs_low, mix_grad, preferred_element_type=f32)
    scores_grad = (
        probs_all * (probs_grad - jnp.sum(probs_all * probs_grad, axis=-1, keepdims=True))
    ).astype(bf16)
    query_nope_grad = (
        jnp.einsum("hqk,khd->qhd", scores_grad, key_nope, preferred_element_type=f32) * score_scale
    )
    query_rope_grad = (
        jnp.einsum("hqk,kr->qhr", scores_grad, rope_all, preferred_element_type=f32) * score_scale
    )
    key_nope_grad = (
        jnp.einsum("hqk,qhd->khd", scores_grad, query_final[..., :HD], preferred_element_type=f32)
        * score_scale
    )
    rope_key_grad = (
        jnp.einsum("hqk,qhr->kr", scores_grad, query_final[..., HD:], preferred_element_type=f32)
        * score_scale
    )
    query_grad = (
        jnp.concatenate(
            [query_nope_grad, rotate(query_rope_grad, cos_all[:, None, :], -sin_all[:, None, :])],
            axis=-1,
        )
        .astype(bf16)
        .reshape(TOK, local_heads * (HD + RD))
    )
    keyval_grad = (
        jnp.concatenate([key_nope_grad, value_grad], axis=-1)
        .astype(bf16)
        .reshape(TOK, local_heads * (HD + VD))
    )
    latent_part = jnp.concatenate([dot(keyval_grad, keyval_full, ((1,), (1,))), rope_key_grad], axis=1)
    latent_grad_local = scatter_tensor(latent_part)
    normed_part = dot(query_grad, query_full, ((1,), (1,)))
    normed_grad_local = scatter_tensor(normed_part)
    query_wgrad = dot(normed_all, query_grad, ((0,), (0,)))
    keyval_wgrad = to_slots(dot(latent_norm, keyval_grad, ((0,), (0,))).astype(bf16), dp, bits, 0)
    latent_c_grad, latent_gain_part = norm_back(
        latent_grad_local[:, :KR], latent_c[:rows], latent_factor[:rows], latent_gain_full
    )
    rope_raw_grad = rotate(latent_grad_local[:, KR:], cos_all[:rows], -sin_all[:rows])
    latent_raw_grad = jnp.concatenate([latent_c_grad, rope_raw_grad], axis=1).astype(bf16)
    latent_raw_grad_all = gather_tensor(latent_raw_grad)
    latent_wgrad = dot(normed_all, latent_raw_grad_all, ((0,), (0,))).astype(bf16)
    latent_wgrad = lax.dynamic_index_in_dim(
        latent_wgrad.reshape(n_dp, n_tensor, pack_rows, KR + RD), tensor, 1, keepdims=False
    )
    normed_grad = normed_grad_local + dot(latent_raw_grad, latent_full, ((1,), (1,)))
    in_back, attn_gain_part = norm_back(normed_grad, resid_in, in_factor[:rows], attn_gain_full)
    res_grad = mid_grad + in_back

    output_owned = scatter_dp(output_wgrad, bits, 1)
    query_owned = scatter_dp(query_wgrad, bits, 0)
    keyval_owned = scatter_dp(keyval_wgrad, bits, 0)
    latent_owned = scatter_dp(latent_wgrad, bits, 0)[0]
    gain_parts = jnp.concatenate(
        [
            attn_gain_part.reshape(n_dp, n_tensor, gain_width),
            ffn_gain_part.reshape(n_dp, n_tensor, gain_width),
            to_slots(latent_gain_part, dp, bits, 0).reshape(n_dp, n_tensor, latent_width),
        ],
        axis=2,
    )
    gain_parts = jnp.stack(
        [
            select_blocks([gain_parts[:, i] for i in range(n_tensor)], tensor)[j]
            for j in tensor_slots
        ],
        axis=0,
    )
    for bit in (0, 1):
        keep, give = jnp.split(gain_parts, 2, axis=0)
        gain_parts = keep + swap_tensor(give, bit)
    gain_parts = gain_parts[0]
    for bit in reversed(bits):
        keep, give = jnp.split(gain_parts, 2, axis=0)
        gain_parts = keep + swap_dp(give, bit)
    gain_owned = gain_parts[0]
    own_grads, other_grads = [], []
    for grad in unit_grads:
        grad = grad.astype(f32)
        for bit in reversed(bits[1:]):
            keep, give = jnp.split(grad, 2, axis=1)
            grad = keep + swap_dp(give.astype(bf16), bit).astype(f32)
        keep, give = jnp.split(grad, 2, axis=1)
        own_grads.append(keep)
        other_grads.append(swap_dp(give.astype(bf16), merge).astype(f32))
    sides = []
    for side in (first, ~first):
        sides.append([jnp.where(side, a, b) for a, b in zip(own_grads, other_grads)])
    expert_units = jnp.stack([unit for side in sides for unit in side[:n_half]], axis=0)
    expert_in_owned = expert_units[:, : 2 * width].reshape(EXPERTS, 2, width, -1).transpose(0, 1, 3, 2)
    expert_out_owned = expert_units[:, 2 * width :]
    shared_in_owned = jnp.stack(
        [
            jnp.concatenate([side[n_half][k * width : (k + 1) * width] for side in sides], axis=0).T
            for k in range(2)
        ],
        axis=0,
    )
    shared_out_owned = jnp.concatenate([side[n_half][2 * width :] for side in sides], axis=0)
    return (
        from_slots(res_out, dp, bits, 1),
        from_slots(res_grad, dp, bits, 1),
        gain_owned[:gain_width],
        gain_owned[2 * gain_width :],
        gain_owned[gain_width : 2 * gain_width],
        latent_owned,
        query_owned,
        keyval_owned,
        output_owned,
        expert_in_owned,
        expert_out_owned,
        shared_in_owned,
        shared_out_owned,
    )


def solution(mesh):
    placed = (
        P(("dp", "tensor"), None),
        P(("dp", "tensor"), None),
        P("dp", None),
        P("dp"),
        P("dp", None, None),
        P("dp", None, None),
        P(("dp", "tensor")),
        P(("dp", "tensor")),
        P(("dp", "tensor")),
        P(("dp", "tensor"), None),
        P("dp", "tensor"),
        P("dp", "tensor"),
        P("tensor", "dp"),
        P(None, None, "dp", "tensor"),
        P(None, "tensor", "dp"),
        P(None, "dp", "tensor"),
        P("tensor", "dp"),
    )
    return jax.shard_map(
        body,
        mesh=mesh,
        in_specs=placed,
        out_specs=(
            P(("dp", "tensor"), None),
            P(("dp", "tensor"), None),
            P(("dp", "tensor")),
            P(("dp", "tensor")),
            P(("dp", "tensor")),
            P(("dp", "tensor"), None),
            P("dp", "tensor"),
            P("dp", "tensor"),
            P("tensor", "dp"),
            P(None, None, "dp", "tensor"),
            P(None, "tensor", "dp"),
            P(None, "dp", "tensor"),
            P("tensor", "dp"),
        ),
        check_vma=False,
    )
```

time: 1960 us -> 1040 us (0.53)
  waiting for transfers between devices: 1450 us -> 591 us
  blocking collectives: 91.7 us -> 0 us
  starting transfers between devices: 2.05 us -> 58.9 us
  matrix products: 204 us -> 164 us
  local copies, waits for them, and re-layouts: 72.9 us -> 109 us
  other arithmetic: 122 us -> 99.5 us
    reduce_scatter x13 -> x0, waiting for transfers between devices: 880 us -> none  [the longest x1 194 us: body(): lax.psum_scatter(expert_in_wgrad.astype(jnp.bfloat16), 'dp', scatter_dime...]
    ppermute x0 -> x76, waiting for transfers between devices: none -> 591 us  [the longest x50 517 us: swap_dp(): return lax.ppermute(values, 'dp', flip_pairs(lax.axis_size('dp'), bit))]
    all_gather x12 -> x0, waiting for transfers between devices: 563 us -> none  [the longest x1 152 us: gather_experts(): lax.all_gather(w_expert_in, 'dp', axis=2, tiled=True)]
    unnamed x2 -> x0, blocking collectives: 82.7 us -> none
    scatter-add x2 -> x0, other arithmetic: 77 us -> none  [the longest x1 38.7 us: body(): ffn_part.at[target]]
    ppermute x0 -> x76, starting transfers between devices: none -> 58.9 us  [the longest x50 46.6 us: swap_dp(): return lax.ppermute(values, 'dp', flip_pairs(lax.axis_size('dp'), bit))]
    gather x2 -> x0, local copies, waits for them, and re-layouts: 44.6 us -> none  [the longest x1 22.3 us: body(): expert_rows = mid_all[slot_rows]]
    dot_general x26 -> x28, matrix products: 176 us -> 133 us  [the longest x24 125 us: dot(): lax.dot_general(a, b, (contract, ((), ())), preferred_element_type=jnp.fl...]
  transfers between devices with their start and end apart: 25 -> 76, of which waited for: 23 -> 38; matrix products, arithmetic and copies ran while one was open for 14% -> 26% of each run, Pallas kernels for 0% -> 0%
where the time goes in v1:
time: 1040 us; the launch traced here: 1030 us
  waiting for transfers between devices  591 us (57%)
  matrix products  164 us (16%)
  local copies, waits for them, and re-layouts  109 us (10%)
  other arithmetic  99.5 us (10%)
  starting transfers between devices  58.9 us (6%)
    ppermute x50, waiting for transfers between devices, swap_dp(): return lax.ppermute(values, 'dp', flip_pairs(lax.axis_size('dp'), bit))  517 us
    dot_general x24, matrix products, dot(): lax.dot_general(a, b, (contract, ((), ())), preferred_element_type=jnp.fl...  125 us
    ppermute x26, waiting for transfers between devices, swap_tensor(): lax.ppermute(values, 'tensor', flip_pairs(lax.axis_size('tensor'), bit))  74.7 us
    unnamed x325, local copies, waits for them, and re-layouts  57.2 us
    ppermute x50, starting transfers between devices, swap_dp(): return lax.ppermute(values, 'dp', flip_pairs(lax.axis_size('dp'), bit))  46.6 us
  transfers between devices with their start and end apart: 76, of which 38 were waited for; matrix products, arithmetic and copies ran while one was open for 26% of the time, Pallas kernels for 0%

profile of v1, /device:TPU:0, one launch (start us, length us, event | category | flops | bytes accessed | tf_op | source)
XLA Modules:
  0.0 1027.5 jit_solution(6814836186101670638)
XLA Ops:
  39.8 9.3 collective-permute-done.13
  70.1 15.5 %collective-permute-done.18 = bf16[1056,256]{1,0:T(8,128)(2,1)S(1)} collective-permute-done((bf16[1056,256]{1,0:T(8,128)(2,1)S(1)}, bf16[1056,256]{1,0:T(8,128)(2,1)S(1)}, u32[]{:S(2)}, u32[]{:S(2)}) %collective-permute-start.18) | collective-permute-done | bytes 540704 | tf_op jit(solution)/shard_map/ppermute | solution.py:63
  86.1 25.9 %collective-permute-done.26 = bf16[1056,256]{1,0:T(8,128)(2,1)S(1)} collective-permute-done((bf16[1056,256]{1,0:T(8,128)(2,1)S(1)}, bf16[1056,256]{1,0:T(8,128)(2,1)S(1)}, u32[]{:S(2)}, u32[]{:S(2)}) %collective-permute-start.26) | collective-permute-done | bytes 540704 | tf_op jit(solution)/shard_map/ppermute | solution.py:63
  139.8 83.1 %collective-permute-done.11 = bf16[512,768]{1,0:T(8,128)(2,1)S(1)} collective-permute-done((bf16[512,768]{1,0:T(8,128)(2,1)S(1)}, bf16[512,768]{1,0:T(8,128)(2,1)S(1)}, u32[]{:S(2)}, u32[]{:S(2)}) %collective-permute-start.11) | collective-permute-done | bytes 786464 | tf_op jit(solution)/shard_map/ppermute | solution.py:63
  230.5 12.4 %collective-permute-done.5 = bf16[1,8,80,576]{3,2,1,0:T(8,128)(2,1)S(1)} collective-permute-done((bf16[1,8,80,576]{3,2,1,0:T(8,128)(2,1)S(1)}, bf16[1,8,80,576]{3,2,1,0:T(8,128)(2,1)S(1)}, u32[]{:S(2)}, u32[]{:S(2)}) %collective-permute-start.5) | collective-permute-done | bytes 737312 | tf_op jit(solution)/shard_map/ppermute | solution.py:67
  248.3 20.9 %collective-permute-done.19 = bf16[2,1056,256]{2,1,0:T(8,128)(2,1)S(1)} collective-permute-done((bf16[2,1056,256]{2,1,0:T(8,128)(2,1)S(1)}, bf16[2,1056,256]{2,1,0:T(8,128)(2,1)S(1)}, u32[]{:S(2)}, u32[]{:S(2)}) %collective-permute-start.19) | collective-permute-done | bytes 1081376 | tf_op jit(solution)/shard_map/ppermute | solution.py:63
  271.0 21.2 %collective-permute-done.27 = bf16[2,1056,256]{2,1,0:T(8,128)(2,1)S(1)} collective-permute-done((bf16[2,1056,256]{2,1,0:T(8,128)(2,1)S(1)}, bf16[2,1056,256]{2,1,0:T(8,128)(2,1)S(1)}, u32[]{:S(2)}, u32[]{:S(2)}) %collective-permute-start.27) | collective-permute-done | bytes 1081376 | tf_op jit(solution)/shard_map/ppermute | solution.py:63
  364.4 13.2 %collective-permute-done.17 = bf16[160,2048]{1,0:T(8,128)(2,1)S(1)} collective-permute-done((bf16[160,2048]{1,0:T(8,128)(2,1)S(1)}, bf16[160,2048]{1,0:T(8,128)(2,1)S(1)}, u32[]{:S(2)}, u32[]{:S(2)}) %collective-permute-start.17) | collective-permute-done | bytes 655392 | tf_op jit(solution)/shard_map/ppermute | solution.py:67
  379.6 60.6 %collective-permute-done.28 = bf16[4,1056,256]{2,1,0:T(8,128)(2,1)} collective-permute-done((bf16[4,1056,256]{2,1,0:T(8,128)(2,1)}, bf16[4,1056,256]{2,1,0:T(8,128)(2,1)}, u32[]{:S(2)}, u32[]{:S(2)}) %collective-permute-start.28) | collective-permute-done | bytes 2162720 | tf_op jit(solution)/shard_map/ppermute | solution.py:63
  447.0 13.2 %collective-permute-done.22 = bf16[160,2048]{1,0:T(8,128)(2,1)S(1)} collective-permute-done((bf16[160,2048]{1,0:T(8,128)(2,1)S(1)}, bf16[160,2048]{1,0:T(8,128)(2,1)S(1)}, u32[]{:S(2)}, u32[]{:S(2)}) %collective-permute-start.22) | collective-permute-done | bytes 655392 | tf_op jit(solution)/shard_map/ppermute | solution.py:67
  460.2 12.7 %collective-permute-done.23 = bf16[160,2048]{1,0:T(8,128)(2,1)S(1)} collective-permute-done((bf16[160,2048]{1,0:T(8,128)(2,1)S(1)}, bf16[160,2048]{1,0:T(8,128)(2,1)S(1)}, u32[]{:S(2)}, u32[]{:S(2)}) %collective-permute-start.23) | collective-permute-done | bytes 655392 | tf_op jit(solution)/shard_map/ppermute | solution.py:67
  588.3 16.5 %add_add_fusion = f32[1280,2048]{1,0:T(8,128)} fusion(f32[1280,2048]{1,0:T(8,128)} %fusion.24, f32[1280,2048]{1,0:T(8,128)} %fusion.20, bf16[1056,2048]{1,0:T(8,128)(2,1)} %copy-done.53, bf16[352,1280]{1,0:T(8,128)(2,1)} %copy-done.105, bf16[352,1280]{1,0:T(8,128)(2,1)S(1)} %copy-done.104), kind=kOutput, calls=%fused_computation.1 | convolution fusion | flops 3699834880 | bytes 36143104 | tf_op jit(solution)/shard_map/dot_general | solution.py:150
  612.0 28.2 %collective-permute-done.67 = bf16[1056,1024]{1,0:T(8,128)(2,1)} collective-permute-done((bf16[1056,1024]{1,0:T(8,128)(2,1)}, bf16[1056,1024]{1,0:T(8,128)(2,1)}, u32[]{:S(2)}, u32[]{:S(2)}) %collective-permute-start.67) | collective-permute-done | bytes 2162720 | tf_op jit(solution)/shard_map/ppermute | solution.py:63
  644.0 41.9 %collective-permute-done.70 = bf16[1056,1024]{1,0:T(8,128)(2,1)} collective-permute-done((bf16[1056,1024]{1,0:T(8,128)(2,1)}, bf16[1056,1024]{1,0:T(8,128)(2,1)}, u32[]{:S(2)}, u32[]{:S(2)}) %collective-permute-start.70) | collective-permute-done | bytes 2162720 | tf_op jit(solution)/shard_map/ppermute | solution.py:63
  703.6 27.3 %collective-permute-done.68 = bf16[1056,512]{1,0:T(8,128)(2,1)} collective-permute-done((bf16[1056,512]{1,0:T(8,128)(2,1)}, bf16[1056,512]{1,0:T(8,128)(2,1)}, u32[]{:S(2)}, u32[]{:S(2)}) %collective-permute-start.68) | collective-permute-done | bytes 1081376 | tf_op jit(solution)/shard_map/ppermute | solution.py:63
  732.7 21.3 %collective-permute-done.71 = bf16[1056,512]{1,0:T(8,128)(2,1)} collective-permute-done((bf16[1056,512]{1,0:T(8,128)(2,1)S(1)}, bf16[1056,512]{1,0:T(8,128)(2,1)}, u32[]{:S(2)}, u32[]{:S(2)}) %collective-permute-start.71) | collective-permute-done | bytes 1081376 | tf_op jit(solution)/shard_map/ppermute | solution.py:63
  756.1 10.5 %collective-permute-done.69 = bf16[1056,256]{1,0:T(8,128)(2,1)S(1)} collective-permute-done((bf16[1056,256]{1,0:T(8,128)(2,1)S(1)}, bf16[1056,256]{1,0:T(8,128)(2,1)S(1)}, u32[]{:S(2)}, u32[]{:S(2)}) %collective-permute-start.69) | collective-permute-done | bytes 540704 | tf_op jit(solution)/shard_map/ppermute | solution.py:63
  767.9 9.8 collective-permute-done.72
  784.4 14.2 %collective-permute-done.41 = bf16[160,2048]{1,0:T(8,128)(2,1)S(1)} collective-permute-done((bf16[160,2048]{1,0:T(8,128)(2,1)S(1)}, bf16[160,2048]{1,0:T(8,128)(2,1)S(1)}, u32[]{:S(2)}, u32[]{:S(2)}) %collective-permute-start.41) | collective-permute-done | bytes 655392 | tf_op jit(solution)/shard_map/ppermute | solution.py:63
  799.2 12.1 %collective-permute-done.34 = bf16[160,2048]{1,0:T(8,128)(2,1)S(1)} collective-permute-done((bf16[160,2048]{1,0:T(8,128)(2,1)S(1)}, bf16[160,2048]{1,0:T(8,128)(2,1)S(1)}, u32[]{:S(2)}, u32[]{:S(2)}) %collective-permute-start.34) | collective-permute-done | bytes 655392 | tf_op jit(solution)/shard_map/ppermute | solution.py:63
  817.5 11.1 %collective-permute-done.42 = bf16[160,2048]{1,0:T(8,128)(2,1)} collective-permute-done((bf16[160,2048]{1,0:T(8,128)(2,1)}, bf16[160,2048]{1,0:T(8,128)(2,1)}, u32[]{:S(2)}, u32[]{:S(2)}) %collective-permute-start.42) | collective-permute-done | bytes 655392 | tf_op jit(solution)/shard_map/ppermute | solution.py:67
  876.9 24.2 %collective-permute-done.61 = bf16[256,1024]{1,0:T(8,128)(2,1)S(1)} collective-permute-done((bf16[256,1024]{1,0:T(8,128)(2,1)S(1)}, bf16[256,1024]{1,0:T(8,128)(2,1)S(1)}, u32[]{:S(2)}, u32[]{:S(2)}) %collective-permute-start.61) | collective-permute-done | bytes 524320 | tf_op jit(solution)/shard_map/ppermute | solution.py:63
  948.3 21.8 %collective-permute-done.56 = bf16[2,64,576]{2,1,0:T(8,128)(2,1)S(1)} collective-permute-done((bf16[2,64,576]{2,1,0:T(8,128)(2,1)S(1)}, bf16[2,64,576]{2,1,0:T(8,128)(2,1)S(1)}, u32[]{:S(2)}, u32[]{:S(2)}) %collective-permute-start.56) | collective-permute-done | bytes 147488 | tf_op jit(solution)/shard_map/ppermute | solution.py:63
  993.7 18.6 %collective-permute-done.51 = f32[2,144]{1,0:T(2,128)S(1)} collective-permute-done((f32[2,144]{1,0:T(2,128)S(1)}, f32[2,144]{1,0:T(2,128)S(1)}, u32[]{:S(2)}, u32[]{:S(2)}) %collective-permute-start.51) | collective-permute-done | bytes 1184 | tf_op jit(solution)/shard_map/ppermute | solution.py:63
  (751 shorter events, 477.1 us)
Async XLA Ops:
  11.8 115.4 %collective-permute-start.36 = (bf16[160,2048]{1,0:T(8,128)(2,1)S(1)}, bf16[160,2048]{1,0:T(8,128)(2,1)}, u32[]{:S(2)}, u32[]{:S(2)}) collective-permute-start(bf16[160,2048]{1,0:T(8,128)(2,1)S(1)} %get-tuple-element.64), channel_id=1, source_target_pairs={{0,2},{1,3},{2,0},{3,1},{4,6},{5,7},{6,4},{7,5},{8,10},{9,11},{10,... | collective-permute-start | bytes 1966088 | tf_op jit(solution)/shard_map/ppermute | solution.py:67
  56.9 74.9 %collective-permute-start = (bf16[160,2048]{1,0:T(8,128)(2,1)S(1)}, bf16[160,2048]{1,0:T(8,128)(2,1)S(1)}, u32[]{:S(2)}, u32[]{:S(2)}) collective-permute-start(bf16[160,2048]{1,0:T(8,128)(2,1)S(1)} %constant_dynamic-update-slice_fusion), channel_id=1, source_target_pairs={{0,2},{1,3},{2,0},{3,1},{4,6},{5,7},{6,4},{7,5},{8,10},{9,11},{10,... | collective-permute-start | bytes 1966088 | tf_op jit(solution)/shard_map/ppermute | solution.py:67
  125.8 97.0 %collective-permute-start.11 = (bf16[512,768]{1,0:T(8,128)(2,1)S(1)}, bf16[512,768]{1,0:T(8,128)(2,1)S(1)}, u32[]{:S(2)}, u32[]{:S(2)}) collective-permute-start(bf16[512,768]{1,0:T(8,128)(2,1)S(1)} %pad_maximum_fusion.41), channel_id=1, source_target_pairs={{0,16},{4,20},{8,24},{12,28},{16,0},{20,4},{24,8},{28,12},{1,17},{... | collective-permute-start | bytes 2359304 | tf_op jit(solution)/shard_map/ppermute | solution.py:63
  127.1 118.9 %collective-permute-start.30 = (bf16[2,1056,256]{2,1,0:T(8,128)(2,1)S(1)}, bf16[2,1056,256]{2,1,0:T(8,128)(2,1)S(1)}, u32[]{:S(2)}, u32[]{:S(2)}) collective-permute-start(bf16[2,1056,256]{2,1,0:T(8,128)(2,1)S(1)} %pad_maximum_fusion.34), channel_id=1, source_target_pairs={{0,16},{4,20},{8,24},{12,28},{16,0},{20,4},{24,8},{28,12},{1,17},{... | collective-permute-start | bytes 3244040 | tf_op jit(solution)/shard_map/ppermute | solution.py:63
  131.7 137.5 %collective-permute-start.19 = (bf16[2,1056,256]{2,1,0:T(8,128)(2,1)S(1)}, bf16[2,1056,256]{2,1,0:T(8,128)(2,1)S(1)}, u32[]{:S(2)}, u32[]{:S(2)}) collective-permute-start(bf16[2,1056,256]{2,1,0:T(8,128)(2,1)S(1)} %pad_maximum_fusion.32), channel_id=1, source_target_pairs={{0,16},{4,20},{8,24},{12,28},{16,0},{20,4},{24,8},{28,12},{1,17},{... | collective-permute-start | bytes 3244040 | tf_op jit(solution)/shard_map/ppermute | solution.py:63
  132.2 160.1 %collective-permute-start.27 = (bf16[2,1056,256]{2,1,0:T(8,128)(2,1)S(1)}, bf16[2,1056,256]{2,1,0:T(8,128)(2,1)S(1)}, u32[]{:S(2)}, u32[]{:S(2)}) collective-permute-start(bf16[2,1056,256]{2,1,0:T(8,128)(2,1)S(1)} %pad_maximum_fusion.33), channel_id=1, source_target_pairs={{0,16},{4,20},{8,24},{12,28},{16,0},{20,4},{24,8},{28,12},{1,17},{... | collective-permute-start | bytes 3244040 | tf_op jit(solution)/shard_map/ppermute | solution.py:63
  137.4 87.1 %collective-permute-start.37 = (bf16[160,2048]{1,0:T(8,128)(2,1)S(1)}, bf16[160,2048]{1,0:T(8,128)(2,1)S(1)}, u32[]{:S(2)}, u32[]{:S(2)}) collective-permute-start(bf16[160,2048]{1,0:T(8,128)(2,1)S(1)} %collective-permute-done.35), channel_id=1, source_target_pairs={{0,2},{1,3},{2,0},{3,1},{4,6},{5,7},{6,4},{7,5},{8,10},{9,11},{10,... | collective-permute-start | bytes 1966088 | tf_op jit(solution)/shard_map/ppermute | solution.py:67
  224.6 76.8 %collective-permute-start.1 = (bf16[320,2048]{1,0:T(8,128)(2,1)S(1)}, bf16[320,2048]{1,0:T(8,128)(2,1)S(1)}, u32[]{:S(2)}, u32[]{:S(2)}) collective-permute-start(bf16[320,2048]{1,0:T(8,128)(2,1)S(1)} %pad_maximum_fusion.23), channel_id=1, source_target_pairs={{0,1},{1,0},{2,3},{3,2},{4,5},{5,4},{6,7},{7,6},{8,9},{9,8},{10,11... | collective-permute-start | bytes 3932168 | tf_op jit(solution)/shard_map/ppermute | solution.py:67
  269.2 210.5 %collective-permute-start.38 = (bf16[640,2048]{1,0:T(8,128)(2,1)}, bf16[640,2048]{1,0:T(8,128)(2,1)}, u32[]{:S(2)}, u32[]{:S(2)}) collective-permute-start(bf16[640,2048]{1,0:T(8,128)(2,1)} %pad_maximum_fusion.6), channel_id=1, source_target_pairs={{0,1},{1,0},{2,3},{3,2},{4,5},{5,4},{6,7},{7,6},{8,9},{9,8},{10,11... | collective-permute-start | bytes 7864328 | tf_op jit(solution)/shard_map/ppermute | solution.py:67
  301.4 172.0 %collective-permute-start.20 = (bf16[4,1056,256]{2,1,0:T(8,128)(2,1)}, bf16[4,1056,256]{2,1,0:T(8,128)(2,1)}, u32[]{:S(2)}, u32[]{:S(2)}) collective-permute-start(bf16[4,1056,256]{2,1,0:T(8,128)(2,1)} %pad_maximum_fusion.11), channel_id=1, source_target_pairs={{0,4},{4,0},{8,12},{12,8},{16,20},{20,16},{24,28},{28,24},{1,5},{5... | collective-permute-start | bytes 6488072 | tf_op jit(solution)/shard_map/ppermute | solution.py:63
  303.5 136.8 %collective-permute-start.28 = (bf16[4,1056,256]{2,1,0:T(8,128)(2,1)}, bf16[4,1056,256]{2,1,0:T(8,128)(2,1)}, u32[]{:S(2)}, u32[]{:S(2)}) collective-permute-start(bf16[4,1056,256]{2,1,0:T(8,128)(2,1)} %pad_maximum_fusion.12), channel_id=1, source_target_pairs={{0,4},{4,0},{8,12},{12,8},{16,20},{20,16},{24,28},{28,24},{1,5},{5... | collective-permute-start | bytes 6488072 | tf_op jit(solution)/shard_map/ppermute | solution.py:63
  543.7 64.5 %collective-permute-start.73 = (bf16[1056,1024]{1,0:T(8,128)(2,1)}, bf16[1056,1024]{1,0:T(8,128)(2,1)}, u32[]{:S(2)}, u32[]{:S(2)}) collective-permute-start(bf16[1056,1024]{1,0:T(8,128)(2,1)} %pad_maximum_fusion.8), channel_id=1, source_target_pairs={{0,4},{4,0},{8,12},{12,8},{16,20},{20,16},{24,28},{28,24},{1,5},{5... | collective-permute-start | bytes 6488072 | tf_op jit(solution)/shard_map/ppermute | solution.py:63
  558.7 81.6 %collective-permute-start.67 = (bf16[1056,1024]{1,0:T(8,128)(2,1)}, bf16[1056,1024]{1,0:T(8,128)(2,1)}, u32[]{:S(2)}, u32[]{:S(2)}) collective-permute-start(bf16[1056,1024]{1,0:T(8,128)(2,1)} %pad_maximum_fusion.10), channel_id=1, source_target_pairs={{0,4},{4,0},{8,12},{12,8},{16,20},{20,16},{24,28},{28,24},{1,5},{5... | collective-permute-start | bytes 6488072 | tf_op jit(solution)/shard_map/ppermute | solution.py:63
  563.2 122.8 %collective-permute-start.70 = (bf16[1056,1024]{1,0:T(8,128)(2,1)}, bf16[1056,1024]{1,0:T(8,128)(2,1)}, u32[]{:S(2)}, u32[]{:S(2)}) collective-permute-start(bf16[1056,1024]{1,0:T(8,128)(2,1)} %pad_maximum_fusion.9), channel_id=1, source_target_pairs={{0,4},{4,0},{8,12},{12,8},{16,20},{20,16},{24,28},{28,24},{1,5},{5... | collective-permute-start | bytes 6488072 | tf_op jit(solution)/shard_map/ppermute | solution.py:63
  579.2 109.6 %collective-permute-start.32 = (bf16[640,2048]{1,0:T(8,128)(2,1)}, bf16[640,2048]{1,0:T(8,128)(2,1)}, u32[]{:S(2)}, u32[]{:S(2)}) collective-permute-start(bf16[640,2048]{1,0:T(8,128)(2,1)} %split.1150), channel_id=1, source_target_pairs={{0,1},{1,0},{2,3},{3,2},{4,5},{5,4},{6,7},{7,6},{8,9},{9,8},{10,11... | collective-permute-start | bytes 7864328 | tf_op jit(solution)/shard_map/ppermute | solution.py:67
  607.8 86.0 %collective-permute-start.39 = (bf16[640,2048]{1,0:T(8,128)(2,1)S(1)}, bf16[640,2048]{1,0:T(8,128)(2,1)}, u32[]{:S(2)}, u32[]{:S(2)}) collective-permute-start(bf16[640,2048]{1,0:T(8,128)(2,1)S(1)} %split.1149), channel_id=1, source_target_pairs={{0,1},{1,0},{2,3},{3,2},{4,5},{5,4},{6,7},{7,6},{8,9},{9,8},{10,11... | collective-permute-start | bytes 7864328 | tf_op jit(solution)/shard_map/ppermute | solution.py:67
  612.0 87.6 %collective-permute-start.74 = (bf16[1056,512]{1,0:T(8,128)(2,1)}, bf16[1056,512]{1,0:T(8,128)(2,1)}, u32[]{:S(2)}, u32[]{:S(2)}) collective-permute-start(bf16[1056,512]{1,0:T(8,128)(2,1)} %split.1156), channel_id=1, source_target_pairs={{0,16},{4,20},{8,24},{12,28},{16,0},{20,4},{24,8},{28,12},{1,17},{... | collective-permute-start | bytes 3244040 | tf_op jit(solution)/shard_map/ppermute | solution.py:63
  644.0 86.9 %collective-permute-start.68 = (bf16[1056,512]{1,0:T(8,128)(2,1)}, bf16[1056,512]{1,0:T(8,128)(2,1)}, u32[]{:S(2)}, u32[]{:S(2)}) collective-permute-start(bf16[1056,512]{1,0:T(8,128)(2,1)} %split.1158), channel_id=1, source_target_pairs={{0,16},{4,20},{8,24},{12,28},{16,0},{20,4},{24,8},{28,12},{1,17},{... | collective-permute-start | bytes 3244040 | tf_op jit(solution)/shard_map/ppermute | solution.py:63
  688.7 65.3 %collective-permute-start.71 = (bf16[1056,512]{1,0:T(8,128)(2,1)S(1)}, bf16[1056,512]{1,0:T(8,128)(2,1)}, u32[]{:S(2)}, u32[]{:S(2)}) collective-permute-start(bf16[1056,512]{1,0:T(8,128)(2,1)S(1)} %split.1157), channel_id=1, source_target_pairs={{0,16},{4,20},{8,24},{12,28},{16,0},{20,4},{24,8},{28,12},{1,17},{... | collective-permute-start | bytes 3244040 | tf_op jit(solution)/shard_map/ppermute | solution.py:63
  693.1 85.0 %collective-permute-start.33 = (bf16[320,2048]{1,0:T(8,128)(2,1)S(1)}, bf16[320,2048]{1,0:T(8,128)(2,1)}, u32[]{:S(2)}, u32[]{:S(2)}) collective-permute-start(bf16[320,2048]{1,0:T(8,128)(2,1)S(1)} %split.1154), channel_id=1, source_target_pairs={{0,2},{1,3},{2,0},{3,1},{4,6},{5,7},{6,4},{7,5},{8,10},{9,11},{10,... | collective-permute-start | bytes 3932168 | tf_op jit(solution)/shard_map/ppermute | solution.py:67
  698.1 82.2 %collective-permute-start.40 = (bf16[320,2048]{1,0:T(8,128)(2,1)S(1)}, bf16[320,2048]{1,0:T(8,128)(2,1)S(1)}, u32[]{:S(2)}, u32[]{:S(2)}) collective-permute-start(bf16[320,2048]{1,0:T(8,128)(2,1)S(1)} %split.1153), channel_id=1, source_target_pairs={{0,2},{1,3},{2,0},{3,1},{4,6},{5,7},{6,4},{7,5},{8,10},{9,11},{10,... | collective-permute-start | bytes 3932168 | tf_op jit(solution)/shard_map/ppermute | solution.py:67
  863.6 72.2 %collective-permute-start.64 = (bf16[512,1024]{1,0:T(8,128)(2,1)}, bf16[512,1024]{1,0:T(8,128)(2,1)}, u32[]{:S(2)}, u32[]{:S(2)}) collective-permute-start(bf16[512,1024]{1,0:T(8,128)(2,1)} %split.1159), channel_id=1, source_target_pairs={{0,4},{4,0},{8,12},{12,8},{16,20},{20,16},{24,28},{28,24},{1,5},{5... | collective-permute-start | bytes 3145736 | tf_op jit(solution)/shard_map/ppermute | solution.py:63
  873.5 99.0 %collective-permute-start.58 = (bf16[1024,768]{1,0:T(8,128)(2,1)}, bf16[1024,768]{1,0:T(8,128)(2,1)}, u32[]{:S(2)}, u32[]{:S(2)}) collective-permute-start(bf16[1024,768]{1,0:T(8,128)(2,1)} %split.1151), channel_id=1, source_target_pairs={{0,4},{4,0},{8,12},{12,8},{16,20},{20,16},{24,28},{28,24},{1,5},{5... | collective-permute-start | bytes 4718600 | tf_op jit(solution)/shard_map/ppermute | solution.py:63
  875.9 69.4 %collective-permute-start.44 = (bf16[320,2048]{1,0:T(8,128)(2,1)}, bf16[320,2048]{1,0:T(8,128)(2,1)}, u32[]{:S(2)}, u32[]{:S(2)}) collective-permute-start(bf16[320,2048]{1,0:T(8,128)(2,1)} %split.1152), channel_id=1, source_target_pairs={{0,1},{1,0},{2,3},{3,2},{4,5},{5,4},{6,7},{7,6},{8,9},{9,8},{10,11... | collective-permute-start | bytes 3932168 | tf_op jit(solution)/shard_map/ppermute | solution.py:67
  (178 other events, 3819.7 us)

commit v2 on v1

v2 whole, which is shorter than its diff:
```python
import functools

import jax
import jax.numpy as jnp
from jax import lax
from jax.experimental import pallas as pl
from jax.experimental.pallas import tpu as pltpu
from jax.sharding import PartitionSpec as P

D = 2048
H = 16
HD = 128
RD = 64
VD = 128
KR = 512
TOK = 640
EXPERTS = 4


NORM_EPS = 1e-06
ROPE_BASE = 50000.0


def rms_factor(values):
    return lax.rsqrt(jnp.mean(values * values, axis=-1, keepdims=True) + NORM_EPS)


def norm_back(grad_out, values, factor, gain_vec):
    scaled = grad_out * gain_vec
    inner_sum = jnp.mean(scaled * values, axis=-1, keepdims=True)
    return (
        factor * (scaled - values * factor * factor * inner_sum),
        jnp.sum(grad_out * values * factor, axis=0),
    )


def rotary_tables(positions):
    half_width = RD // 2
    inv_freq = ROPE_BASE ** (-jnp.arange(half_width, dtype=jnp.float32) / half_width)
    angles = positions.astype(jnp.float32)[:, None] * inv_freq[None, :]
    return (jnp.cos(angles), jnp.sin(angles))


def rotate(values, cosine_table, sine_table):
    half_width = values.shape[-1] // 2
    first_half = values[..., :half_width]
    second_half = values[..., half_width:]
    return jnp.concatenate(
        [
            first_half * cosine_table - second_half * sine_table,
            second_half * cosine_table + first_half * sine_table,
        ],
        axis=-1,
    )


def silu_parts(gate_pre):
    sigma_gate = jax.nn.sigmoid(gate_pre)
    return (gate_pre * sigma_gate, sigma_gate * (1.0 + gate_pre * (1.0 - sigma_gate)))


def flip_pairs(count, bit):
    return [(i, i ^ (1 << bit)) for i in range(count)]


def dot(a, b, contract):
    return lax.dot_general(a, b, (contract, ((), ())), preferred_element_type=jnp.float32)


class Line:
    def __init__(self, token):
        self.token = token

    def start(self, values, axis, bit):
        values, _ = lax.optimization_barrier((values, self.token))
        return lax.ppermute(values, axis, flip_pairs(lax.axis_size(axis), bit))

    def wait(self, values, *more):
        values, self.token, *more = lax.optimization_barrier((values, self.token, *more))
        return (values, *more) if more else values


def slot_order(bits):
    order = [0]
    for bit in bits:
        order = order + [j ^ (1 << bit) for j in order]
    return order


def take_slots(values, picks, count, axis):
    size = values.shape[axis] // count
    runs = []
    for k in picks:
        if runs and runs[-1][1] == k:
            runs[-1][1] = k + 1
        else:
            runs.append([k, k + 1])
    parts = [lax.slice_in_dim(values, a * size, b * size, axis=axis) for a, b in runs]
    return parts[0] if len(parts) == 1 else jnp.concatenate(parts, axis=axis)


def reorder(values, order, wanted, axis):
    if order == wanted:
        return values
    return take_slots(values, [order.index(j) for j in wanted], len(order), axis)


def select_blocks(blocks, index):
    step = 1
    while step < len(blocks):
        hit = (index & step) != 0
        blocks = [jnp.where(hit, blocks[i ^ step], blocks[i]) for i in range(len(blocks))]
        step *= 2
    return blocks


def to_slots(values, index, order, axis):
    blocks = select_blocks(jnp.split(values, len(order), axis=axis), index)
    return jnp.concatenate([blocks[j] for j in order], axis=axis)


def from_slots(values, index, order, axis):
    slots = jnp.split(values, len(order), axis=axis)
    blocks = [slots[order.index(i)] for i in range(len(order))]
    return jnp.concatenate(select_blocks(blocks, index), axis=axis)


def halves(values, order, bit, axis):
    keep = [k for k, j in enumerate(order) if not (j >> bit) & 1]
    give = [order.index(order[k] ^ (1 << bit)) for k in keep]
    return (
        take_slots(values, keep, len(order), axis),
        take_slots(values, give, len(order), axis),
        [order[k] for k in keep],
    )


class Sum:
    def __init__(self, line, values, order, bits, axis, name="dp", wire=jnp.bfloat16):
        self.line, self.values, self.order, self.bits = line, values, order, list(bits)
        self.axis, self.name, self.wire = axis, name, wire

    def start(self):
        bit = self.bits.pop(0)
        self.keep, give, self.order = halves(self.values, self.order, bit, self.axis)
        self.flying = self.line.start(give.astype(self.wire), self.name, bit)
        return self

    def wait(self):
        got = self.line.wait(self.flying)
        self.values = self.keep.astype(jnp.float32) + got.astype(jnp.float32)
        return self

    def next(self):
        return self.wait().start()

    def finish(self):
        while self.bits:
            self.start().wait()
        return self.values


class Gather:
    def __init__(self, line, values, bits, name="dp"):
        self.line, self.values, self.bits, self.name = line, values, list(bits), name
        self.order = [0]

    def start(self):
        self.bit = self.bits.pop(0)
        self.flying = self.line.start(self.values, self.name, self.bit)
        return self

    def wait(self):
        got = self.line.wait(self.flying)
        self.values = jnp.concatenate([self.values, got], axis=0)
        self.order = self.order + [j ^ (1 << self.bit) for j in self.order]
        return self

    def next(self):
        return self.wait().start()

    def finish(self):
        while self.bits:
            self.start().wait()
        return self.values


MESH = pl.DeviceIdType.MESH
LANE_CHUNKS = 3


class Copies:
    def __init__(self, send_sems, recv_sems, local_sems):
        self.send_sems, self.recv_sems, self.local_sems = send_sems, recv_sems, local_sems
        self.count = 0
        self.local_count = 0

    def across(self, axis, bit):
        index = lax.axis_index(axis)
        side = lax.rem(index // (1 << bit), 2)
        return {axis: index + (1 - 2 * side) * (1 << bit)}

    def start(self, source, target, axis, bit):
        copy = pltpu.make_async_remote_copy(
            src_ref=source,
            dst_ref=target,
            send_sem=self.send_sems.at[self.count],
            recv_sem=self.recv_sems.at[self.count],
            device_id=self.across(axis, bit),
            device_id_type=MESH,
        )
        self.count += 1
        copy.start()
        return copy

    def local(self, source, target):
        copy = pltpu.make_async_copy(source, target, self.local_sems.at[self.local_count])
        self.local_count += 1
        copy.start()
        return copy

    def greet(self, dp_bits, tensor_bits=(1, 0)):
        barrier = pltpu.get_barrier_semaphore()
        for axis, bits in (("dp", dp_bits), ("tensor", tensor_bits)):
            for bit in bits:
                pl.semaphore_signal(
                    barrier, inc=1, device_id=self.across(axis, bit), device_id_type=MESH
                )
        pl.semaphore_wait(barrier, len(dp_bits) + len(tensor_bits))


class SlotGather:
    def __init__(self, copies, source, slots, bits, axis="dp", cut=None):
        self.copies, self.source, self.slots, self.bits, self.axis = copies, source, slots, list(bits), axis
        self.cut = (slice(None),) if cut is None else (pl.ds(*cut),)
        self.done, self.have, self.own, self.flying = 0, 1, None, None

    def view(self, first, count):
        return self.slots.at[(pl.ds(first, count), *self.cut)]

    def start(self):
        bit = self.bits[self.done]
        if self.done == 0 and self.source is not None:
            source = self.source.at[(pl.ds(0, 1), *self.cut)]
            self.own = self.copies.local(source, self.view(0, 1))
        else:
            if self.own is not None:
                self.own.wait()
                self.own = None
            source = self.view(0, self.have)
        self.flying = self.copies.start(source, self.view(self.have, self.have), self.axis, bit)
        self.done += 1
        self.have *= 2

    def wait(self):
        self.flying.wait()
        self.flying = None
        if self.done < len(self.bits):
            self.start()
        elif self.own is not None:
            self.own.wait()
            self.own = None

    def finish(self):
        while self.flying is not None:
            self.wait()


def gather_kernel(
    n_bits,
    n_pieces,
    width,
    tokens_ref,
    grad_ref,
    grad_over_ref,
    pack_ref,
    keyval_ref,
    query_ref,
    output_ref,
    own_ref,
    other_ref,
    tokens_all,
    grad_pair,
    pack_all,
    keyval_all,
    query_all,
    output_all,
    units_all,
    send_sems,
    recv_sems,
    local_sems,
):
    copies = Copies(send_sems, recv_sems, local_sems)
    merge = 1
    high = list(range(n_bits - 1, 1, -1))
    far_first = high + [merge, 0]
    copies.greet(list(range(n_bits)))

    pack = SlotGather(copies, pack_ref, pack_all.at[0], far_first)
    keyval = SlotGather(copies, keyval_ref, keyval_all, far_first)
    half = query_ref.shape[1] // 2
    query = [
        SlotGather(copies, query_ref, query_all, far_first, cut=(k * half, half)) for k in range(2)
    ]
    tokens = SlotGather(copies, tokens_ref, tokens_all, [1, 0], "tensor")
    output = SlotGather(copies, output_ref, output_all, [0] + high + [merge])
    pack.start()
    keyval.start()
    query[0].start()
    tokens.start()
    output.start()
    query[1].start()

    units = []
    for p in range(n_pieces):
        for part in range(LANE_CHUNKS):
            units.append((p, part))
    chains = [None] * len(units)
    locals_of = [None] * len(units)

    def unit_first(i):
        p, part = units[i]
        cut = pl.ds(part * width, width)
        locals_of[i] = copies.local(own_ref.at[pl.ds(p, 1), cut], units_all.at[p, pl.ds(0, 1), cut])
        chains[i] = copies.start(
            other_ref.at[pl.ds(p, 1), cut], units_all.at[p, pl.ds(1, 1), cut], "dp", merge
        )

    def unit_second(i):
        p, part = units[i]
        chains[i].wait()
        locals_of[i].wait()
        chain = SlotGather(
            copies, None, units_all.at[p], high + [0], cut=(part * width, width)
        )
        chain.have = 2
        chain.start()
        chains[i] = chain

    grad_own = copies.local(grad_ref, grad_pair.at[pl.ds(0, 1)])

    unit_first(0)
    for _ in high:
        pack.wait()
    for _ in high:
        keyval.wait()
    tokens.wait()
    grad_x = copies.start(grad_ref, grad_pair.at[pl.ds(2, 1)], "tensor", 1)
    for _ in high:
        query[0].wait()
    output.wait()
    pack.wait()
    keyval.wait()
    for _ in high:
        query[1].wait()
    unit_second(0)
    unit_first(1)
    query[0].wait()
    pack.wait()
    pack_tensor = SlotGather(copies, None, pack_all, [1, 0], "tensor")
    pack_tensor.start()
    grad_z = copies.start(grad_over_ref, grad_pair.at[pl.ds(1, 1)], "dp", merge)
    query[1].wait()
    unit_second(1)
    unit_first(2)
    for _ in high:
        output.wait()
    grad_x.wait()
    pack_tensor.wait()
    keyval.wait()
    grad_z.wait()
    grad_zx = copies.start(
        grad_pair.at[pl.ds(1, 1)], grad_pair.at[pl.ds(3, 1)], "tensor", 1
    )
    pack_tensor.wait()
    tokens.wait()
    query[0].wait()
    for _ in high:
        chains[0].wait()
    unit_second(2)
    unit_first(3)
    query[1].wait()
    output.wait()
    grad_zx.wait()
    grad_own.wait()
    grad_c = copies.start(grad_pair.at[pl.ds(0, 4)], grad_pair.at[pl.ds(4, 4)], "tensor", 0)
    for i in range(1, len(units)):
        for _ in high:
            chains[i].wait()
        if i + 2 < len(units):
            unit_second(i + 2)
        if i + 3 < len(units):
            unit_first(i + 3)
    grad_c.wait()
    for chain in chains:
        chain.finish()


def gather_all(tokens, grad, grad_over, pack, keyval, query, output, own, other):
    n_dp = lax.axis_size("dp")
    n_bits = n_dp.bit_length() - 1
    n_pieces, width = own.shape[0], own.shape[1] // LANE_CHUNKS
    bf16 = jnp.bfloat16
    n_copies = 5 * (n_bits + 2) + n_pieces * LANE_CHUNKS * n_bits + 8
    any_spec = pl.BlockSpec(memory_space=pl.ANY)
    shapes = [
        (4, *tokens.shape),
        (8, *grad.shape),
        (4, n_dp, *pack.shape),
        (n_dp, *keyval.shape),
        (n_dp, *query.shape),
        (n_dp, *output.shape),
        (n_pieces, n_dp, *own.shape[1:]),
    ]
    operands = [tokens[None], grad[None], grad_over[None], pack[None], keyval[None], query[None], output[None], own, other]
    return pl.pallas_call(
        functools.partial(gather_kernel, n_bits, n_pieces, width),
        out_shape=[jax.ShapeDtypeStruct(s, bf16) for s in shapes],
        in_specs=[any_spec] * len(operands),
        out_specs=[any_spec] * len(shapes),
        scratch_shapes=[
            pltpu.SemaphoreType.DMA((n_copies,)),
            pltpu.SemaphoreType.DMA((n_copies,)),
            pltpu.SemaphoreType.DMA((32,)),
        ],
        compiler_params=pltpu.CompilerParams(collective_id=0, has_side_effects=True),
        name="gather_all",
    )(*operands)


def body(
    res_in,
    out_grad,
    seg_ids,
    tok_counts,
    slot_table,
    slot_gates,
    attn_gain,
    latent_gain,
    ffn_gain,
    w_latent,
    w_query,
    w_keyval,
    w_output,
    w_expert_in,
    w_expert_out,
    w_shared_in,
    w_shared_out,
):
    f32 = jnp.float32
    bf16 = jnp.bfloat16
    n_tensor = lax.axis_size("tensor")
    n_dp = lax.axis_size("dp")
    dp = lax.axis_index("dp")
    tensor = lax.axis_index("tensor")
    merge = 1
    high = list(range(n_dp.bit_length() - 2, 1, -1))
    far_first = high + [merge, 0]
    order = slot_order(far_first)
    tensor_order = slot_order([1, 0])
    rows = res_in.shape[0]
    local_heads = H // n_tensor
    score_scale = (HD + RD) ** (-0.5)
    line = Line(tok_counts)

    def steps(thing, count):
        for _ in range(count):
            thing.wait()
            if thing.bits:
                thing.start()

    res_local = to_slots(res_in, dp, order, 1)
    pack_rows = w_latent.shape[0]
    gain_row = jnp.concatenate([attn_gain, ffn_gain, latent_gain])
    gain_row = jnp.pad(gain_row, (0, w_latent.shape[1] - gain_row.shape[0]))
    pack = jnp.concatenate([w_latent, jnp.broadcast_to(gain_row, (16, w_latent.shape[1]))], axis=0)

    first = ((dp >> merge) & 1) == 0
    n_half = EXPERTS // 2
    width = w_expert_out.shape[1]
    expert_units = jnp.concatenate(
        [
            w_expert_in.transpose(0, 1, 3, 2).reshape(EXPERTS, -1, w_expert_in.shape[2]),
            w_expert_out,
        ],
        axis=1,
    )
    shared_t = w_shared_in.transpose(0, 2, 1)
    units = []
    for side in range(2):
        cut = slice(side * width, (side + 1) * width)
        shared_unit = jnp.concatenate([shared_t[0, cut], shared_t[1, cut], w_shared_out[cut]], axis=0)
        units.append([*expert_units[side * n_half : (side + 1) * n_half], shared_unit])
    own_units = [jnp.where(first, a, b) for a, b in zip(*units)]
    other_units = [jnp.where(first, b, a) for a, b in zip(*units)]

    token_ids = jnp.concatenate(
        [(tensor ^ j) * rows + jnp.arange(rows, dtype=jnp.int32) for j in tensor_order]
    )
    segment_canon = seg_ids[0]
    segment_row = jnp.concatenate(
        [lax.dynamic_slice_in_dim(segment_canon, (tensor ^ j) * rows, rows) for j in tensor_order]
    )
    valid_all = (token_ids < tok_counts[0]).astype(f32)
    valid_rows = valid_all[:rows, None]
    group_gate = jnp.sum(
        jnp.where(slot_table[0][:, :, None] == token_ids[None, None, :], slot_gates[0][:, :, None], 0.0),
        axis=1,
    )
    grad_in = to_slots(out_grad, dp, order, 1).astype(f32)
    ffn_grad = (valid_rows * grad_in).astype(bf16)

    def partner_columns(values):
        return take_slots(
            values, [order.index(j ^ (1 << merge)) for j in order], n_dp, values.ndim - 1
        )

    over_gate = lax.ppermute(group_gate, "dp", flip_pairs(n_dp, merge))
    (
        tokens_all,
        grad_pair,
        pack_all,
        keyval_slots,
        query_slots,
        output_slots,
        units_all,
    ) = gather_all(
        res_local,
        ffn_grad,
        partner_columns(ffn_grad),
        pack,
        w_keyval,
        w_query,
        w_output,
        jnp.stack(own_units),
        jnp.stack(other_units),
    )
    grad_pair = grad_pair.reshape(-1, D)
    other_gate = over_gate

    pack_blocks = [pack_all[tensor_order.index(j)] for j in range(n_tensor)]
    pack_all = jnp.stack(select_blocks(pack_blocks, tensor), axis=1)
    latent_full = pack_all[:, :, :pack_rows].reshape(D, KR + RD)
    gains = pack_all[:, :, pack_rows]
    gain_width, latent_width = D // (n_dp * n_tensor), KR // (n_dp * n_tensor)
    attn_gain_full = gains[..., :gain_width].reshape(D)
    ffn_gain_full = gains[..., gain_width : 2 * gain_width].reshape(D)
    latent_gain_full = from_slots(
        gains[..., 2 * gain_width : 2 * gain_width + latent_width].reshape(KR), dp, order, 0
    )
    keyval_full = from_slots(keyval_slots.reshape(KR, -1), dp, order, 0)

    positions = token_ids - jnp.sum(
        (segment_canon[None, :] < segment_row[:, None]).astype(jnp.int32), axis=1
    )
    cos_all, sin_all = rotary_tables(positions)
    allowed = (segment_row[:, None] == segment_row[None, :]) & (
        token_ids[None, :] <= token_ids[:, None]
    )
    resid_all = tokens_all.reshape(TOK, D).astype(f32)
    in_factor = rms_factor(resid_all)
    normed_all = (resid_all * in_factor * attn_gain_full).astype(bf16)
    latent_raw = jnp.dot(normed_all, latent_full, preferred_element_type=f32)
    latent_c = latent_raw[:, :KR]
    latent_factor = rms_factor(latent_c)
    latent_norm = (latent_c * latent_factor * latent_gain_full).astype(bf16)
    rope_all = rotate(latent_raw[:, KR:], cos_all, sin_all).astype(bf16)
    keyval_all = (
        jnp.dot(latent_norm, keyval_full, preferred_element_type=f32)
        .astype(bf16)
        .reshape(TOK, local_heads, HD + VD)
    )
    key_nope = keyval_all[..., :HD]
    values_all = keyval_all[..., HD:]

    query_full = query_slots.reshape(D, -1)
    query_raw = jnp.dot(normed_all, query_full, preferred_element_type=f32).reshape(
        TOK, local_heads, HD + RD
    )
    query_final = jnp.concatenate(
        [
            query_raw[..., :HD],
            rotate(query_raw[..., HD:], cos_all[:, None, :], sin_all[:, None, :]),
        ],
        axis=-1,
    ).astype(bf16)
    raw_scores = jnp.einsum(
        "qhd,khd->hqk", query_final[..., :HD], key_nope, preferred_element_type=f32
    )
    raw_scores = raw_scores + jnp.einsum(
        "qhr,kr->hqk", query_final[..., HD:], rope_all, preferred_element_type=f32
    )
    scores = jnp.where(allowed[None], raw_scores * score_scale, -1e30)
    top_score = jnp.max(scores, axis=-1, keepdims=True)
    exp_scores = jnp.exp(scores - top_score)
    probs_all = exp_scores / jnp.sum(exp_scores, axis=-1, keepdims=True)
    probs_low = probs_all.astype(bf16)
    attn_mix = (
        jnp.einsum("hqk,khd->qhd", probs_low, values_all, preferred_element_type=f32)
        .astype(bf16)
        .reshape(TOK, local_heads * VD)
    )
    output_order = slot_order([0] + high + [merge])
    output_full = jnp.concatenate([output_slots[output_order.index(j)] for j in order], axis=1)
    attn_part = jnp.dot(attn_mix, output_full, preferred_element_type=f32)
    attn_sum = Sum(line, attn_part, tensor_order, [0, 1], 0, "tensor").start()
    steps(attn_sum, 1)
    steps(attn_sum, 1)
    attn_out = attn_sum.values
    resid_in = res_local.astype(f32)
    mid_resid = resid_in + valid_rows * attn_out
    mid_factor = rms_factor(mid_resid)
    normed_mid = (mid_resid * mid_factor * ffn_gain_full).astype(bf16)

    mid_x = line.start(normed_mid, "tensor", 1)
    mid_z = line.start(partner_columns(normed_mid), "dp", merge)
    mid_z = line.wait(mid_z)
    mid_x = line.wait(mid_x)
    mid_zx = line.start(mid_z, "tensor", 1)
    mid_zx = line.wait(mid_zx)
    mid_own = jnp.concatenate([normed_mid, mid_z, mid_x, mid_zx], axis=0)
    mid_c = line.start(mid_own, "tensor", 0)
    mid_pair = jnp.concatenate([mid_own, line.wait(mid_c)], axis=0)

    unit_order = slot_order([merge] + high + [0])
    gate_rows = []
    for slot in range(n_tensor):
        place = [0, 1, 2, 3][slot]
        for gate in (group_gate, other_gate):
            gate_rows.append(gate[:, place * rows : (place + 1) * rows])
    pair_gate = jnp.concatenate(gate_rows, axis=1)
    pair_gate = jnp.where(first, pair_gate[:n_half], pair_gate[n_half:])
    mid_pair_grad = None
    hidden_parts, out_parts, unit_sums = [], [], []
    for p in range(n_half + 1):
        piece = jnp.concatenate([units_all[p, unit_order.index(j)] for j in order], axis=1)
        gate_up = dot(piece[: 2 * width], mid_pair, ((1,), (1,)))
        gate_pre, up = gate_up[:width], gate_up[width:]
        silu, slope = silu_parts(gate_pre)
        hidden_grad = dot(piece[2 * width :], grad_pair, ((1,), (1,)))
        hidden = silu * up
        if p < n_half:
            hidden = hidden * pair_gate[p][None]
            hidden_grad = hidden_grad * pair_gate[p][None]
        hidden = hidden.astype(bf16)
        pre_grad = jnp.concatenate(
            [(hidden_grad * up * slope).astype(bf16), (hidden_grad * silu).astype(bf16)], axis=0
        )
        back = dot(pre_grad, piece[: 2 * width], ((0,), (0,)))
        mid_pair_grad = back if mid_pair_grad is None else mid_pair_grad + back
        hidden_parts.append(hidden)
        out_parts.append(piece[2 * width :])
        if p == n_half:
            mid_sum = Sum(line, mid_pair_grad, [0, 1], [0], 0, "tensor").start()
        in_wgrad = dot(pre_grad, mid_pair, ((1,), (0,)))
        out_wgrad = dot(hidden, grad_pair, ((1,), (0,)))
        unit_grad = jnp.concatenate([in_wgrad, out_wgrad], axis=0).astype(bf16)
        unit_sums.append(Sum(line, unit_grad, order, [0] + high[::-1] + [merge], 1).start())
    mid_sum.wait()
    mid_sum = Sum(line, mid_sum.values, [0, 2], [1], 0, "tensor").start()
    unit_sums[0].wait().start()
    ffn_part = dot(
        jnp.concatenate(hidden_parts, axis=0), jnp.concatenate(out_parts, axis=0), ((0,), (0,))
    )
    mid_sum.wait()
    own_part, over_part = jnp.split(mid_sum.values, 2, axis=0)
    mid_over = line.start(partner_columns(over_part).astype(bf16), "dp", merge)
    unit_sums[1].wait().start()
    mid_grad_local = own_part + line.wait(mid_over).astype(f32)

    mid_back, ffn_gain_part = norm_back(mid_grad_local, mid_resid, mid_factor, ffn_gain_full)
    mid_grad = grad_in + mid_back
    attn_grad = (valid_rows * mid_grad).astype(bf16)
    back_tokens = Gather(line, attn_grad, [1, 0], "tensor").start()
    for _ in high[1:]:
        unit_sums[0].wait().start()
    steps(back_tokens, 1)
    unit_sums[2].wait().start()
    steps(back_tokens, 1)
    attn_grad_all = back_tokens.values
    output_wgrad = dot(attn_mix, attn_grad_all, ((0,), (0,)))
    mix_grad = (
        dot(attn_grad_all, output_full, ((1,), (1,))).astype(bf16).reshape(TOK, local_heads, VD)
    )
    output_sum = Sum(line, output_wgrad, order, [merge] + high[::-1] + [0], 1).start()
    ffn_sum = Sum(line, ffn_part, [0, 1], [0], 0, "tensor").start()
    probs_grad = jnp.einsum("qhd,khd->hqk", mix_grad, values_all, preferred_element_type=f32)
    value_grad = jnp.einsum("hqk,qhd->khd", probs_low, mix_grad, preferred_element_type=f32)
    scores_grad = (
        probs_all * (probs_grad - jnp.sum(probs_all * probs_grad, axis=-1, keepdims=True))
    ).astype(bf16)
    query_nope_grad = (
        jnp.einsum("hqk,khd->qhd", scores_grad, key_nope, preferred_element_type=f32) * score_scale
    )
    query_rope_grad = (
        jnp.einsum("hqk,kr->qhr", scores_grad, rope_all, preferred_element_type=f32) * score_scale
    )
    key_nope_grad = (
        jnp.einsum("hqk,qhd->khd", scores_grad, query_final[..., :HD], preferred_element_type=f32)
        * score_scale
    )
    rope_key_grad = (
        jnp.einsum("hqk,qhr->kr", scores_grad, query_final[..., HD:], preferred_element_type=f32)
        * score_scale
    )
    query_grad = (
        jnp.concatenate(
            [query_nope_grad, rotate(query_rope_grad, cos_all[:, None, :], -sin_all[:, None, :])],
            axis=-1,
        )
        .astype(bf16)
        .reshape(TOK, local_heads * (HD + RD))
    )
    keyval_grad = (
        jnp.concatenate([key_nope_grad, value_grad], axis=-1)
        .astype(bf16)
        .reshape(TOK, local_heads * (HD + VD))
    )
    unit_sums[0].wait().start()
    ffn_sum.wait()
    query_wgrad = dot(normed_all, query_grad, ((0,), (0,)))
    query_sum = Sum(line, query_wgrad, order, far_first[::-1], 0).start()
    latent_part = jnp.concatenate([dot(keyval_grad, keyval_full, ((1,), (1,))), rope_key_grad], axis=1)
    normed_part = dot(query_grad, query_full, ((1,), (1,)))
    back_part = jnp.concatenate([latent_part, normed_part], axis=1)
    back_sum = Sum(line, back_part, tensor_order, [0, 1], 0, "tensor").start()
    keyval_wgrad = to_slots(dot(latent_norm, keyval_grad, ((0,), (0,))).astype(bf16), dp, order, 0)
    keyval_sum = Sum(line, keyval_wgrad, order, far_first[::-1], 0).start()
    back_sum.wait().start()
    output_sum.wait().start()
    for _ in high[1:]:
        unit_sums[1].wait().start()
    unit_sums[1].wait().start()
    back_sum.wait()
    latent_grad_local = back_sum.values[:, : KR + RD]
    normed_grad_local = back_sum.values[:, KR + RD :]
    latent_c_grad, latent_gain_part = norm_back(
        latent_grad_local[:, :KR], latent_c[:rows], latent_factor[:rows], latent_gain_full
    )
    rope_raw_grad = rotate(latent_grad_local[:, KR:], cos_all[:rows], -sin_all[:rows])
    latent_raw_grad = jnp.concatenate([latent_c_grad, rope_raw_grad], axis=1).astype(bf16)
    latent_back = Gather(line, latent_raw_grad, [1, 0], "tensor").start()
    for _ in high:
        output_sum.wait().start()
    keyval_sum.wait().start()
    latent_back.wait().start()
    query_sum.wait().start()
    latent_back.wait()
    latent_wgrad = dot(normed_all, latent_back.values, ((0,), (0,))).astype(bf16)
    latent_wgrad = lax.dynamic_index_in_dim(
        latent_wgrad.reshape(n_dp, n_tensor, pack_rows, KR + RD), tensor, 1, keepdims=False
    )
    latent_sum = Sum(line, latent_wgrad, order, far_first[::-1], 0).start()
    normed_grad = normed_grad_local + dot(latent_raw_grad, latent_full, ((1,), (1,)))
    in_back, attn_gain_part = norm_back(normed_grad, resid_in, in_factor[:rows], attn_gain_full)
    res_grad = mid_grad + in_back
    gain_parts = jnp.concatenate(
        [
            attn_gain_part.reshape(n_dp, n_tensor, gain_width),
            ffn_gain_part.reshape(n_dp, n_tensor, gain_width),
            to_slots(latent_gain_part, dp, order, 0).reshape(n_dp, n_tensor, latent_width),
        ],
        axis=2,
    )
    gain_blocks = select_blocks([gain_parts[:, i] for i in range(n_tensor)], tensor)
    gain_parts = jnp.stack([gain_blocks[j] for j in tensor_order], axis=0)
    gain_sum = Sum(line, gain_parts, tensor_order, [0, 1], 0, "tensor", f32).start()
    output_owned = output_sum.wait().values
    ffn_sum = Sum(line, ffn_sum.values, [0, 2], [1], 0, "tensor").start()
    for _ in high:
        unit_sums[2].wait().start()
    keyval_sum.wait().start()
    gain_sum.wait().start()
    latent_sum.wait().start()
    query_sum.wait().start()
    ffn_sum.wait()
    ffn_own, ffn_over = jnp.split(ffn_sum.values, 2, axis=0)
    ffn_over = line.start(partner_columns(ffn_over).astype(bf16), "dp", merge)
    gain_sum.wait()
    gain_dp = Sum(line, gain_sum.values[0], order, far_first[::-1], 0, "dp", f32).start()
    for _ in high[1:]:
        keyval_sum.wait().start()
        latent_sum.wait().start()
        query_sum.wait().start()
        gain_dp.wait().start()
    latent_sum.wait().start()
    gain_dp.wait().start()
    ffn_out = ffn_own + line.wait(ffn_over).astype(f32)
    res_out = (mid_resid + valid_rows * ffn_out).astype(bf16)
    own_grads, other_grads = [], []
    for s in unit_sums:
        other_grads.append(line.wait(s.flying).astype(f32))
        own_grads.append(s.keep)
    gain_dp.wait().start()
    keyval_owned = keyval_sum.wait().values
    latent_owned = latent_sum.wait().values[0]
    query_owned = query_sum.wait().values
    gain_owned = gain_dp.wait().values[0]

    sides = []
    for side in (first, ~first):
        sides.append([jnp.where(side, a, b) for a, b in zip(own_grads, other_grads)])
    expert_units = jnp.stack([unit for side in sides for unit in side[:n_half]], axis=0)
    expert_in_owned = expert_units[:, : 2 * width].reshape(EXPERTS, 2, width, -1).transpose(0, 1, 3, 2)
    expert_out_owned = expert_units[:, 2 * width :]
    shared_in_owned = jnp.stack(
        [
            jnp.concatenate([side[n_half][k * width : (k + 1) * width] for side in sides], axis=0).T
            for k in range(2)
        ],
        axis=0,
    )
    shared_out_owned = jnp.concatenate([side[n_half][2 * width :] for side in sides], axis=0)
    return (
        from_slots(res_out, dp, order, 1),
        from_slots(res_grad, dp, order, 1),
        gain_owned[:gain_width],
        gain_owned[2 * gain_width :],
        gain_owned[gain_width : 2 * gain_width],
        latent_owned,
        query_owned,
        keyval_owned,
        output_owned,
        expert_in_owned,
        expert_out_owned,
        shared_in_owned,
        shared_out_owned,
    )


def solution(mesh):
    placed = (
        P(("dp", "tensor"), None),
        P(("dp", "tensor"), None),
        P("dp", None),
        P("dp"),
        P("dp", None, None),
        P("dp", None, None),
        P(("dp", "tensor")),
        P(("dp", "tensor")),
        P(("dp", "tensor")),
        P(("dp", "tensor"), None),
        P("dp", "tensor"),
        P("dp", "tensor"),
        P("tensor", "dp"),
        P(None, None, "dp", "tensor"),
        P(None, "tensor", "dp"),
        P(None, "dp", "tensor"),
        P("tensor", "dp"),
    )
    return jax.shard_map(
        body,
        mesh=mesh,
        in_specs=placed,
        out_specs=(
            P(("dp", "tensor"), None),
            P(("dp", "tensor"), None),
            P(("dp", "tensor")),
            P(("dp", "tensor")),
            P(("dp", "tensor")),
            P(("dp", "tensor"), None),
            P("dp", "tensor"),
            P("dp", "tensor"),
            P("tensor", "dp"),
            P(None, None, "dp", "tensor"),
            P(None, "tensor", "dp"),
            P(None, "dp", "tensor"),
            P("tensor", "dp"),
        ),
        check_vma=False,
    )
```

time: 1040 us -> 986 us (0.948)
  waiting for transfers between devices: 591 us -> 222 us
  Pallas kernels: 0 us -> 275 us
  local copies, waits for them, and re-layouts: 109 us -> 148 us
  other arithmetic: 99.5 us -> 119 us
  starting transfers between devices: 58.9 us -> 44.6 us
    ppermute x76 -> x45, waiting for transfers between devices: 591 us -> 222 us  [the longest x44 222 us: start(): return lax.ppermute(values, axis, flip_pairs(lax.axis_size(axis), bit))]
    pallas_call x0 -> x1, Pallas kernels: none -> 275 us  [gather_all(): pl.pallas_call(functools.partial(gather_kernel, n_bits, n_pieces, width),...]
    slice x6 -> x45, local copies, waits for them, and re-layouts: 5.33 us -> 32.1 us  [the longest x38 24.1 us: take_slots(): lax.slice_in_dim(values, a * size, b * size, axis=axis)]
    split x29 -> x0, local copies, waits for them, and re-layouts: 15.1 us -> none  [the longest x9 6.91 us: scatter_tensor(): keep, give = jnp.split(values, 2, axis=0)]
    ppermute x76 -> x45, starting transfers between devices: 58.9 us -> 44.6 us  [the longest x44 44.5 us: start(): return lax.ppermute(values, axis, flip_pairs(lax.axis_size(axis), bit))]
    another operation x12 -> x14, other arithmetic: 5.92 us -> 18.3 us
    concatenate x25 -> x17, other arithmetic: 26.6 us -> 15.3 us  [the longest x3 5.08 us: body(): unit_grad = jnp.concatenate([in_wgrad, out_wgrad], axis=0).astype(bf16)]
    add x28 -> x23, other arithmetic: 34.9 us -> 25.3 us  [wait(): self.values = self.keep.astype(jnp.float32) + got.astype(jnp.float32)]
  transfers between devices with their start and end apart: 76 -> 45, of which waited for: 38 -> 16; matrix products, arithmetic and copies ran while one was open for 26% -> 26% of each run, Pallas kernels for 0% -> 0%
where the time goes in v2:
time: 986 us; the launch traced here: 976 us
  Pallas kernels  275 us (28%)
  waiting for transfers between devices  222 us (23%)
  matrix products  164 us (17%)
  local copies, waits for them, and re-layouts  148 us (15%)
  other arithmetic  119 us (12%)
  starting transfers between devices  44.6 us (5%)
    pallas_call x1, Pallas kernels, gather_all(): pl.pallas_call(functools.partial(gather_kernel, n_bits, n_pieces, width),...  275 us
    ppermute x44, waiting for transfers between devices, start(): return lax.ppermute(values, axis, flip_pairs(lax.axis_size(axis), bit))  222 us
    dot_general x24, matrix products, dot(): lax.dot_general(a, b, (contract, ((), ())), preferred_element_type=jnp.fl...  128 us
    unnamed x364, local copies, waits for them, and re-layouts  59.3 us
    ppermute x44, starting transfers between devices, start(): return lax.ppermute(values, axis, flip_pairs(lax.axis_size(axis), bit))  44.5 us
    add x23, other arithmetic, wait(): self.values = self.keep.astype(jnp.float32) + got.astype(jnp.float32)  25.3 us
    slice x38, local copies, waits for them, and re-layouts, take_slots(): lax.slice_in_dim(values, a * size, b * size, axis=axis)  24.1 us
  transfers between devices with their start and end apart: 45, of which 16 were waited for; matrix products, arithmetic and copies ran while one was open for 26% of the time, Pallas kernels for 0%

profile of v2, /device:TPU:0, one launch (start us, length us, event | category | flops | bytes accessed | tf_op | source)
XLA Modules:
  0.0 976.4 jit_solution(13412168132828714614)
XLA Ops:
  25.1 274.6 %gather_all.1 = (bf16[4,160,2048]{2,1,0:T(8,128)(2,1)}, bf16[8,160,2048]{2,1,0:T(8,128)(2,1)}, bf16[4,8,80,576]{3,2,1,0:T(8,128)(2,1)}, bf16[8,64,1024]{2,1,0:T(...) custom-call(bf16[1,160,2048]{2,1,0:T(8,128)(2,1)} %bitcast.277, ...), custom_call_target="tpu_custom_call" | custom-call | tf_op jit(solution)/shard_map/gather_all/pallas_call | solution.py:416
  358.3 13.1 %copy.163 = bf16[640,4,128]{0,2,1:T(8,128)(2,1)} copy(bf16[640,4,128]{2,1,0:T(4,128)(2,1)S(1)} %get-tuple-element.464) | data formatting | bytes 1310720
  371.3 6.8 fusion.39
  393.8 10.5 %collective-permute-done.1 = bf16[160,2048]{1,0:T(8,128)(2,1)} collective-permute-done((bf16[160,2048]{1,0:T(8,128)(2,1)}, bf16[160,2048]{1,0:T(8,128)(2,1)}, u32[]{:S(2)}, u32[]{:S(2)}) %collective-permute-start.1) | collective-permute-done | bytes 655392 | tf_op jit(solution)/shard_map/ppermute | solution.py:76
  415.4 8.7 collective-permute-done.2
  431.4 8.5 collective-permute-done.4
  468.8 7.4 fusion.25
  476.2 5.8 fusion.21
  491.4 8.6 fusion.23
  510.9 8.7 fusion.19
  540.5 16.7 %add_add_fusion = f32[1280,2048]{1,0:T(8,128)} fusion(f32[1280,2048]{1,0:T(8,128)} %fusion.23, f32[1280,2048]{1,0:T(8,128)} %fusion.19, bf16[1056,2048]{1,0:T(8,128)(2,1)} %get-tuple-element.386, bf16[352,1280]{1,0:T(8,128)(2,1)} %copy-done.149, bf16[352,1280]{1,0:T(8,128)(2,1)} %copy-done.148), kind=kOutput, calls=%fused_computation.1 | convolution fusion | flops 3699834880 | bytes 36143104 | tf_op jit(solution)/shard_map/dot_general | solution.py:67
  575.1 9.6 fusion.5
  586.8 6.3 slice_add_fusion
  600.8 24.2 %collective-permute-done.8 = bf16[320,2048]{1,0:T(8,128)(2,1)S(1)} collective-permute-done((bf16[320,2048]{1,0:T(8,128)(2,1)}, bf16[320,2048]{1,0:T(8,128)(2,1)S(1)}, u32[]{:S(2)}, u32[]{:S(2)}) %collective-permute-start.8) | collective-permute-done | bytes 1310752 | tf_op jit(solution)/shard_map/ppermute | solution.py:76
  625.0 45.8 %collective-permute-done.11 = bf16[1056,1024]{1,0:T(8,128)(2,1)} collective-permute-done((bf16[1056,1024]{1,0:T(8,128)(2,1)}, bf16[1056,1024]{1,0:T(8,128)(2,1)}, u32[]{:S(2)}, u32[]{:S(2)}) %collective-permute-start.11) | collective-permute-done | bytes 2162720 | tf_op jit(solution)/shard_map/ppermute | solution.py:76
  675.5 12.5 %collective-permute-done.10 = bf16[160,2048]{1,0:T(8,128)(2,1)S(1)} collective-permute-done((bf16[160,2048]{1,0:T(8,128)(2,1)S(1)}, bf16[160,2048]{1,0:T(8,128)(2,1)S(1)}, u32[]{:S(2)}, u32[]{:S(2)}) %collective-permute-start.10) | collective-permute-done | bytes 655392 | tf_op jit(solution)/shard_map/ppermute | solution.py:76
  695.4 11.0 %collective-permute-done.12 = bf16[160,2048]{1,0:T(8,128)(2,1)} collective-permute-done((bf16[160,2048]{1,0:T(8,128)(2,1)S(1)}, bf16[160,2048]{1,0:T(8,128)(2,1)}, u32[]{:S(2)}, u32[]{:S(2)}) %collective-permute-start.12) | collective-permute-done | bytes 655392 | tf_op jit(solution)/shard_map/ppermute | solution.py:76
  722.5 7.6 fusion.58
  746.9 8.9 concatenate.314
  779.1 41.3 %collective-permute-done.17 = bf16[512,1024]{1,0:T(8,128)(2,1)} collective-permute-done((bf16[512,1024]{1,0:T(8,128)(2,1)}, bf16[512,1024]{1,0:T(8,128)(2,1)}, u32[]{:S(2)}, u32[]{:S(2)}) %collective-permute-start.17) | collective-permute-done | bytes 1048608 | tf_op jit(solution)/shard_map/ppermute | solution.py:76
  827.5 13.9 %collective-permute-done.20 = bf16[160,2624]{1,0:T(8,128)(2,1)S(1)} collective-permute-done((bf16[160,2624]{1,0:T(8,128)(2,1)S(1)}, bf16[160,2624]{1,0:T(8,128)(2,1)S(1)}, u32[]{:S(2)}, u32[]{:S(2)}) %collective-permute-start.20) | collective-permute-done | bytes 839712 | tf_op jit(solution)/shard_map/ppermute | solution.py:76
  842.4 6.7 collective-permute-done.19
  910.7 11.4 %collective-permute-done.43 = bf16[256,768]{1,0:T(8,128)(2,1)S(1)} collective-permute-done((bf16[256,768]{1,0:T(8,128)(2,1)S(1)}, bf16[256,768]{1,0:T(8,128)(2,1)S(1)}, u32[]{:S(2)}, u32[]{:S(2)}) %collective-permute-start.43) | collective-permute-done | bytes 393248 | tf_op jit(solution)/shard_map/ppermute | solution.py:76
  936.9 21.1 %collective-permute-done.42 = bf16[1,64,576]{2,1,0:T(8,128)(2,1)S(1)} collective-permute-done((bf16[1,64,576]{2,1,0:T(8,128)(2,1)S(1)}, bf16[1,64,576]{2,1,0:T(8,128)(2,1)S(1)}, u32[]{:S(2)}, u32[]{:S(2)}) %collective-permute-start.42) | collective-permute-done | bytes 73760 | tf_op jit(solution)/shard_map/ppermute | solution.py:76
  (736 shorter events, 382.1 us)
Async XLA Ops:
  383.1 76.9 %collective-permute-start.6 = (f32[4,640]{1,0:T(4,128)S(1)}, f32[4,640]{1,0:T(4,128)S(1)}, u32[]{:S(2)}, u32[]{:S(2)}) collective-permute-start(f32[4,640]{1,0:T(4,128)S(1)} %select_reduce_fusion), channel_id=1, source_target_pairs={{0,8},{4,12},{8,0},{12,4},{16,24},{20,28},{24,16},{28,20},{1,9},{5... | collective-permute-start | bytes 30728 | tf_op jit(solution)/shard_map/ppermute | solution.py:518
  442.6 22.6 %collective-permute-start.5 = (bf16[640,2048]{1,0:T(8,128)(2,1)}, bf16[640,2048]{1,0:T(8,128)(2,1)}, u32[]{:S(2)}, u32[]{:S(2)}) collective-permute-start(bf16[640,2048]{1,0:T(8,128)(2,1)} %pad_maximum_fusion.4), channel_id=1, source_target_pairs={{0,1},{1,0},{2,3},{3,2},{4,5},{5,4},{6,7},{7,6},{8,9},{9,8},{10,11... | collective-permute-start | bytes 7864328 | tf_op jit(solution)/shard_map/ppermute | solution.py:76
  528.3 58.5 %collective-permute-start.9 = (bf16[1056,1024]{1,0:T(8,128)(2,1)}, bf16[1056,1024]{1,0:T(8,128)(2,1)}, u32[]{:S(2)}, u32[]{:S(2)}) collective-permute-start(bf16[1056,1024]{1,0:T(8,128)(2,1)} %fusion.29), channel_id=1, source_target_pairs={{0,4},{4,0},{8,12},{12,8},{16,20},{20,16},{24,28},{28,24},{1,5},{5... | collective-permute-start | bytes 6488072 | tf_op jit(solution)/shard_map/ppermute | solution.py:76
  560.2 26.6 %collective-permute-start.7 = (bf16[640,2048]{1,0:T(8,128)(2,1)S(1)}, bf16[640,2048]{1,0:T(8,128)(2,1)}, u32[]{:S(2)}, u32[]{:S(2)}) collective-permute-start(bf16[640,2048]{1,0:T(8,128)(2,1)S(1)} %slice.1710), channel_id=1, source_target_pairs={{0,1},{1,0},{2,3},{3,2},{4,5},{5,4},{6,7},{7,6},{8,9},{9,8},{10,11... | collective-permute-start | bytes 7864328 | tf_op jit(solution)/shard_map/ppermute | solution.py:76
  566.8 139.5 %collective-permute-start.14 = (bf16[1056,1024]{1,0:T(8,128)(2,1)}, bf16[1056,1024]{1,0:T(8,128)(2,1)}, u32[]{:S(2)}, u32[]{:S(2)}) collective-permute-start(bf16[1056,1024]{1,0:T(8,128)(2,1)} %fusion.27), channel_id=1, source_target_pairs={{0,4},{4,0},{8,12},{12,8},{16,20},{20,16},{24,28},{28,24},{1,5},{5... | collective-permute-start | bytes 6488072 | tf_op jit(solution)/shard_map/ppermute | solution.py:76
  574.0 96.8 %collective-permute-start.11 = (bf16[1056,1024]{1,0:T(8,128)(2,1)}, bf16[1056,1024]{1,0:T(8,128)(2,1)}, u32[]{:S(2)}, u32[]{:S(2)}) collective-permute-start(bf16[1056,1024]{1,0:T(8,128)(2,1)} %fusion.28), channel_id=1, source_target_pairs={{0,4},{4,0},{8,12},{12,8},{16,20},{20,16},{24,28},{28,24},{1,5},{5... | collective-permute-start | bytes 6488072 | tf_op jit(solution)/shard_map/ppermute | solution.py:76
  594.4 30.6 %collective-permute-start.8 = (bf16[320,2048]{1,0:T(8,128)(2,1)}, bf16[320,2048]{1,0:T(8,128)(2,1)S(1)}, u32[]{:S(2)}, u32[]{:S(2)}) collective-permute-start(bf16[320,2048]{1,0:T(8,128)(2,1)} %slice.1715), channel_id=1, source_target_pairs={{0,2},{1,3},{2,0},{3,1},{4,6},{5,7},{6,4},{7,5},{8,10},{9,11},{10,... | collective-permute-start | bytes 3932168 | tf_op jit(solution)/shard_map/ppermute | solution.py:76
  599.1 135.3 %collective-permute-start.16 = (bf16[1056,512]{1,0:T(8,128)(2,1)}, bf16[1056,512]{1,0:T(8,128)(2,1)}, u32[]{:S(2)}, u32[]{:S(2)}) collective-permute-start(bf16[1056,512]{1,0:T(8,128)(2,1)} %pad_maximum_fusion.24), channel_id=1, source_target_pairs={{0,16},{4,20},{8,24},{12,28},{16,0},{20,4},{24,8},{28,12},{1,17},{... | collective-permute-start | bytes 3244040 | tf_op jit(solution)/shard_map/ppermute | solution.py:76
  693.0 127.5 %collective-permute-start.21 = (bf16[1056,512]{1,0:T(8,128)(2,1)}, bf16[1056,512]{1,0:T(8,128)(2,1)}, u32[]{:S(2)}, u32[]{:S(2)}) collective-permute-start(bf16[1056,512]{1,0:T(8,128)(2,1)} %pad_maximum_fusion.25), channel_id=1, source_target_pairs={{0,16},{4,20},{8,24},{12,28},{16,0},{20,4},{24,8},{28,12},{1,17},{... | collective-permute-start | bytes 3244040 | tf_op jit(solution)/shard_map/ppermute | solution.py:76
  711.5 171.6 %collective-permute-start.32 = (bf16[1056,512]{1,0:T(8,128)(2,1)}, bf16[1056,512]{1,0:T(8,128)(2,1)}, u32[]{:S(2)}, u32[]{:S(2)}) collective-permute-start(bf16[1056,512]{1,0:T(8,128)(2,1)} %pad_maximum_fusion.26), channel_id=1, source_target_pairs={{0,16},{4,20},{8,24},{12,28},{16,0},{20,4},{24,8},{28,12},{1,17},{... | collective-permute-start | bytes 3244040 | tf_op jit(solution)/shard_map/ppermute | solution.py:76
  737.6 224.9 %collective-permute-start.40 = (bf16[1056,256]{1,0:T(8,128)(2,1)}, bf16[1056,256]{1,0:T(8,128)(2,1)}, u32[]{:S(2)}, u32[]{:S(2)}) collective-permute-start(bf16[1056,256]{1,0:T(8,128)(2,1)} %slice.1720), channel_id=1, source_target_pairs={{0,8},{4,12},{8,0},{12,4},{16,24},{20,28},{24,16},{28,20},{1,9},{5... | collective-permute-start | bytes 1622024 | tf_op jit(solution)/shard_map/ppermute | solution.py:76
  738.5 27.4 %collective-permute-start.15 = (bf16[640,2048]{1,0:T(8,128)(2,1)S(1)}, bf16[640,2048]{1,0:T(8,128)(2,1)}, u32[]{:S(2)}, u32[]{:S(2)}) collective-permute-start(bf16[640,2048]{1,0:T(8,128)(2,1)S(1)} %copy-done.52), channel_id=1, source_target_pairs={{0,1},{1,0},{2,3},{3,2},{4,5},{5,4},{6,7},{7,6},{8,9},{9,8},{10,11... | collective-permute-start | bytes 7864328 | tf_op jit(solution)/shard_map/ppermute | solution.py:76
  762.7 57.8 %collective-permute-start.17 = (bf16[512,1024]{1,0:T(8,128)(2,1)}, bf16[512,1024]{1,0:T(8,128)(2,1)}, u32[]{:S(2)}, u32[]{:S(2)}) collective-permute-start(bf16[512,1024]{1,0:T(8,128)(2,1)} %pad_maximum_fusion.29), channel_id=1, source_target_pairs={{0,8},{4,12},{8,0},{12,4},{16,24},{20,28},{24,16},{28,20},{1,9},{5... | collective-permute-start | bytes 3145736 | tf_op jit(solution)/shard_map/ppermute | solution.py:76
  778.5 70.6 %collective-permute-start.24 = (bf16[256,1024]{1,0:T(8,128)(2,1)S(1)}, bf16[256,1024]{1,0:T(8,128)(2,1)S(1)}, u32[]{:S(2)}, u32[]{:S(2)}) collective-permute-start(bf16[256,1024]{1,0:T(8,128)(2,1)S(1)} %pad_maximum_fusion.39), channel_id=1, source_target_pairs={{0,4},{4,0},{8,12},{12,8},{16,20},{20,16},{24,28},{28,24},{1,5},{5... | collective-permute-start | bytes 1572872 | tf_op jit(solution)/shard_map/ppermute | solution.py:76
  823.7 25.4 %collective-permute-start.19 = (bf16[512,512]{1,0:T(8,128)(2,1)S(1)}, bf16[512,512]{1,0:T(8,128)(2,1)S(1)}, u32[]{:S(2)}, u32[]{:S(2)}) collective-permute-start(bf16[512,512]{1,0:T(8,128)(2,1)S(1)} %pad_maximum_fusion.38), channel_id=1, source_target_pairs={{0,16},{4,20},{8,24},{12,28},{16,0},{20,4},{24,8},{28,12},{1,17},{... | collective-permute-start | bytes 1572872 | tf_op jit(solution)/shard_map/ppermute | solution.py:76
  841.4 37.6 %collective-permute-start.26 = (bf16[1024,768]{1,0:T(8,128)(2,1)}, bf16[1024,768]{1,0:T(8,128)(2,1)}, u32[]{:S(2)}, u32[]{:S(2)}) collective-permute-start(bf16[1024,768]{1,0:T(8,128)(2,1)} %slice.1713), channel_id=1, source_target_pairs={{0,4},{4,0},{8,12},{12,8},{16,20},{20,16},{24,28},{28,24},{1,5},{5... | collective-permute-start | bytes 4718600 | tf_op jit(solution)/shard_map/ppermute | solution.py:76
  852.0 24.3 %collective-permute-start.23 = (bf16[160,576]{1,0:T(8,128)(2,1)}, bf16[160,576]{1,0:T(8,128)(2,1)}, u32[]{:S(2)}, u32[]{:S(2)}) collective-permute-start(bf16[160,576]{1,0:T(8,128)(2,1)} %pad_maximum_fusion.44), channel_id=1, source_target_pairs={{0,2},{1,3},{2,0},{3,1},{4,6},{5,7},{6,4},{7,5},{8,10},{9,11},{10,... | collective-permute-start | bytes 552968 | tf_op jit(solution)/shard_map/ppermute | solution.py:76
  853.9 29.2 %collective-permute-start.22 = (bf16[512,256]{1,0:T(8,128)(2,1)}, bf16[512,256]{1,0:T(8,128)(2,1)}, u32[]{:S(2)}, u32[]{:S(2)}) collective-permute-start(bf16[512,256]{1,0:T(8,128)(2,1)} %slice.1725), channel_id=1, source_target_pairs={{0,4},{4,0},{8,12},{12,8},{16,20},{20,16},{24,28},{28,24},{1,5},{5... | collective-permute-start | bytes 786440 | tf_op jit(solution)/shard_map/ppermute | solution.py:76
  898.7 30.7 %collective-permute-start.27 = (bf16[320,2048]{1,0:T(8,128)(2,1)S(1)}, bf16[320,2048]{1,0:T(8,128)(2,1)S(1)}, u32[]{:S(2)}, u32[]{:S(2)}) collective-permute-start(bf16[320,2048]{1,0:T(8,128)(2,1)S(1)} %copy-done.67), channel_id=1, source_target_pairs={{0,2},{1,3},{2,0},{3,1},{4,6},{5,7},{6,4},{7,5},{8,10},{9,11},{10,... | collective-permute-start | bytes 3932168 | tf_op jit(solution)/shard_map/ppermute | solution.py:76
  900.4 62.1 %collective-permute-start.39 = (bf16[1056,256]{1,0:T(8,128)(2,1)S(1)}, bf16[1056,256]{1,0:T(8,128)(2,1)S(1)}, u32[]{:S(2)}, u32[]{:S(2)}) collective-permute-start(bf16[1056,256]{1,0:T(8,128)(2,1)S(1)} %copy-done.86), channel_id=1, source_target_pairs={{0,8},{4,12},{8,0},{12,4},{16,24},{20,28},{24,16},{28,20},{1,9},{5... | collective-permute-start | bytes 1622024 | tf_op jit(solution)/shard_map/ppermute | solution.py:76
  908.5 22.8 %collective-permute-start.34 = (f32[1,8,144]{2,0,1:T(1,128)S(1)}, f32[1,8,144]{2,0,1:T(1,128)S(1)}, u32[]{:S(2)}, u32[]{:S(2)}) collective-permute-start(f32[1,8,144]{2,0,1:T(1,128)S(1)} %slice.1401), channel_id=1, source_target_pairs={{0,2},{1,3},{2,0},{3,1},{4,6},{5,7},{6,4},{7,5},{8,10},{9,11},{10,... | collective-permute-start | bytes 13832 | tf_op jit(solution)/shard_map/ppermute | solution.py:76
  929.3 33.1 %collective-permute-start.38 = (bf16[1056,256]{1,0:T(8,128)(2,1)S(1)}, bf16[1056,256]{1,0:T(8,128)(2,1)S(1)}, u32[]{:S(2)}, u32[]{:S(2)}) collective-permute-start(bf16[1056,256]{1,0:T(8,128)(2,1)S(1)} %slice.1722), channel_id=1, source_target_pairs={{0,8},{4,12},{8,0},{12,4},{16,24},{20,28},{24,16},{28,20},{1,9},{5... | collective-permute-start | bytes 1622024 | tf_op jit(solution)/shard_map/ppermute | solution.py:76
  933.0 29.1 %collective-permute-start.33 = (bf16[160,2048]{1,0:T(8,128)(2,1)S(1)}, bf16[160,2048]{1,0:T(8,128)(2,1)S(1)}, u32[]{:S(2)}, u32[]{:S(2)}) collective-permute-start(bf16[160,2048]{1,0:T(8,128)(2,1)S(1)} %pad_maximum_fusion.34), channel_id=1, source_target_pairs={{0,8},{4,12},{8,0},{12,4},{16,24},{20,28},{24,16},{28,20},{1,9},{5... | collective-permute-start | bytes 1966088 | tf_op jit(solution)/shard_map/ppermute | solution.py:76
  935.0 23.1 %collective-permute-start.42 = (bf16[1,64,576]{2,1,0:T(8,128)(2,1)S(1)}, bf16[1,64,576]{2,1,0:T(8,128)(2,1)S(1)}, u32[]{:S(2)}, u32[]{:S(2)}) collective-permute-start(bf16[1,64,576]{2,1,0:T(8,128)(2,1)S(1)} %slice.1728), channel_id=1, source_target_pairs={{0,16},{4,20},{8,24},{12,28},{16,0},{20,4},{24,8},{28,12},{1,17},{... | collective-permute-start | bytes 221192 | tf_op jit(solution)/shard_map/ppermute | solution.py:76
  (188 other events, 1430.0 us)

commit v3 on v1

--- a/solution.py
+++ b/solution.py
@@ -1,6 +1,12 @@
+import functools
+import types
+
 import jax
 import jax.numpy as jnp
+import numpy as np
 from jax import lax
+from jax.experimental import pallas as pl
+from jax.experimental.pallas import tpu as pltpu
 from jax.sharding import PartitionSpec as P
 
 D = 2048
@@ -60,15 +66,15 @@
 
 
 def swap_dp(values, bit):
-    return lax.ppermute(values, "dp", flip_pairs(lax.axis_size("dp"), bit))
+    return lax.ppermute(values, DP, flip_pairs(lax.axis_size(DP), bit))
 
 
 def swap_tensor(values, bit):
-    return lax.ppermute(values, "tensor", flip_pairs(lax.axis_size("tensor"), bit))
+    return lax.ppermute(values, TENSOR, flip_pairs(lax.axis_size(TENSOR), bit))
 
 
 def dp_bits():
-    top = lax.axis_size("dp").bit_length() - 1
+    top = lax.axis_size(DP).bit_length() - 1
     return [1] + list(range(top - 1, 1, -1)) + [0]
 
 
@@ -129,7 +135,7 @@
 
 
 def partner_columns(values):
-    count = lax.axis_size("dp")
+    count = lax.axis_size(DP)
     slots = jnp.split(values, count, axis=-1)
     return jnp.concatenate([slots[k ^ 1] for k in range(count)], axis=-1)
 
@@ -150,7 +156,7 @@
     return lax.dot_general(a, b, (contract, ((), ())), preferred_element_type=jnp.float32)
 
 
-def body(
+def general_body(
     res_in,
     out_grad,
     seg_ids,
@@ -171,10 +177,10 @@
 ):
     f32 = jnp.float32
     bf16 = jnp.bfloat16
-    n_tensor = lax.axis_size("tensor")
-    n_dp = lax.axis_size("dp")
-    dp = lax.axis_index("dp")
-    tensor = lax.axis_index("tensor")
+    n_tensor = lax.axis_size(TENSOR)
+    n_dp = lax.axis_size(DP)
+    dp = lax.axis_index(DP)
+    tensor = lax.axis_index(TENSOR)
     bits = dp_bits()
     merge = bits[0]
     half = (dp >> merge) & 1
@@ -469,44 +475,1590 @@
     )
 
 
+DP, TENSOR = "dp", "tensor"
+MESH = pl.DeviceIdType.MESH
+F32 = jnp.float32
+BF16 = jnp.bfloat16
+CHUNKS = 3
+SECONDS = 9
+THIRDS = 7
+SLOT = 256
+GIVEN_VMEM = 60 * 1024 * 1024
+FAR_FIRST = (2, 1, 0)
+FLIPS = (1, 2, 0)
+TENSOR_BITS = (1, 0)
+
+
+COLUMNS = slot_order(FAR_FIRST)
+UNIT_SLOTS = slot_order(FLIPS)
+ROWS = slot_order(TENSOR_BITS)
+
+
+def nn(a, b):
+    return lax.dot_general(a, b, (((1,), (0,)), ((), ())), preferred_element_type=F32)
+
+
+def nt(a, b):
+    return lax.dot_general(a, b, (((1,), (1,)), ((), ())), preferred_element_type=F32)
+
+
+def tn(a, b):
+    return lax.dot_general(a, b, (((0,), (0,)), ((), ())), preferred_element_type=F32)
+
+
+def lanes(k, width=SLOT):
+    return slice(k * width, (k + 1) * width)
+
+
+def crossed(index, constant, bits):
+    total = 0
+    for bit in range(bits):
+        own = lax.rem(index // (1 << bit), 2)
+        total = total + ((1 - own) if (constant >> bit) & 1 else own) * (1 << bit)
+    return total
+
+
+class Copies:
+    def __init__(self, send_sems, recv_sems, local_sems=None):
+        self.send_sems, self.recv_sems, self.local_sems = send_sems, recv_sems, local_sems
+        self.count = 0
+        self.local_count = 0
+
+    def across(self, axis, bit):
+        index = lax.axis_index(axis)
+        side = lax.rem(index // (1 << bit), 2)
+        return {axis: index + (1 - 2 * side) * (1 << bit)}
+
+    def start(self, source, target, axis, bit):
+        copy = pltpu.make_async_remote_copy(
+            src_ref=source,
+            dst_ref=target,
+            send_sem=self.send_sems.at[self.count],
+            recv_sem=self.recv_sems.at[self.count],
+            device_id=self.across(axis, bit),
+            device_id_type=MESH,
+        )
+        self.count += 1
+        copy.start()
+        return copy
+
+    def local(self, source, target):
+        copy = pltpu.make_async_copy(source, target, self.local_sems.at[self.local_count])
+        self.local_count += 1
+        copy.start()
+        return copy
+
+    def greet(self, dp_bits, tensor_bits=TENSOR_BITS):
+        barrier = pltpu.get_barrier_semaphore()
+        for axis, bits in ((DP, dp_bits), (TENSOR, tensor_bits)):
+            for bit in bits:
+                pl.semaphore_signal(
+                    barrier, inc=1, device_id=self.across(axis, bit), device_id_type=MESH
+                )
+        pl.semaphore_wait(barrier, len(dp_bits) + len(tensor_bits))
+
+    def swapped(self, source, target, first, width):
+        parts = []
+        for a in range(first, first + width, 1024):
+            for b, c in ((a, a + 512), (a + 512, a)):
+                parts.append(
+                    self.start(
+                        source.at[(slice(None),) * (len(source.shape) - 1) + (pl.ds(b, 512),)],
+                        target.at[(slice(None),) * (len(target.shape) - 1) + (pl.ds(c, 512),)],
+                        DP,
+                        1,
+                    )
+                )
+        return Several(parts)
+
+
+class Several:
+    def __init__(self, parts):
+        self.parts = parts
+
+    def wait(self):
+        for part in self.parts:
+            part.wait()
+
+
+class SlotGather:
+    def __init__(self, copies, source, slots, bits, axis=DP, cut=None):
+        self.copies, self.source, self.slots, self.bits, self.axis = copies, source, slots, list(bits), axis
+        self.cut = (slice(None),) if cut is None else (pl.ds(*cut),)
+        self.done, self.have, self.own, self.flying = 0, 1, None, None
+
+    def view(self, first, count):
+        return self.slots.at[(pl.ds(first, count), *self.cut)]
+
+    def start(self):
+        bit = self.bits[self.done]
+        if self.done == 0 and self.source is not None:
+            source = self.source.at[(pl.ds(0, 1), *self.cut)]
+            self.own = self.copies.local(source, self.view(0, 1))
+        else:
+            if self.own is not None:
+                self.own.wait()
+                self.own = None
+            source = self.view(0, self.have)
+        self.flying = self.copies.start(source, self.view(self.have, self.have), self.axis, bit)
+        self.done += 1
+        self.have *= 2
+
+    def wait(self):
+        self.flying.wait()
+        self.flying = None
+        if self.done < len(self.bits):
+            self.start()
+
+    def finish(self):
+        while self.flying is not None:
+            self.wait()
+
+
+ANY_SPEC = pl.BlockSpec(memory_space=pl.ANY)
+VMEM_SPEC = pl.BlockSpec(memory_space=pltpu.VMEM)
+SMEM_SPEC = pl.BlockSpec(memory_space=pltpu.SMEM)
+
+
+def cost(micros):
+    return pl.CostEstimate(flops=micros * 10**9, bytes_accessed=micros * 10**6, transcendentals=0)
+
+
+def like(shape, dtype=BF16):
+    return jax.ShapeDtypeStruct(shape, dtype)
+
+
+def turn(a, b, cos, sin):
+    return a * cos - b * sin, b * cos + a * sin
+
+
+def head_lanes(rows, head):
+    lane = lax.broadcasted_iota(jnp.int32, (rows, SLOT), 1)
+    return lax.rem(lane // 32, 4) == head
+
+
+def spread_block(copies, pair_ref, between):
+    block = lambda k: pair_ref.at[pl.ds(k, 1)]
+    x_own = copies.start(block(0), block(2), TENSOR, 1)
+    z_own = copies.swapped(block(0), block(1), 0, D)
+    waits = [copies.start(block(0), block(4), TENSOR, 0)]
+    between()
+    z_own.wait()
+    over_both = copies.start(block(1), block(3), TENSOR, 1)
+    waits.append(copies.start(block(1), block(5), TENSOR, 0))
+    between()
+    x_own.wait()
+    waits.append(copies.start(block(2), block(6), TENSOR, 0))
+    between()
+    over_both.wait()
+    waits.append(copies.start(block(3), block(7), TENSOR, 0))
+    for copy in waits:
+        copy.wait()
+
+
+class Places:
+    def __init__(self):
+        self.dp, self.tensor = lax.axis_index(DP), lax.axis_index(TENSOR)
+
+    def __getitem__(self, k):
+        if k == 12:
+            return lax.rem(self.dp // 2, 2)
+        return crossed(self.dp, COLUMNS[k], 3) if k < 8 else crossed(self.tensor, ROWS[k - 8], 2)
+
+
+class Kept:
+    output = ((8, 512, SLOT), BF16)
+    mix = ((TOK, 512), BF16)
+    query_final = ((TOK, 768), BF16)
+    keyval_final = ((TOK, 1024), BF16)
+    key_rope = ((TOK, SLOT), BF16)
+    lse = ((TOK, 128), F32)
+    query = ((8, SLOT, 768), BF16)
+    w_keyval = ((KR, 1024), BF16)
+    normed = ((TOK, D), BF16)
+    latent_norm = ((TOK, KR), BF16)
+    col = ((TOK, 128), F32)
+    row = ((8, TOK), F32)
+    cos = ((TOK, 128), F32)
+    sin = ((TOK, 128), F32)
+    gains = ((8, D), F32)
+    latent_gain = ((8, KR), F32)
+    latent_c = ((160, KR), F32)
+    w_latent = ((D, KR + 128), BF16)
+    mid = ((160, D), F32)
+    mid_pair = ((8, 160, D), BF16)
+    res = ((160, D), BF16)
+    grad = ((160, D), BF16)
+    valid = ((160, 128), F32)
+    gates = ((8, TOK), F32)
+
+
+class Landing:
+    tokens = ((4, 160, D), BF16)
+    pack = ((4, 8, 64, KR + 128), BF16)
+    keyval = ((8, 64, 1024), BF16)
+    part = ((4, 160, D), BF16)
+    got_c = ((2, 160, D), BF16)
+    give_x = ((1, 160, D), BF16)
+    got_x = ((1, 160, D), BF16)
+    gain_rows = ((KR, 128), BF16)
+    masked = ((1, 160, D), BF16)
+    own_query = ((1, SLOT, 768), BF16)
+
+
+def fields(kind):
+    return [name for name in vars(kind) if not name.startswith("_")]
+
+
+def buffers(kind):
+    return [getattr(kind, name) for name in fields(kind)]
+
+
+def masks(col, row, cut):
+    return (col[cut, 0:1] == row[0:1]) & (row[1:2] <= col[cut, 1:2])
+
+
+def sort_columns(rows):
+    column = lax.broadcasted_iota(jnp.int32, (768, 768), 1)
+    row = lax.broadcasted_iota(jnp.int32, (768, 768), 0)
+    wide = (column // 128) * 192 + lax.rem(column, 128)
+    late = column - 512
+    narrow = (lax.rem(late, 128) // 32) * 192 + 128 + (late // 128) * 32 + lax.rem(late, 32)
+    return jnp.where(row == jnp.where(column < 512, wide, narrow), 1.0, 0.0).astype(BF16)
+
+
+def front_kernel(
+    width,
+    count_ref,
+    pack_ref,
+    keyval_ref,
+    output_ref,
+    expert_in,
+    expert_out,
+    shared_in,
+    shared_out,
+    res_ref,
+    grad_ref,
+    query_ref,
+    segment_row,
+    table_ref,
+    slot_gates,
+    frequency_ref,
+    grad_pair,
+    gates_over,
+    *rest,
+):
+    n_units = 3
+    lows, highs = rest[:n_units], rest[n_units : 2 * n_units]
+    rest = rest[2 * n_units :]
+    kept, names = fields(Kept), fields(Kept) + fields(Landing)
+    outs = types.SimpleNamespace(**dict(zip(kept, rest)))
+    rest = rest[len(kept) :]
+    at = types.SimpleNamespace(**dict(zip(names, rest)))
+    send_sems, recv_sems, local_sems = rest[len(names) :]
+    copies = Copies(send_sems, recv_sems, local_sems)
+    places = Places()
+    copies.greet((0, 1, 2))
+    saved = []
+
+    def save(pick):
+        for source, target in zip(pick(at), pick(outs)):
+            saved.append(copies.local(source, target))
+
+    pack = SlotGather(copies, pack_ref, at.pack.at[0], FAR_FIRST)
+    keyval = SlotGather(copies, keyval_ref, at.keyval, FAR_FIRST)
+    part = query_ref.shape[0] // 4
+    queries = [
+        SlotGather(copies, at.own_query, at.query, FAR_FIRST, cut=(k * part, part)) for k in range(4)
+    ]
+    part = output_ref.shape[1] // 2
+    outputs = [SlotGather(copies, output_ref, at.output, FAR_FIRST, cut=(k * part, part)) for k in range(2)]
+    pack.start()
+    keyval.start()
+    for k in range(8):
+        block = pl.ds(pl.multiple_of(places[k] * SLOT, SLOT), SLOT)
+        at.res[:, lanes(k)] = res_ref[:, block]
+        at.grad[:, lanes(k)] = grad_ref[:, block]
+    at.tokens[0] = at.res[...]
+    tokens = SlotGather(copies, None, at.tokens, TENSOR_BITS, TENSOR)
+    tokens.start()
+    at.own_query[0] = nn(query_ref[...], sort_columns(768)).astype(BF16)
+    items = [pack, keyval, *queries, *outputs]
+    units = [(p, part) for p in range(n_units) for part in range(CHUNKS)]
+    flights = [None] * len(units)
+    owns = [None] * len(units)
+    state = [0, 0, 0]
+
+    def unit_source(side, p, part):
+        if p < 2:
+            expert = pl.ds(side * 2 + p, 1)
+            return expert_out.at[expert] if part == 2 else expert_in.at[expert, part]
+        cut = pl.ds(pl.multiple_of(side * width, 16), width)
+        return shared_out.at[pl.ds(0, 1), cut] if part == 2 else shared_in.at[pl.ds(part, 1), cut]
+
+    def unit_first():
+        i = state[0]
+        if i >= len(units):
+            return
+        p, part = units[i]
+        cut = pl.ds(part * width, width)
+        side = places[12]
+        owns[i] = copies.local(unit_source(side, p, part), lows[p].at[pl.ds(0, 1), cut])
+        flights[i] = copies.start(
+            unit_source(1 - side, p, part), lows[p].at[pl.ds(1, 1), cut], DP, FLIPS[0]
+        )
+        state[0] = i + 1
+
+    def unit_second():
+        i = state[1]
+        if i >= min(state[0], SECONDS):
+            return
+        p, part = units[i]
+        cut = pl.ds(part * width, width)
+        flights[i].wait()
+        owns[i].wait()
+        flights[i] = copies.start(
+            lows[p].at[pl.ds(0, 2), cut], lows[p].at[pl.ds(2, 2), cut], DP, FLIPS[1]
+        )
+        state[1] = i + 1
+
+    def unit_third():
+        i = state[2]
+        if i >= min(state[1], THIRDS):
+            return
+        p, part = units[i]
+        cut = pl.ds(part * width, width)
+        flights[i].wait()
+        flights[i] = copies.start(lows[p].at[pl.ds(0, 4), cut], highs[p].at[pl.ds(0, 4), cut], DP, FLIPS[2])
+        state[2] = i + 1
+
+    def pump():
+        unit_third()
+        unit_second()
+        unit_first()
+
+    def place_tokens():
+        segments = segment_row[...].astype(F32)
+        at.col[:, 0:8] = jnp.broadcast_to(segments, (8, TOK)).T
+        for b in range(4):
+            start = pl.multiple_of(places[8 + b] * 160, 8)
+            at.cos[b * 160 : (b + 1) * 160] = jnp.broadcast_to(at.col[pl.ds(start, 160), 0:1], (160, 128))
+        for b in range(4):
+            start = pl.multiple_of(places[8 + b] * 160, 8)
+            cut = slice(b * 160, (b + 1) * 160)
+            segment = at.cos[cut, 0:1]
+            token = start + lax.broadcasted_iota(jnp.int32, (160, 128), 0)
+            lane = lax.broadcasted_iota(jnp.int32, (160, 128), 1)
+            at.col[cut] = jnp.where(lane == 0, segment, token.astype(F32))
+            before = jnp.sum((segments < segment).astype(F32), axis=1, keepdims=True)
+            angle = (token.astype(F32) - before) * frequency_ref[...]
+            at.cos[cut] = jnp.cos(angle)
+            at.sin[cut] = jnp.sin(angle)
+        at.row[...] = at.col[...].T[0:8]
+        at.valid[...] = (at.col[0:160, 1:2] < count_ref[0].astype(F32)).astype(F32) + jnp.zeros((160, 128), F32)
+        at.masked[0] = (at.grad[...].astype(F32) * at.valid[:, 0:1]).astype(BF16)
+
+    def route_tokens():
+        slots = jnp.concatenate([table_ref[...].astype(F32), slot_gates[...]], axis=0).T
+        token_row = at.row[1:2]
+        for e in range(4):
+            hit = jnp.where(slots[:, e : e + 1] == token_row, slots[:, 4 + e : 5 + e], 0.0)
+            at.gates[e : e + 1] = jnp.sum(hit, axis=0, keepdims=True)
+        at.gates[4:8] = jnp.zeros((4, TOK), F32)
+        save(lambda v: (v.col, v.row, v.cos, v.sin, v.valid, v.res, v.grad, v.gates))
+
+    def make_keys():
+        for s in range(4):
+            for k in range(8):
+                start = pl.multiple_of(k * SLOT + places[8 + s] * 64, 64)
+                at.w_latent[pl.ds(start, 64)] = at.pack[s, k]
+                start = pl.multiple_of(places[k] * 64 + places[8 + s] * 16, 16)
+                at.gain_rows[pl.ds(start, 16)] = at.pack[s, k, 0:16, KR : KR + 128]
+        for k in range(8):
+            at.w_keyval[pl.ds(pl.multiple_of(places[k] * 64, 64), 64)] = at.keyval[k]
+        tail = at.w_latent[:, KR : KR + 128]
+        turned = tail.astype(F32).T
+        attn_gain = turned[64:65]
+        at.gains[...] = turned[64:72]
+        latent_gain = at.gain_rows[...].astype(F32).T[66:67]
+        at.latent_gain[...] = jnp.broadcast_to(latent_gain, (8, KR))
+        row = lax.broadcasted_iota(jnp.int32, (128, SLOT), 0)
+        lane = lax.broadcasted_iota(jnp.int32, (128, SLOT), 1)
+        spread = jnp.where(row == lax.rem(lane, 32) + 32 * (lane // 128), 1.0, 0.0).astype(BF16)
+        w_rope = nn(tail, spread).astype(BF16)
+        for b in range(4):
+            cut = slice(b * 160, (b + 1) * 160)
+            x = at.tokens[b].astype(F32)
+            factor = lax.rsqrt(jnp.mean(x * x, axis=1, keepdims=True) + NORM_EPS)
+            at.normed[cut] = (x * factor * attn_gain).astype(BF16)
+        for b in range(2):
+            cut = slice(b * 320, (b + 1) * 320)
+            normed = at.normed[cut]
+            latent_c = nn(normed, at.w_latent[:, :KR])
+            factor = lax.rsqrt(jnp.mean(latent_c * latent_c, axis=1, keepdims=True) + NORM_EPS)
+            latent_norm = (latent_c * factor * latent_gain).astype(BF16)
+            if b == 0:
+                at.latent_c[...] = latent_c[:160]
+            at.latent_norm[cut] = latent_norm
+            rope = nn(normed, w_rope)
+            key_a, key_b = turn(rope[:, :128], rope[:, 128:], at.cos[cut], at.sin[cut])
+            at.key_rope[cut] = jnp.concatenate([key_a, key_b], axis=1).astype(BF16)
+            at.keyval_final[cut] = nn(latent_norm, at.w_keyval[...]).astype(BF16)
+        save(lambda v: (v.w_latent, v.w_keyval, v.gains, v.latent_gain, v.normed, v.latent_c, v.latent_norm, v.key_rope, v.keyval_final,))
+
+
+    unit_first()
+    for tau in range(len(items) + 1):
+        if tau >= 1:
+            items[tau - 1].wait()
+        if tau < len(items):
+            items[tau].wait()
+        if tau + 2 < len(items):
+            items[tau + 2].start()
+        if tau == 0:
+            place_tokens()
+        elif tau == 1:
+            tokens.wait()
+            grad_own = copies.local(at.masked, grad_pair.at[pl.ds(0, 1)])
+            grad_x = copies.start(at.masked, grad_pair.at[pl.ds(2, 1)], TENSOR, 1)
+        elif tau == 2:
+            unit_first()
+        elif tau == 3:
+            pack.wait()
+            pack_tensor = SlotGather(copies, None, at.pack, TENSOR_BITS, TENSOR)
+            pack_tensor.start()
+            unit_second()
+        elif tau == 4:
+            unit_first()
+            route_tokens()
+            gates_flight = copies.start(at.gates, gates_over, DP, 1)
+        elif tau == 5:
+            tokens.wait()
+            unit_second()
+        elif tau == 6:
+            pack_tensor.wait()
+            unit_first()
+        elif tau == 7:
+            keyval.wait()
+            pack_tensor.wait()
+            make_keys()
+            unit_second()
+    grad_x.wait()
+    grad_z = copies.swapped(at.masked, grad_pair.at[pl.ds(1, 1)], 0, D)
+    pump()
+    for query in queries:
+        query.wait()
+
+    save(lambda v: (v.query,))
+    gates_flight.wait()
+    w_query = at.query[...].reshape(D, 768)
+    scale = (HD + RD) ** (-0.5)
+    for b in range(2):
+        cut = slice(b * 320, (b + 1) * 320)
+        found = nn(at.normed[cut], w_query)
+        turned_a, turned_b = turn(found[:, 512:640], found[:, 640:768], at.cos[cut], at.sin[cut])
+        at.query_final[cut] = jnp.concatenate([found[:, :512], turned_a, turned_b], axis=1).astype(BF16)
+        allowed = masks(at.col, at.row, cut)
+        lse_lane = lax.broadcasted_iota(jnp.int32, (320, 128), 1)
+        lse_all = jnp.zeros((320, 128), F32)
+        for h in range(4):
+            rope = at.query_final[cut, 512:768]
+            rope = jnp.where(head_lanes(320, h), rope, jnp.zeros_like(rope))
+            keys = at.keyval_final[:, h * 256 : h * 256 + 128]
+            scores = nt(at.query_final[cut, lanes(h, 128)], keys) + nt(rope, at.key_rope[...])
+            scores = jnp.where(allowed, scores * scale, -1e30)
+            top = jnp.max(scores, axis=1, keepdims=True)
+            weight = jnp.exp(scores - top)
+            total = jnp.sum(weight, axis=1, keepdims=True)
+            probs = (weight / total).astype(BF16)
+            lse_all = jnp.where(lse_lane == h, top + jnp.log(total), lse_all)
+            mix = nn(probs, at.keyval_final[:, h * 256 + 128 : h * 256 + 256])
+            at.mix[cut, lanes(h, 128)] = mix.astype(BF16)
+        at.lse[cut] = lse_all
+        if b == 0:
+            pump()
+            grad_z.wait()
+            grad_zx = copies.start(
+                grad_pair.at[pl.ds(1, 1)], grad_pair.at[pl.ds(3, 1)], TENSOR, 1
+            )
+    for output in outputs:
+        output.wait()
+    save(lambda v: (v.query_final, v.mix, v.lse, v.output,))
+    for b in range(2):
+        cut = slice((1 - b) * 320, (2 - b) * 320)
+        for k in range(8):
+            w_output = at.output[k]
+            part = nn(at.mix[cut], w_output).astype(BF16)
+            at.part[2 - 2 * b, :, lanes(k)] = part[:160]
+            at.part[3 - 2 * b, :, lanes(k)] = part[160:]
+        if b == 0:
+            block = lambda ref, k: ref.at[pl.ds(k, 1)]
+            c_far = copies.start(block(at.part, 3), block(at.got_c, 1), TENSOR, 0)
+            c_near = copies.start(block(at.part, 2), block(at.got_c, 0), TENSOR, 0)
+    c_far.wait()
+    at.give_x[0] = (at.part[1].astype(F32) + at.got_c[1].astype(F32)).astype(BF16)
+    x_far = copies.start(at.give_x, at.got_x, TENSOR, 1)
+    grad_zx.wait()
+    grad_own.wait()
+    grad_c = copies.start(grad_pair.at[pl.ds(0, 4)], grad_pair.at[pl.ds(4, 4)], TENSOR, 0)
+    pump()
+    c_near.wait()
+    x_far.wait()
+    attn_out = at.part[0].astype(F32) + at.got_c[0].astype(F32) + at.got_x[0].astype(F32)
+    mid = at.res[...].astype(F32) + at.valid[:, 0:1] * attn_out
+    at.mid[...] = mid
+    save(lambda v: (v.mid,))
+    factor = lax.rsqrt(jnp.mean(mid * mid, axis=1, keepdims=True) + NORM_EPS)
+    at.mid_pair[0] = (mid * factor * at.gains[1:2]).astype(BF16)
+    spread_block(copies, at.mid_pair, pump)
+    save(lambda v: (v.mid_pair,))
+    grad_c.wait()
+    while state[0] < len(units) or state[1] < SECONDS or state[2] < THIRDS:
+        pump()
+    for i in range(SECONDS, len(units)):
+        owns[i].wait()
+    for flight in flights:
+        if flight is not None:
+            flight.wait()
+    for copy in saved:
+        copy.wait()
+
+
+def front(counts, pack, keyval, output, expert_in, expert_out, shared_in, shared_out, res, grad, query, segment, table, gates):
+    n_units, width = 3, expert_out.shape[1]
+    half = (4, 3 * width, SLOT)
+    frequency = ROPE_BASE ** (-np.arange(RD // 2, dtype=np.float32) / np.float32(RD // 2))
+    frequency = jnp.asarray(np.tile(frequency.astype(np.float32), 4)[None])
+    operands = [
+        counts,
+        pack[None],
+        keyval[None],
+        output[None],
+        expert_in.transpose(0, 1, 3, 2),
+        expert_out,
+        shared_in.transpose(0, 2, 1),
+        shared_out[None],
+        res,
+        grad,
+        query,
+        segment,
+        table,
+        gates,
+        frequency,
+    ]
+    shapes = [like((8, *res.shape)), like((8, TOK), F32)] + [like(half)] * (2 * n_units - 1) + [like((4, width, SLOT))]
+    shapes += [like(*buffer) for buffer in buffers(Kept)]
+    results = pl.pallas_call(
+        functools.partial(front_kernel, width),
+        out_shape=shapes,
+        in_specs=[SMEM_SPEC] + [ANY_SPEC] * 7 + [VMEM_SPEC] * 7,
+        out_specs=[ANY_SPEC] * len(shapes),
+        scratch_shapes=[pltpu.VMEM(*buffer) for buffer in buffers(Kept) + buffers(Landing)]
+        + [
+            pltpu.SemaphoreType.DMA((80,)),
+            pltpu.SemaphoreType.DMA((80,)),
+            pltpu.SemaphoreType.DMA((48,)),
+        ],
+        compiler_params=pltpu.CompilerParams(
+            collective_id=0, has_side_effects=True, vmem_limit_bytes=GIVEN_VMEM
+        ),
+        cost_estimate=cost(220),
+        name="front",
+    )(*operands)
+    grad_pair, gates_over, results = results[0], results[1], results[2:]
+    lows, results = results[:n_units], results[n_units:]
+    highs, results = results[:n_units], results[n_units:]
+    return grad_pair, gates_over, lows, highs, types.SimpleNamespace(**dict(zip(fields(Kept), results)))
+
+
+TOKEN_BLOCK = 256
+
+
+class Freight:
+    def __init__(self, copies, bits, sources, targets):
+        self.copies, self.bits, self.pairs = copies, bits, list(zip(sources, targets))
+        self.flights = []
+
+    def start(self):
+        for bit, (source, target) in zip(self.bits, self.pairs):
+            self.flights.append(self.copies.start(source, target, DP, bit))
+
+    def wait(self):
+        for flight in self.flights:
+            flight.wait()
+
+
+def experts_kernel(width, has_sum, bits, parts, *refs):
+    refs = list(refs)
+    take = lambda n: [refs.pop(0) for _ in range(n)]
+    mid_ref, grad_ref, gate_ref = take(3)
+    unit_refs = take(len(parts))
+    if has_sum:
+        back_in, out_in = take(2)
+    sources = take(len(bits))
+    back_ref, out_ref = take(2)
+    keep_refs, give_refs = take(3), take(3)
+    targets = take(len(bits))
+    whole, total, send_sems, recv_sems = take(4)
+    step = pl.program_id(0)
+    copies = Copies(send_sems, recv_sems)
+
+    def flights():
+        return [
+            pltpu.make_async_remote_copy(
+                src_ref=cut.view(source),
+                dst_ref=target,
+                send_sem=send_sems.at[k],
+                recv_sem=recv_sems.at[k],
+                device_id=copies.across(DP, cut.bit),
+                device_id_type=MESH,
+            )
+            for k, (cut, source, target) in enumerate(zip(bits, sources, targets))
+        ]
+
+    @pl.when(step == 0)
+    def _():
+        copies.greet(sorted({cut.bit for cut in bits}), ())
+        for flight in flights():
+            flight.start()
+        for ref, (slot, count, start, size, skip) in zip(unit_refs, parts):
+            for j in range(count):
+                k = COLUMNS.index(UNIT_SLOTS[slot + j])
+                whole[start : start + size, lanes(k)] = ref[j, skip : skip + size]
+        total[...] = jnp.zeros_like(total)
+
+    mid, grad = mid_ref[...], grad_ref[...]
+    gate_up = nt(whole[: 2 * width], mid)
+    hidden_grad = nt(whole[2 * width :], grad)
+    gate = gate_up[:width]
+    up = gate_up[width:]
+    sigma = 1.0 / (1.0 + jnp.exp(-gate))
+    silu = gate * sigma
+    slope = sigma * (1.0 + gate * (1.0 - sigma))
+    weight = gate_ref[...]
+    hidden_grad = hidden_grad * weight
+    hidden = (silu * up * weight).astype(BF16)
+    pre = jnp.concatenate(
+        [(hidden_grad * up * slope).astype(BF16), (hidden_grad * silu).astype(BF16)], axis=0
+    )
+    back = tn(pre, whole[: 2 * width])
+    out = tn(hidden, whole[2 * width :])
+    if has_sum:
+        back = back + back_in[...]
+        out = out + out_in[...]
+    back_ref[...] = back.astype(back_ref.dtype)
+    out_ref[...] = out.astype(out_ref.dtype)
+    total[: 2 * width] += nn(pre, mid)
+    total[2 * width :] += nn(hidden, grad)
+
+    @pl.when(step == pl.num_programs(0) - 1)
+    def _():
+        for g in range(3):
+            cut = slice(g * width, (g + 1) * width)
+            for k in range(4):
+                keep_refs[g][k] = total[cut, lanes((0, 2, 1, 3)[k])].astype(BF16)
+                give_refs[g][k] = total[cut, lanes(4 + (0, 2, 1, 3)[k])].astype(BF16)
+        for flight in flights():
+            flight.wait()
+
+
+class Cut:
+    def __init__(self, array, bit, slots=None, rows=None):
+        self.array, self.bit = array, bit
+        self.slots = slots or (0, array.shape[0])
+        self.rows = rows or (0, array.shape[1])
+
+    def shape(self):
+        return (self.slots[1], self.rows[1], self.array.shape[2])
+
+    def view(self, ref):
+        return ref.at[pl.ds(*self.slots), pl.ds(*self.rows)]
+
+
+def experts_step(mid_pair, grad_pair, unit, gate, sums, last, freight, ident):
+    tokens, block = mid_pair.shape[0], TOKEN_BLOCK
+    width = unit[0][0].shape[1] // 3
+    rows = pl.BlockSpec((block, D), lambda i: (i, 0))
+    fixed = lambda *shape: pl.BlockSpec(shape, lambda i: (0,) * len(shape))
+    kind = BF16 if last else F32
+    part = (4, width, SLOT)
+    operands = [mid_pair, grad_pair, gate[None]] + [part[0] for part in unit]
+    specs = [rows, rows, pl.BlockSpec((1, block), lambda i: (0, i))]
+    specs += [fixed(*part[0].shape) for part in unit]
+    if sums is not None:
+        operands += list(sums)
+        specs += [rows, rows]
+    results = pl.pallas_call(
+        functools.partial(
+            experts_kernel, width, sums is not None, tuple(freight), tuple(p[1:] for p in unit)
+        ),
+        grid=(tokens // block,),
+        out_shape=[like((tokens, D), kind)] * 2
+        + [like(part)] * 6
+        + [like(cut.shape()) for cut in freight],
+        in_specs=specs + [ANY_SPEC] * len(freight),
+        out_specs=[rows, rows] + [fixed(*part)] * 6 + [ANY_SPEC] * len(freight),
+        scratch_shapes=[
+            pltpu.VMEM((3 * width, D), BF16),
+            pltpu.VMEM((3 * width, D), F32),
+            pltpu.SemaphoreType.DMA((len(freight),)),
+            pltpu.SemaphoreType.DMA((len(freight),)),
+        ],
+        compiler_params=pltpu.CompilerParams(
+            collective_id=ident, has_side_effects=True, vmem_limit_bytes=GIVEN_VMEM
+        ),
+        cost_estimate=cost(35),
+        name="experts_step",
+    )(*operands, *[cut.array for cut in freight])
+    return list(results[:2]), list(results[2:5]), list(results[5:8]), list(results[8:])
+
+
+def halve_kernel(count, *refs):
+    keeps, gots, stays, gives = (refs[k * count : (k + 1) * count] for k in range(4))
+    for keep, got, stay, give in zip(keeps, gots, stays, gives):
+        half = stay.shape[0]
+        for k in range(half):
+            stay[k] = (keep[k].astype(F32) + got[k].astype(F32)).astype(BF16)
+            give[k] = (keep[half + k].astype(F32) + got[half + k].astype(F32)).astype(BF16)
+
+
+def halve(pairs):
+    count = len(pairs)
+    shapes = [like((keep.shape[0] // 2, *keep.shape[1:])) for keep, _ in pairs]
+    results = pl.pallas_call(
+        functools.partial(halve_kernel, count),
+        out_shape=shapes * 2,
+        in_specs=[VMEM_SPEC] * (2 * count),
+        out_specs=[VMEM_SPEC] * (2 * count),
+        cost_estimate=cost(3),
+        name="halve",
+    )(*[keep for keep, _ in pairs], *[got for _, got in pairs])
+    return list(zip(results[:count], results[count:]))
+
+
+class PairSum:
+    def __init__(self, copies, blocks, got_c, give_a, give_b, got_a, got_b, end_a, end_b, last_a, last_b):
+        self.copies, self.blocks, self.got_c = copies, blocks, got_c
+        self.give_a, self.give_b, self.got_a, self.got_b = give_a, give_b, got_a, got_b
+        self.end_a, self.end_b, self.last_a, self.last_b = end_a, end_b, last_a, last_b
+
+    def both(self, k, first):
+        cut = slice(first, first + 1024)
+        return self.blocks[k, :, cut].astype(F32) + self.got_c[k, :, cut].astype(F32)
+
+    def start(self):
+        self.flights = {}
+        for k in (3, 2, 1, 0):
+            self.flights[k] = self.copies.start(
+                self.blocks.at[pl.ds(4 + k, 1)], self.got_c.at[pl.ds(k, 1)], TENSOR, 0
+            )
+
+    def cross(self):
+        self.flights[3].wait()
+        self.give_a[1] = self.both(3, 0).astype(BF16)
+        self.give_b[1] = self.both(3, 1024).astype(BF16)
+        self.flights[2].wait()
+        self.give_a[0] = self.both(2, 0).astype(BF16)
+        self.across_a = self.copies.start(self.give_a, self.got_a, TENSOR, 1)
+        self.flights[1].wait()
+        self.give_b[0] = self.both(1, 1024).astype(BF16)
+        self.across_b = self.copies.swapped(self.give_b, self.got_b, 0, 1024)
+        self.flights[0].wait()
+
+    def end(self):
+        self.across_a.wait()
+        self.end_a[0] = (self.both(1, 0) + self.got_a[1].astype(F32)).astype(BF16)
+        self.ends_a = self.copies.swapped(self.end_a, self.last_a, 0, 1024)
+        self.across_b.wait()
+        self.end_b[0] = (self.both(2, 1024) + self.got_b[1].astype(F32)).astype(BF16)
+        self.ends_b = self.copies.start(self.end_b, self.last_b, TENSOR, 1)
+
+    def settle(self, total, end_a, end_b):
+        self.across_a.wait()
+        end_a[0] = (self.both(1, 0) + self.got_a[1].astype(F32)).astype(BF16)
+        self.across_b.wait()
+        end_b[0] = (self.both(2, 1024) + self.got_b[1].astype(F32)).astype(BF16)
+        total[:, :1024] = self.both(0, 0) + self.got_a[0].astype(F32)
+        total[:, 1024:] = self.both(0, 1024) + self.got_b[0].astype(F32)
+
+    def total(self):
+        self.ends_a.wait()
+        self.ends_b.wait()
+        return (
+            self.both(0, 0) + self.got_a[0].astype(F32) + self.last_a[0].astype(F32),
+            self.both(0, 1024) + self.got_b[0].astype(F32) + self.last_b[0].astype(F32),
+        )
+
+
+def sum_scratch():
+    half = pltpu.VMEM((2, 160, 1024), BF16)
+    end = pltpu.VMEM((1, 160, 1024), BF16)
+    return [pltpu.VMEM((4, 160, D), BF16), half, half, half, half, end, end, end, end]
+
+
+def back_kernel(bits, *refs):
+    refs = list(refs)
+    take = lambda n: [refs.pop(0) for _ in range(n)]
+    back_ref, grad_ref, mid_ref, gains_ref, valid_ref = take(5)
+    sources = take(len(bits))
+    mid_grad_ref, gain_part_ref, tokens_ref = take(3)
+    targets = take(len(bits))
+    *buffers, send_sems, recv_sems = refs
+    copies = Copies(send_sems, recv_sems)
+    copies.greet((0, 1, 2))
+    freight = Freight(copies, bits, sources, targets)
+    freight.start()
+    pair = PairSum(copies, back_ref, *buffers)
+    pair.start()
+    pair.cross()
+    pair.end()
+    first, second = pair.total()
+    mid_grad_ref[:, :1024] = first
+    mid_grad_ref[:, 1024:] = second
+    grad, mid = mid_grad_ref[...], mid_ref[...]
+    factor = lax.rsqrt(jnp.mean(mid * mid, axis=1, keepdims=True) + NORM_EPS)
+    scaled = grad * gains_ref[1:2]
+    inner = jnp.mean(scaled * mid, axis=1, keepdims=True)
+    gain_part_ref[...] = jnp.broadcast_to(jnp.sum(grad * mid * factor, axis=0, keepdims=True), (8, D))
+    mid_grad = grad_ref[...].astype(F32) + factor * (scaled - mid * factor * factor * inner)
+    mid_grad_ref[...] = mid_grad
+    tokens_ref[0] = (valid_ref[:, 0:1] * mid_grad).astype(BF16)
+    own = tokens_ref.at[pl.ds(0, 1)]
+    x_own = copies.start(own, tokens_ref.at[pl.ds(1, 1)], TENSOR, 1)
+    c_own = copies.start(own, tokens_ref.at[pl.ds(2, 1)], TENSOR, 0)
+    x_own.wait()
+    c_far = copies.start(tokens_ref.at[pl.ds(1, 1)], tokens_ref.at[pl.ds(3, 1)], TENSOR, 0)
+    c_own.wait()
+    c_far.wait()
+    freight.wait()
+
+
+def back_tokens(back, grad_slots, mid, gains, valid, freight):
+    rows = (160, D)
+    bits = tuple(bit for bit, _ in freight)
+    goods = [array for _, array in freight]
+    results = pl.pallas_call(
+        functools.partial(back_kernel, bits),
+        out_shape=[like(rows, F32), like((8, D), F32), like((4, *rows))]
+        + [like(g.shape, g.dtype) for g in goods],
+        in_specs=[VMEM_SPEC] * 5 + [ANY_SPEC] * len(goods),
+        out_specs=[VMEM_SPEC] * 3 + [ANY_SPEC] * len(goods),
+        scratch_shapes=sum_scratch() + [pltpu.SemaphoreType.DMA((24,)), pltpu.SemaphoreType.DMA((24,))],
+        compiler_params=pltpu.CompilerParams(
+            collective_id=2, has_side_effects=True, vmem_limit_bytes=GIVEN_VMEM
+        ),
+        cost_estimate=cost(55),
+        name="back_tokens",
+    )(back, grad_slots, mid, gains, valid, *goods)
+    return results[:3], list(results[3:])
+
+
+def attention_backward_kernel(bits, *refs):
+    refs = list(refs)
+    take = lambda n: [refs.pop(0) for _ in range(n)]
+    (
+        grad_ref,
+        output_ref,
+        mix_ref,
+        query_ref,
+        keyval_ref,
+        key_rope_ref,
+        lse_ref,
+        w_query_ref,
+        w_keyval_ref,
+        normed_ref,
+        latent_norm_ref,
+        col_ref,
+        row_ref,
+        cos_ref,
+        sin_ref,
+        out_ref,
+    ) = take(16)
+    sources = take(len(bits))
+    output_wgrad, query_wgrad, keyval_wgrad, part_ref, out_sum, out_end_a, out_end_b = take(7)
+    targets = take(len(bits))
+    output_got = take(1)[0]
+    mix_grad, query_grad, keyval_grad, key_grad, rope_grad, wide, send_sems, recv_sems = take(8)
+    copies = Copies(send_sems, recv_sems)
+    copies.greet((0, 1, 2))
+    pair = PairSum(copies, out_ref, *refs, None, None, None, None)
+    pair.start()
+    freight = Freight(copies, bits, sources, targets)
+    freight.start()
+    places = Places()
+    scale = (HD + RD) ** (-0.5)
+    w_query = w_query_ref[...].reshape(D, w_query_ref.shape[2])
+    for k in range(8):
+        block = jnp.concatenate([grad_ref[b, :, lanes(k)] for b in range(4)], axis=0)
+        s = k
+        output_wgrad[s] = tn(mix_ref[...], block).astype(BF16)
+        term = nt(block, output_ref[s])
+        if k == 0:
+            wide[:, :512] = term
+        else:
+            wide[:, :512] += term
+    mix_grad[...] = wide[:, :512].astype(BF16)
+    output_flight = copies.start(output_wgrad.at[pl.ds(4, 4)], output_got, DP, 0)
+    pair.cross()
+    for b in range(2):
+        cut = slice(b * 320, (b + 1) * 320)
+        allowed = masks(col_ref, row_ref, cut)
+        lse_lane = lax.broadcasted_iota(jnp.int32, (320, 128), 1)
+        rope_sum = jnp.zeros((320, SLOT), F32)
+        for h in range(4):
+            nope = query_ref[cut, lanes(h, 128)]
+            rope = query_ref[cut, 512:768]
+            mask = head_lanes(320, h)
+            rope = jnp.where(mask, rope, jnp.zeros_like(rope))
+            keys = keyval_ref[:, h * 256 : h * 256 + 128]
+            values = keyval_ref[:, h * 256 + 128 : h * 256 + 256]
+            scores = nt(nope, keys) + nt(rope, key_rope_ref[...])
+            lse = jnp.sum(jnp.where(lse_lane == h, lse_ref[cut], 0.0), axis=1, keepdims=True)
+            probs = jnp.where(allowed, jnp.exp(scores * scale - lse), 0.0)
+            grad = mix_grad[cut, lanes(h, 128)]
+            probs_grad = nt(grad, values)
+            inner = jnp.sum(probs * probs_grad, axis=1, keepdims=True)
+            scores_grad = (probs * (probs_grad - inner)).astype(BF16)
+            value_grad = tn(probs.astype(BF16), grad)
+            nope_grad = tn(scores_grad, nope) * scale
+            rope_part = tn(scores_grad, rope)
+            low, high = slice(h * 256, h * 256 + 128), slice(h * 256 + 128, h * 256 + 256)
+            if b == 0:
+                key_grad[:, low] = nope_grad
+                key_grad[:, high] = value_grad
+            else:
+                key_grad[:, low] += nope_grad
+                key_grad[:, high] += value_grad
+            if b == 0 and h == 0:
+                rope_grad[...] = rope_part
+            else:
+                rope_grad[...] += rope_part
+            query_grad[cut, lanes(h, 128)] = (nn(scores_grad, keys) * scale).astype(BF16)
+            rope_sum = rope_sum + jnp.where(mask, nn(scores_grad, key_rope_ref[...]), 0.0)
+        rope_sum = rope_sum * scale
+        back_a, back_b = turn(rope_sum[:, :128], rope_sum[:, 128:], cos_ref[cut], -sin_ref[cut])
+        query_grad[cut, 512:640] = back_a.astype(BF16)
+        query_grad[cut, 640:768] = back_b.astype(BF16)
+    keyval_grad[...] = key_grad[...].astype(BF16)
+    plain = nt(query_grad[...], sort_columns(768)).astype(BF16)
+    for k in range(8):
+        query_wgrad[k] = tn(normed_ref[:, lanes(k)], plain).astype(BF16)
+    wide[:512, :] = tn(latent_norm_ref[...], keyval_grad[...])
+    for k in range(8):
+        start = pl.multiple_of(places[k] * 64, 64)
+        keyval_wgrad[k] = wide[pl.ds(start, 64), :].astype(BF16)
+    row = lax.broadcasted_iota(jnp.int32, (SLOT, 128), 0)
+    lane = lax.broadcasted_iota(jnp.int32, (SLOT, 128), 1)
+    fold = jnp.where(lane == lax.rem(row, 32) + 32 * (row // 128), scale, 0.0)
+    for b in range(4):
+        cut = slice(b * 160, (b + 1) * 160)
+        for k in range(4):
+            columns = lanes(k, 512)
+            part_ref[b, :, columns] = nt(query_grad[cut], w_query[columns]).astype(BF16)
+        part_ref[b, :, D : D + KR] = nt(keyval_grad[cut], w_keyval_ref[...]).astype(BF16)
+        rope = lax.dot_general(
+            rope_grad[cut],
+            fold,
+            (((1,), (0,)), ((), ())),
+            precision=lax.Precision.HIGHEST,
+            preferred_element_type=F32,
+        )
+        part_ref[b, :, D + KR :] = rope.astype(BF16)
+    pair.settle(out_sum, out_end_a, out_end_b)
+    output_flight.wait()
+    freight.wait()
+
+
+def attention_backward(grad, saved, out, freight):
+    shapes = [like((8, 512, SLOT)), like((8, SLOT, 768)), like((8, 64, 1024)), like((4, 160, D + KR + 128))]
+    shapes += [like((160, D), F32), like((1, 160, 1024)), like((1, 160, 1024))]
+    bits = tuple(bit for bit, _ in freight)
+    goods = [array for _, array in freight]
+    kept = (saved.output, saved.mix, saved.query_final, saved.keyval_final, saved.key_rope, saved.lse, saved.query)
+    kept += (saved.w_keyval, saved.normed, saved.latent_norm, saved.col, saved.row, saved.cos, saved.sin)
+    results = pl.pallas_call(
+        functools.partial(attention_backward_kernel, bits),
+        out_shape=shapes + [like(g.shape) for g in goods] + [like((4, 512, SLOT))],
+        in_specs=[VMEM_SPEC] * 16 + [ANY_SPEC] * len(goods),
+        out_specs=[VMEM_SPEC] * len(shapes) + [ANY_SPEC] * (len(goods) + 1),
+        scratch_shapes=[
+            pltpu.VMEM((TOK, 512), BF16),
+            pltpu.VMEM((TOK, 768), BF16),
+            pltpu.VMEM((TOK, 1024), BF16),
+            pltpu.VMEM((TOK, 1024), F32),
+            pltpu.VMEM((TOK, SLOT), F32),
+            pltpu.VMEM((TOK, 1024), F32),
+            pltpu.SemaphoreType.DMA((32,)),
+            pltpu.SemaphoreType.DMA((32,)),
+            *sum_scratch()[:5],
+        ],
+        compiler_params=pltpu.CompilerParams(
+            collective_id=4, has_side_effects=True, vmem_limit_bytes=GIVEN_VMEM
+        ),
+        cost_estimate=cost(30),
+        name="attention_backward",
+    )(grad, *kept, out, *goods)
+    return results[:7], list(results[7:])
+
+
+class SlotSum:
+    def __init__(self, copies, values, bits, got, give, rows=None):
+        self.copies, self.values, self.bits, self.got, self.give = copies, values, list(bits), got, give
+        self.rows = rows or (0, values.shape[1])
+        self.level = 0
+        self.flying = None
+
+    def view(self, ref, first, count):
+        return ref.at[pl.ds(first, count), pl.ds(*self.rows)]
+
+    def start(self):
+        half = 4 >> self.level
+        if self.level == 0:
+            source = self.view(self.values, half, half)
+        else:
+            first, size = self.rows
+            for k in range(half):
+                self.give[self.level - 1][k, first : first + size] = self.total(half + k).astype(BF16)
+            source = self.view(self.give[self.level - 1], 0, half)
+        target = self.view(self.got[self.level], 0, half)
+        self.flying = self.copies.start(source, target, DP, self.bits[self.level])
+        self.level += 1
+
+    def total(self, k):
+        cut = slice(self.rows[0], self.rows[0] + self.rows[1])
+        value = self.values[k, cut].astype(F32)
+        for level in range(self.level):
+            value = value + self.got[level][k, cut].astype(F32)
+        return value
+
+    def wait(self):
+        self.flying.wait()
+        if self.level < len(self.bits):
+            self.start()
+
+
+def slot_sum_scratch(shape):
+    spaces = [pltpu.VMEM((n, *shape), BF16) for n in (4, 2, 1)]
+    return spaces + [pltpu.VMEM((n, *shape), BF16) for n in (2, 1)]
+
+
+def tail_kernel(
+    n_rest,
+    n_last,
+    part_ref,
+    output_wgrad,
+    query_wgrad,
+    keyval_wgrad,
+    normed_ref,
+    w_latent_ref,
+    gains_ref,
+    latent_gain_ref,
+    latent_c_ref,
+    res_ref,
+    mid_grad_ref,
+    ffn_gain_ref,
+    output_came,
+    mid_ref,
+    valid_ref,
+    out_sum,
+    out_end_a,
+    out_end_b,
+    cos_ref,
+    sin_ref,
+    *refs,
+):
+    refs = list(refs)
+    take = lambda n: [refs.pop(0) for _ in range(n)]
+    rest_refs, stay_refs = take(n_rest), take(n_rest)
+    last_refs = take(n_last)
+    output_owned, query_owned, keyval_owned, latent_owned, res_grad_ref, res_out_ref = take(6)
+    rest_cames, end_cames = take(n_rest), take(n_rest)
+    last_cames = take(n_last)
+    send_sems, recv_sems = take(2)
+    sums = []
+    copies = Copies(send_sems, recv_sems)
+    for values, bits in (
+        (query_wgrad, (0, 1, 2)),
+        (keyval_wgrad, (0, 1, 2)),
+        (output_wgrad, (0, 1, 2)),
+    ):
+        space = take(5)
+        if values is query_wgrad:
+            half = values.shape[1] // 2
+            for k in range(2):
+                sums.append(SlotSum(copies, values, bits, space[:3], space[3:], (k * half, half)))
+        else:
+            sums.append(SlotSum(copies, values, bits, space[:3], space[3:]))
+    latent_values = take(1)[0]
+    space = take(5)
+    latent_sum = SlotSum(copies, latent_values, (0, 1, 2), space[:3], space[3:])
+    got_c, give_x, got_x = take(3)
+    latent_all, gain_rows, gain_c, gain_x, gain_columns, wide, end_one, end_two, end_sum, local_sems = take(10)
+    copies.local_sems = local_sems
+    copies.greet((0, 1, 2))
+    last_a, last_b = take(2)
+    out_ends = [copies.swapped(out_end_a, last_a, 0, 1024), copies.start(out_end_b, last_b, TENSOR, 1)]
+    rests = [copies.start(a, b, DP, 2) for a, b in zip(rest_refs, rest_cames)]
+    lasts = [copies.start(a, b, DP, 1) for a, b in zip(last_refs, last_cames)]
+    stays = [copies.local(stay_refs[g].at[1], end_one.at[g]) for g in range(n_rest)]
+    query_first, query_second, keyval_sum, output_sum = sums
+    output_sum.got[0] = output_came
+    output_sum.level = 1
+    query_first.start()
+    output_sum.start()
+    c_far = copies.start(part_ref.at[pl.ds(3, 1)], got_c.at[pl.ds(1, 1)], TENSOR, 0)
+    c_near = copies.start(part_ref.at[pl.ds(2, 1)], got_c.at[pl.ds(0, 1)], TENSOR, 0)
+    c_far.wait()
+    give_x[0] = (part_ref[1].astype(F32) + got_c[1].astype(F32)).astype(BF16)
+    x_far = copies.start(give_x, got_x, TENSOR, 1)
+    c_near.wait()
+    query_first.wait()
+    query_second.start()
+    x_far.wait()
+
+    def summed(columns):
+        return (
+            part_ref[0, :, columns].astype(F32)
+            + got_c[0, :, columns].astype(F32)
+            + got_x[0, :, columns].astype(F32)
+        )
+
+    latent_c = latent_c_ref[...]
+    latent_gain = latent_gain_ref[0:1]
+    factor = lax.rsqrt(jnp.mean(latent_c * latent_c, axis=1, keepdims=True) + NORM_EPS)
+    grad = summed(slice(D, D + KR))
+    scaled = grad * latent_gain
+    inner = jnp.mean(scaled * latent_c, axis=1, keepdims=True)
+    latent_back = factor * (scaled - latent_c * factor * factor * inner)
+    latent_gain_part = jnp.sum(grad * latent_c * factor, axis=0, keepdims=True)
+    rope = summed(slice(D + KR, D + KR + 128))
+    cos, sin = cos_ref[...], sin_ref[...]
+    lane = lax.broadcasted_iota(jnp.int32, rope.shape, 1)
+    other = jnp.where(lane < 32, pltpu.roll(rope, 96, 1), pltpu.roll(rope, 32, 1))
+    rope_back = jnp.where(lane < 32, rope * cos + other * sin, rope * cos - other * sin)
+    rope_back = jnp.where(lane < RD, rope_back, 0.0)
+    latent_all[0, :, :KR] = latent_back.astype(BF16)
+    latent_all[0, :, KR:] = rope_back.astype(BF16)
+    own = latent_all.at[pl.ds(0, 1)]
+    l_x = copies.start(own, latent_all.at[pl.ds(1, 1)], TENSOR, 1)
+    l_c = copies.start(own, latent_all.at[pl.ds(2, 1)], TENSOR, 0)
+    res = res_ref[...].astype(F32)
+    factor = lax.rsqrt(jnp.mean(res * res, axis=1, keepdims=True) + NORM_EPS)
+    grad = summed(slice(0, D)) + nt(latent_all[0], w_latent_ref[...])
+    scaled = grad * gains_ref[0:1]
+    inner = jnp.mean(scaled * res, axis=1, keepdims=True)
+    res_grad_ref[...] = mid_grad_ref[...] + factor * (scaled - res * factor * factor * inner)
+    row = lax.broadcasted_iota(jnp.int32, (8, D), 0)
+    attn_part = jnp.broadcast_to(jnp.sum(grad * res * factor, axis=0, keepdims=True), (8, D))
+    gain_rows[0] = jnp.where(row == 0, attn_part, jnp.where(row == 1, ffn_gain_ref[...], 0.0))
+    latent_row = jnp.broadcast_to(latent_gain_part, (8, KR))
+    gain_rows[0, :, :KR] = jnp.where(
+        lax.broadcasted_iota(jnp.int32, (8, KR), 0) == 2, latent_row, gain_rows[0, :, :KR]
+    )
+    g_c = copies.start(gain_rows, gain_c, TENSOR, 0)
+    query_second.wait()
+    keyval_sum.start()
+    query_first.wait()
+    l_x.wait()
+    l_far = copies.start(latent_all.at[pl.ds(1, 1)], latent_all.at[pl.ds(3, 1)], TENSOR, 0)
+    g_c.wait()
+    gain_rows[0] = gain_rows[0] + gain_c[0]
+    g_x = copies.start(gain_rows, gain_x, TENSOR, 1)
+    l_c.wait()
+    l_far.wait()
+    g_x.wait()
+    output_sum.wait()
+    keyval_sum.wait()
+    query_second.wait()
+    gain_columns[:, 0:8] = (gain_rows[0] + gain_x[0]).T
+    tensor = lax.axis_index(TENSOR)
+    dp = lax.axis_index(DP)
+    latent_rows = jnp.concatenate([latent_all[b] for b in range(4)], axis=0)
+    for k in range(8):
+        wide[...] = tn(normed_ref[:, lanes(k)], latent_rows)
+        block = wide[pl.ds(pl.multiple_of(tensor * 64, 64), 64), :]
+        start = pl.multiple_of(k * SLOT + tensor * 64, 64)
+        columns = gain_columns[pl.ds(start, 64), 0:8]
+        start = pl.multiple_of(crossed(dp, COLUMNS[k], 3) * 64 + tensor * 16, 16)
+        latent_values[k] = block.astype(BF16)
+        lane = lax.broadcasted_iota(jnp.int32, (64, 128), 1)
+        ends = block[:, KR : KR + 128]
+        ends = jnp.where(lane == 64, columns[:, 0:1], ends)
+        ends = jnp.where(lane == 65, columns[:, 1:2], ends)
+        latent_values[k, :, KR:] = ends.astype(BF16)
+        corner = gain_columns[pl.ds(start, 16), 0:8][:, 2:3]
+        lane = lax.broadcasted_iota(jnp.int32, (16, 128), 1)
+        latent_values[k, 0:16, KR:] = jnp.where(lane == 66, corner, ends[0:16]).astype(BF16)
+    latent_sum.start()
+    ends = []
+    for g in range(n_rest):
+        rests[g].wait()
+        stays[g].wait()
+        comes = copies.local(rest_cames[g].at[1], end_two.at[g])
+        comes.wait()
+        end_sum[g] = (end_one[g].astype(F32) + end_two[g].astype(F32)).astype(BF16)
+        ends.append(copies.start(end_sum.at[pl.ds(g, 1)], end_cames[g], DP, 1))
+    keyval_sum.wait()
+    output_sum.wait()
+    output_owned[...] = output_sum.total(0)
+    latent_sum.wait()
+    for flight in out_ends:
+        flight.wait()
+    valid = valid_ref[:, 0:1]
+    res_out_ref[:, :1024] = (mid_ref[:, :1024] + valid * (out_sum[:, :1024] + last_a[0].astype(F32))).astype(BF16)
+    res_out_ref[:, 1024:] = (mid_ref[:, 1024:] + valid * (out_sum[:, 1024:] + last_b[0].astype(F32))).astype(BF16)
+    latent_sum.wait()
+    half = query_owned.shape[0] // 2
+    query_first.wait()
+    query_owned[:half] = query_first.total(0)
+    keyval_sum.wait()
+    keyval_owned[...] = keyval_sum.total(0)
+    query_second.wait()
+    query_owned[half:] = query_second.total(0)
+    latent_sum.wait()
+    latent_owned[...] = latent_sum.total(0)
+    for copy in lasts + ends:
+        copy.wait()
+
+
+def tail(part, wgrads, output_came, out_parts, saved, mid_grad, ffn_gain, rests, stays, lasts):
+    output_wgrad, query_wgrad, keyval_wgrad = wgrads
+    rows = (160, D)
+    latent = (64, KR + 128)
+    shapes = [
+        like((512, SLOT), F32),
+        like((SLOT, 768), F32),
+        like((64, 1024), F32),
+        like(latent, F32),
+        like(rows, F32),
+        like(rows),
+    ]
+    part_row = (160, D + KR + 128)
+    unit = rests[0].shape[1:]
+    rows_spec = pl.BlockSpec((160, 128), lambda i: (0, 0))
+    results = pl.pallas_call(
+        functools.partial(tail_kernel, len(rests), len(lasts)),
+        out_shape=shapes + [like((2, *unit))] * len(rests) + [like((1, *unit))] * (len(rests) + len(lasts)),
+        grid=(1,),
+        in_specs=[VMEM_SPEC] * 18 + [rows_spec] * 2 + [ANY_SPEC] * (2 * len(rests) + len(lasts)),
+        out_specs=[VMEM_SPEC] * len(shapes) + [ANY_SPEC] * (2 * len(rests) + len(lasts)),
+        scratch_shapes=[
+            pltpu.SemaphoreType.DMA((40,)),
+            pltpu.SemaphoreType.DMA((40,)),
+            *slot_sum_scratch((SLOT, 768)),
+            *slot_sum_scratch((64, 1024)),
+            *slot_sum_scratch((512, SLOT)),
+            pltpu.VMEM((8, *latent), BF16),
+            *slot_sum_scratch(latent),
+            pltpu.VMEM((2, *part_row), BF16),
+            pltpu.VMEM((1, *part_row), BF16),
+            pltpu.VMEM((1, *part_row), BF16),
+            pltpu.VMEM((4, 160, KR + 128), BF16),
+            pltpu.VMEM((1, 8, D), F32),
+            pltpu.VMEM((1, 8, D), F32),
+            pltpu.VMEM((1, 8, D), F32),
+            pltpu.VMEM((D, 128), F32),
+            pltpu.VMEM((SLOT, KR + 128), F32),
+            pltpu.VMEM((3, *unit), BF16),
+            pltpu.VMEM((3, *unit), BF16),
+            pltpu.VMEM((3, *unit), BF16),
+            pltpu.SemaphoreType.DMA((8,)),
+            pltpu.VMEM((1, 160, 1024), BF16),
+            pltpu.VMEM((1, 160, 1024), BF16),
+        ],
+        compiler_params=pltpu.CompilerParams(
+            collective_id=3, has_side_effects=True, vmem_limit_bytes=GIVEN_VMEM
+        ),
+        cost_estimate=cost(110),
+        name="tail",
+    )(
+        part,
+        output_wgrad,
+        query_wgrad,
+        keyval_wgrad,
+        saved.normed,
+        saved.w_latent,
+        saved.gains,
+        saved.latent_gain,
+        saved.latent_c,
+        saved.res,
+        mid_grad,
+        ffn_gain,
+        output_came,
+        saved.mid,
+        saved.valid,
+        *out_parts,
+        saved.cos,
+        saved.sin,
+        *rests,
+        *stays,
+        *lasts,
+    )
+    n = len(rests)
+    return results[:6], results[6 : 6 + n], results[6 + n : 6 + 2 * n], results[6 + 2 * n :]
+
+
+def finish_kernel(
+    n_came,
+    places,
+    res_out_ref,
+    res_grad_ref,
+    latent_ref,
+    *refs,
+):
+    refs = list(refs)
+    take = lambda n: [refs.pop(0) for _ in range(n)]
+    stays, cames, others = take(9), take(n_came), take(9)
+    res_out, res_grad, latent, gains, expert_in, expert_out, shared_in, shared_out = refs
+    for k in range(8):
+        block = pl.ds(pl.multiple_of(places[k] * SLOT, SLOT), SLOT)
+        res_out[:, block] = res_out_ref[:, lanes(k)]
+        res_grad[:, block] = res_grad_ref[:, lanes(k)]
+    latent[...] = latent_ref[:, : KR + RD]
+    gains[...] = latent_ref[:, KR : KR + 128].T[64:72]
+    side = places[8]
+    n_half = expert_in.shape[0] // 2
+    width = expert_out.shape[1]
+    for p in range(n_half + 1):
+        for mine in (True, False):
+            which = side if mine else 1 - side
+            for g in range(3):
+                value = (stays if mine else others)[3 * p + g][0].astype(F32)
+                late = 3 * p + g - 9 + n_came
+                if mine and late >= 0:
+                    value = value + cames[late][0].astype(F32)
+                if p < n_half and g < 2:
+                    expert_in[which * n_half + p, g] = value
+                elif p < n_half:
+                    expert_out[which * n_half + p] = value
+                else:
+                    cut = pl.ds(pl.multiple_of(which * width, 8), width)
+                    if g < 2:
+                        shared_in[g, cut] = value
+                    else:
+                        shared_out[cut] = value
+
+
+def finish(places, res_out, res_grad, latent, stays, cames, others, width):
+    shapes = [
+        like(res_out.shape),
+        like(res_grad.shape, F32),
+        like((64, KR + RD), F32),
+        like((8, 64), F32),
+        like((EXPERTS, 2, width, SLOT), F32),
+        like((EXPERTS, width, SLOT), F32),
+        like((2, 2 * width, SLOT), F32),
+        like((2 * width, SLOT), F32),
+    ]
+    return pl.pallas_call(
+        functools.partial(finish_kernel, len(cames)),
+        out_shape=shapes,
+        in_specs=[SMEM_SPEC] + [VMEM_SPEC] * (21 + len(cames)),
+        out_specs=[VMEM_SPEC] * len(shapes),
+        compiler_params=pltpu.CompilerParams(vmem_limit_bytes=GIVEN_VMEM),
+        cost_estimate=cost(10),
+        name="finish",
+    )(places, res_out, res_grad, latent, *stays, *cames, *others)
+
+
+def body(
+    res_in,
+    out_grad,
+    seg_ids,
+    tok_counts,
+    slot_table,
+    slot_gates,
+    attn_gain,
+    latent_gain,
+    ffn_gain,
+    w_latent,
+    w_query,
+    w_keyval,
+    w_output,
+    w_expert_in,
+    w_expert_out,
+    w_shared_in,
+    w_shared_out,
+):
+    dp = lax.axis_index(DP)
+    rows = res_in.shape[0]
+    first = ((dp >> 1) & 1) == 0
+    n_half = EXPERTS // 2
+    width = w_expert_out.shape[1]
+    pack = jnp.concatenate(
+        [
+            w_latent,
+            attn_gain[:, None],
+            ffn_gain[:, None],
+            jnp.pad(latent_gain, (0, w_latent.shape[0] - latent_gain.shape[0]))[:, None],
+            jnp.zeros((w_latent.shape[0], 61), BF16),
+        ],
+        axis=1,
+    )
+    grad_pair, over_gate, lows, highs, saved = front(
+        tok_counts,
+        pack,
+        w_keyval,
+        w_output,
+        w_expert_in,
+        w_expert_out,
+        w_shared_in,
+        w_shared_out,
+        res_in,
+        out_grad,
+        w_query,
+        seg_ids,
+        slot_table[0],
+        slot_gates[0],
+    )
+    pair_gate = jnp.concatenate(
+        [g[:, k * rows : (k + 1) * rows] for k in range(4) for g in (saved.gates, over_gate)], axis=1
+    )
+    pair_gate = jnp.where(first, pair_gate[:n_half], pair_gate[n_half : 2 * n_half])
+    mid_pair = saved.mid_pair.reshape(-1, D)
+    grad_pair = grad_pair.reshape(-1, D)
+    ones = jnp.ones_like(pair_gate[0])
+    whole = 3 * width
+    low, high = lows[2], highs[2]
+    sums, keep0, give0, (high_far,) = experts_step(
+        mid_pair,
+        grad_pair,
+        [(lows[0], 0, 4, 0, whole, 0), (highs[0], 4, 4, 0, whole, 0)],
+        pair_gate[0],
+        None,
+        False,
+        [Cut(low, 0, (0, 4), (width, whole - width))],
+        5,
+    )
+    sums, keep1, give1, (y0a, y0b) = experts_step(
+        mid_pair,
+        grad_pair,
+        [(lows[1], 0, 4, 0, whole, 0), (highs[1], 4, 4, 0, whole, 0)],
+        pair_gate[1],
+        sums,
+        False,
+        [Cut(give0[0], 0), Cut(give0[1], 0)],
+        6,
+    )
+    (k0a, h0a), (k0b, h0b) = halve([(keep0[0], y0a), (keep0[1], y0b)])
+    (back, out), keep2, give2, (y0c, y1a, z0a, z0b) = experts_step(
+        mid_pair,
+        grad_pair,
+        [
+            (low, 0, 4, 0, whole, 0),
+            (high, 4, 4, 0, width, 0),
+            (high_far, 4, 4, width, whole - width, 0),
+        ],
+        ones,
+        sums,
+        True,
+        [Cut(give0[2], 0), Cut(give1[0], 0), Cut(h0a, 2), Cut(h0b, 2)],
+        7,
+    )
+    (k0c, h0c), (k1a, h1a), (s0a, m0a), (s0b, m0b) = halve(
+        [(keep0[2], y0c), (keep1[0], y1a), (k0a, z0a), (k0b, z0b)]
+    )
+    back = back.reshape(8, rows, D)
+    out = out.reshape(8, rows, D)
+    (mid_grad, ffn_gain_part, attn_grad), (y1b, y1c, y2a, y2b, z0c, z1a, o0a, o0b) = back_tokens(
+        back,
+        saved.grad,
+        saved.mid,
+        saved.gains,
+        saved.valid,
+        [(0, give1[1]), (0, give1[2]), (0, give2[0]), (0, give2[1]), (2, h0c), (2, h1a), (1, m0a), (1, m0b)],
+    )
+    (k1b, h1b), (k1c, h1c), (k2a, h2a), (k2b, h2b), (s0c, m0c), (s1a, m1a) = halve(
+        [(keep1[1], y1b), (keep1[2], y1c), (keep2[0], y2a), (keep2[1], y2b), (k0c, z0c), (k1a, z1a)]
+    )
+    (*wgrads, back_part, out_sum, out_a, out_b), (y2c, z1b, z1c, z2a, o0c, o1a, output_came) = attention_backward(
+        attn_grad,
+        saved,
+        out,
+        [(0, give2[2]), (2, h1b), (2, h1c), (2, h2a), (1, m0c), (1, m1a)],
+    )
+    (k2c, h2c), (s1b, m1b), (s1c, m1c), (s2a, m2a) = halve(
+        [(keep2[2], y2c), (k1b, z1b), (k1c, z1c), (k2a, z2a)]
+    )
+    (output_owned, query_owned, keyval_owned, latent_owned, res_grad, res_out), cames, ends, (o1b, o1c, o2a) = tail(
+        back_part,
+        wgrads,
+        output_came,
+        (out_sum, out_a, out_b),
+        saved,
+        mid_grad,
+        ffn_gain_part,
+        [h2b, h2c],
+        [k2b, k2c],
+        [m1b, m1c, m2a],
+    )
+    places = jnp.concatenate([dp ^ jnp.array(COLUMNS, jnp.int32), ((dp >> 1) & 1)[None]])
+    res_out, res_grad, latent_owned, gains, expert_in, expert_out, shared_in, shared_out = finish(
+        places,
+        res_out,
+        res_grad,
+        latent_owned,
+        [s0a, s0b, s0c, s1a, s1b, s1c, s2a, k2b, k2c],
+        cames,
+        [o0a, o0b, o0c, o1a, o1b, o1c, o2a, *ends],
+        width,
+    )
+    return (
+        res_out,
+        res_grad,
+        gains[0],
+        gains[2, : KR // 32],
+        gains[1],
+        latent_owned,
+        query_owned,
+        keyval_owned,
+        output_owned,
+        expert_in.transpose(0, 1, 3, 2),
+        expert_out,
+        shared_in.transpose(0, 2, 1),
+        shared_out,
+    )
+
+
 def solution(mesh):
     placed = (
-        P(("dp", "tensor"), None),
-        P(("dp", "tensor"), None),
-        P("dp", None),
-        P("dp"),
-        P("dp", None, None),
-        P("dp", None, None),
-        P(("dp", "tensor")),
-        P(("dp", "tensor")),
-        P(("dp", "tensor")),
-        P(("dp", "tensor"), None),
-        P("dp", "tensor"),
-        P("dp", "tensor"),
-        P("tensor", "dp"),
-        P(None, None, "dp", "tensor"),
-        P(None, "tensor", "dp"),
-        P(None, "dp", "tensor"),
-        P("tensor", "dp"),
-    )
+        P((DP, TENSOR), None),
+        P((DP, TENSOR), None),
+        P(DP, None),
+        P(DP),
+        P(DP, None, None),
+        P(DP, None, None),
+        P((DP, TENSOR)),
+        P((DP, TENSOR)),
+        P((DP, TENSOR)),
+        P((DP, TENSOR), None),
+        P(DP, TENSOR),
+        P(DP, TENSOR),
+        P(TENSOR, DP),
+        P(None, None, DP, TENSOR),
+        P(None, TENSOR, DP),
+        P(None, DP, TENSOR),
+        P(TENSOR, DP),
+    )
+    fits = mesh.shape[DP] == 8 and mesh.shape[TENSOR] == 4
     return jax.shard_map(
-        body,
+        body if fits else general_body,
         mesh=mesh,
         in_specs=placed,
         out_specs=(
-            P(("dp", "tensor"), None),
-            P(("dp", "tensor"), None),
-            P(("dp", "tensor")),
-            P(("dp", "tensor")),
-            P(("dp", "tensor")),
-            P(("dp", "tensor"), None),
-            P("dp", "tensor"),
-            P("dp", "tensor"),
-            P("tensor", "dp"),
-            P(None, None, "dp", "tensor"),
-            P(None, "tensor", "dp"),
-            P(None, "dp", "tensor"),
-            P("tensor", "dp"),
+            P((DP, TENSOR), None),
+            P((DP, TENSOR), None),
+            P((DP, TENSOR)),
+            P((DP, TENSOR)),
+            P((DP, TENSOR)),
+            P((DP, TENSOR), None),
+            P(DP, TENSOR),
+            P(DP, TENSOR),
+            P(TENSOR, DP),
+            P(None, None, DP, TENSOR),
+            P(None, TENSOR, DP),
+            P(None, DP, TENSOR),
+            P(TENSOR, DP),
         ),
         check_vma=False,
     )

time: 1040 us -> 642 us (0.62)
  Pallas kernels: 0 us -> 625 us
  waiting for transfers between devices: 591 us -> 0 us
  matrix products: 164 us -> 0 us
  other arithmetic: 99.5 us -> 0.6 us
  local copies, waits for them, and re-layouts: 109 us -> 11 us
  starting transfers between devices: 58.9 us -> 0 us
    pallas_call x0 -> x12, Pallas kernels: none -> 625 us  [the longest x1 234 us: front(): pl.pallas_call(functools.partial(front_kernel, width), out_shape=shapes,...]
    ppermute x76 -> x0, waiting for transfers between devices: 591 us -> none  [the longest x50 517 us: swap_dp(): return lax.ppermute(values, 'dp', flip_pairs(lax.axis_size('dp'), bit))]
    dot_general x37 -> x0, matrix products: 164 us -> none  [the longest x24 125 us: dot(): lax.dot_general(a, b, (contract, ((), ())), preferred_element_type=jnp.fl...]
    ppermute x76 -> x0, starting transfers between devices: 58.9 us -> none  [the longest x50 46.6 us: swap_dp(): return lax.ppermute(values, 'dp', flip_pairs(lax.axis_size('dp'), bit))]
    unnamed x325 -> x11, local copies, waits for them, and re-layouts: 57.2 us -> 2.39 us
    add x31 -> x0, other arithmetic: 35.3 us -> none  [the longest x6 12.8 us: scatter_tensor(): keep + swap_tensor(give.astype(jnp.bfloat16), bit).astype(jnp.float32)]
    concatenate x36 -> x1, other arithmetic: 29 us -> 0.59 us  [body(): jnp.concatenate([dp ^ jnp.array(COLUMNS, jnp.int32), (dp >> 1 & 1)[None]])]
    split x29 -> x0, local copies, waits for them, and re-layouts: 15.1 us -> none  [the longest x9 6.91 us: scatter_tensor(): keep, give = jnp.split(values, 2, axis=0)]
  transfers between devices with their start and end apart: 76 -> 0, of which waited for: 38 -> 0; matrix products, arithmetic and copies ran while one was open for 26% -> 0% of each run, Pallas kernels for 0% -> 0%
where the time goes in v3:
time: 642 us; the launch traced here: 639 us
  Pallas kernels  625 us (97%)
  local copies, waits for them, and re-layouts  11 us (2%)
    pallas_call x1, Pallas kernels, front(): pl.pallas_call(functools.partial(front_kernel, width), out_shape=shapes,...  234 us
    pallas_call x3, Pallas kernels, experts_step(): pl.pallas_call(functools.partial(experts_kernel, width, sums is not None,...  121 us
    pallas_call x1, Pallas kernels, tail(): pl.pallas_call(functools.partial(tail_kernel, len(rests), len(lasts)), ou...  114 us
    pallas_call x1, Pallas kernels, back_tokens(): pl.pallas_call(functools.partial(back_kernel, bits), out_shape=[like(rows...  72.6 us
    pallas_call x1, Pallas kernels, attention_backward(): pl.pallas_call(functools.partial(attention_backward_kernel, bits), out_sh...  63 us
    pallas_call x4, Pallas kernels, halve(): pl.pallas_call(functools.partial(halve_kernel, count), out_shape=shapes *...  14.9 us

profile of v3, /device:TPU:0, one launch (start us, length us, event | category | flops | bytes accessed | tf_op | source)
XLA Modules:
  0.0 638.6 jit_solution(13881675069759831600)
XLA Ops:
  0.6 0.7 pad_bitcast_fusion
  1.4 0.8 copy.32
  2.2 0.8 copy.33
  2.9 1.6 concatenate.10
  5.2 233.6 %front.1 = (bf16[8,160,2048]{2,1,0:T(8,128)(2,1)}, f32[8,640]{1,0:T(8,128)}, bf16[4,1056,256]{2,1,0:T(8,128)(2,1)}, bf16[4,1056,256]{2,1,0:T(8,128)(2,1)}, bf16[...) custom-call(s32[1]{0:T(128)S(6)} %copy.38.count_ref, ...), custom_call_target="tpu_custom_call" | custom-call | flops 219999993856 | bytes 220000000 | tf_op jit(solution)/shard_map/front/pallas_call | solution.py:1051
  238.8 0.9 fusion
  239.9 0.6 fusion.2
  240.5 39.9 %experts_step.3 = (f32[1280,2048]{1,0:T(8,128)}, f32[1280,2048]{1,0:T(8,128)}, bf16[4,352,256]{2,1,0:T(8,128)(2,1)}, bf16[4,352,256]{2,1,0:T(8,128)(2,1)}, bf16[...) custom-call(bf16[1280,2048]{1,0:T(8,128)(2,1)} %bitcast.38, ...), custom_call_target="tpu_custom_call" | custom-call | flops 35000000512 | bytes 35000000 | tf_op jit(solution)/shard_map/experts_step/pallas_call | solution.py:1191
  280.4 41.0 %experts_step.4 = (f32[1280,2048]{1,0:T(8,128)}, f32[1280,2048]{1,0:T(8,128)}, bf16[4,352,256]{2,1,0:T(8,128)(2,1)}, bf16[4,352,256]{2,1,0:T(8,128)(2,1)}, bf16[...) custom-call(bf16[1280,2048]{1,0:T(8,128)(2,1)} %bitcast.39, ...), custom_call_target="tpu_custom_call" | custom-call | flops 35000000512 | bytes 35000000 | tf_op jit(solution)/shard_map/experts_step/pallas_call | solution.py:1191
  321.4 2.9 halve.4
  324.3 0.6 broadcast_in_dim_broadcast_in_dim.3.refs_2_
  324.9 40.2 %experts_step.5 = (bf16[1280,2048]{1,0:T(8,128)(2,1)}, bf16[1280,2048]{1,0:T(8,128)(2,1)}, bf16[4,352,256]{2,1,0:T(8,128)(2,1)}, bf16[4,352,256]{2,1,0:T(8,128)(...) custom-call(bf16[1280,2048]{1,0:T(8,128)(2,1)} %bitcast.40, ...), custom_call_target="tpu_custom_call" | custom-call | flops 35000000512 | bytes 35000000 | tf_op jit(solution)/shard_map/experts_step/pallas_call | solution.py:1191
  365.1 3.6 halve.5
  368.8 72.6 %back_tokens.1 = (f32[160,2048]{1,0:T(8,128)}, f32[8,2048]{1,0:T(8,128)}, bf16[4,160,2048]{2,1,0:T(8,128)(2,1)}, bf16[4,352,256]{2,1,0:T(8,128)(2,1)}, bf16[4,35...) custom-call(bf16[8,160,2048]{2,1,0:T(8,128)(2,1)} %bitcast.42, ...), custom_call_target="tpu_custom_call" | custom-call | flops 54999998464 | bytes 55000000 | tf_op jit(solution)/shard_map/back_tokens/pallas_call | solution.py:1340
  441.4 5.0 halve.6
  446.4 63.0 %attention_backward.1 = (bf16[8,512,256]{2,1,0:T(8,128)(2,1)}, bf16[8,256,768]{2,1,0:T(8,128)(2,1)}, bf16[8,64,1024]{2,1,0:T(8,128)(2,1)}, bf16[4,160,2688]{2,1,...) custom-call(bf16[4,160,2048]{2,1,0:T(8,128)(2,1)} %get-tuple-element, ...), custom_call_target="tpu_custom_call" | custom-call | flops 30000001024 | bytes 30000000 | tf_op jit(solution)/shard_map/attention_backward/pallas_call | solution.py:1479
  509.4 3.2 halve.7
  512.7 113.8 %tail.1 = (f32[512,256]{1,0:T(8,128)}, f32[256,768]{1,0:T(8,128)}, f32[64,1024]{1,0:T(8,128)}, f32[64,640]{1,0:T(8,128)}, f32[160,2048]{1,0:T(8,128)}, /*index=5...) custom-call(bf16[4,160,2688]{2,1,0:T(8,128)(2,1)} %get-tuple-element, ...), custom_call_target="tpu_custom_call" | custom-call | flops 109999996928 | bytes 110000000 | tf_op jit(solution)/shard_map/tail/pallas_call | solution.py:1739
  627.1 6.4 %finish.1 = (bf16[160,2048]{1,0:T(8,128)(2,1)}, f32[160,2048]{1,0:T(8,128)}, f32[64,576]{1,0:T(8,128)}, f32[8,64]{1,0:T(8,128)}, f32[4,2,352,256]{3,2,1,0:T(8,12...) custom-call(s32[9]{0:T(128)} %pad_add_fusion.places, ...), custom_call_target="tpu_custom_call" | custom-call | flops 10000000000 | bytes 10000000 | tf_op jit(solution)/shard_map/finish/pallas_call | solution.py:1853
  633.6 1.3 slice_bitcast_fusion
  634.9 1.2 slice_bitcast_fusion.1
  636.1 0.9 copy.39
  636.9 0.7 copy.40
  637.6 0.8 copy.41
  (14 shorter events, 0.8 us)
Async XLA Ops:
  512.7 113.8 %copy-start.3 = (s32[8]{0:T(128)S(1)}, s32[8]{0:T(128)}, u32[]{:S(2)}) copy-start(s32[8]{0:T(128)} %constant.20.clone) | copy-start | bytes 100
  627.1 8.9 %copy-start = (f32[256,768]{1,0:T(8,128)S(1)}, f32[256,768]{1,0:T(8,128)}, u32[]{:S(2)}) copy-start(f32[256,768]{1,0:T(8,128)} %get-tuple-element.330) | copy-start | bytes 2359300
  627.1 9.8 %copy-start.2 = (f32[64,1024]{1,0:T(8,128)S(1)}, f32[64,1024]{1,0:T(8,128)}, u32[]{:S(2)}) copy-start(f32[64,1024]{1,0:T(8,128)} %get-tuple-element.331) | copy-start | bytes 786436
  633.6 4.1 copy-start.1

commit v4 on v3

--- a/solution.py
+++ b/solution.py
@@ -921,8 +921,6 @@
             tokens.wait()
             grad_own = copies.local(at.masked, grad_pair.at[pl.ds(0, 1)])
             grad_x = copies.start(at.masked, grad_pair.at[pl.ds(2, 1)], TENSOR, 1)
-        elif tau == 2:
-            unit_first()
         elif tau == 3:
             pack.wait()
             pack_tensor = SlotGather(copies, None, at.pack, TENSOR_BITS, TENSOR)
@@ -998,6 +996,7 @@
     c_far.wait()
     at.give_x[0] = (at.part[1].astype(F32) + at.got_c[1].astype(F32)).astype(BF16)
     x_far = copies.start(at.give_x, at.got_x, TENSOR, 1)
+    pump()
     grad_zx.wait()
     grad_own.wait()
     grad_c = copies.start(grad_pair.at[pl.ds(0, 4)], grad_pair.at[pl.ds(4, 4)], TENSOR, 0)
@@ -1088,6 +1087,40 @@
             flight.wait()
 
 
+class Split:
+    def __init__(self, copies, keep, got, kept, gone):
+        self.copies, self.kept, self.gone = copies, kept, gone
+        self.loads = [copies.local(keep, kept), copies.local(got, gone)]
+        self.half = kept.shape[0] // 2
+        self.flights = []
+
+    def send(self, bit, target, stay=None):
+        for load in self.loads:
+            load.wait()
+        for k in range(2 * self.half):
+            target_ref = self.kept if k < self.half else self.gone
+            target_ref[k] = (self.kept[k].astype(F32) + self.gone[k].astype(F32)).astype(BF16)
+        self.flights.append(
+            self.copies.start(self.gone.at[pl.ds(self.half, self.half)], target, DP, bit)
+        )
+        if stay is not None:
+            self.flights.append(self.copies.local(self.kept.at[pl.ds(0, self.half)], stay))
+
+    def wait(self):
+        for flight in self.flights:
+            flight.wait()
+
+
+def split_scratch(splits):
+    return [pltpu.VMEM(keep.shape, BF16) for keep, _, _ in splits for _ in range(2)] + [
+        pltpu.SemaphoreType.DMA((4 * len(splits),))
+    ]
+
+
+def split_outputs(splits):
+    return [like((keep.shape[0] // 2, *keep.shape[1:])) for keep, _, _ in splits for _ in range(2)]
+
+
 def experts_kernel(width, has_sum, bits, parts, *refs):
     refs = list(refs)
     take = lambda n: [refs.pop(0) for _ in range(n)]
@@ -1296,20 +1329,26 @@
     return [pltpu.VMEM((4, 160, D), BF16), half, half, half, half, end, end, end, end]
 
 
-def back_kernel(bits, *refs):
+def back_kernel(bits, splits, *refs):
     refs = list(refs)
     take = lambda n: [refs.pop(0) for _ in range(n)]
     back_ref, grad_ref, mid_ref, gains_ref, valid_ref = take(5)
     sources = take(len(bits))
+    pairs = take(2 * len(splits))
     mid_grad_ref, gain_part_ref, tokens_ref = take(3)
     targets = take(len(bits))
-    *buffers, send_sems, recv_sems = refs
-    copies = Copies(send_sems, recv_sems)
+    ends = take(2 * len(splits))
+    rooms = take(2 * len(splits))
+    local_sems, *buffers, send_sems, recv_sems = refs
+    copies = Copies(send_sems, recv_sems, local_sems)
+    parts = [Split(copies, *pairs[2 * k : 2 * k + 2], *rooms[2 * k : 2 * k + 2]) for k in range(len(splits))]
     copies.greet((0, 1, 2))
     freight = Freight(copies, bits, sources, targets)
     freight.start()
     pair = PairSum(copies, back_ref, *buffers)
     pair.start()
+    for k, bit in enumerate(splits):
+        parts[k].send(bit, ends[2 * k + 1], ends[2 * k])
     pair.cross()
     pair.end()
     first, second = pair.total()
@@ -1331,29 +1370,34 @@
     c_own.wait()
     c_far.wait()
     freight.wait()
-
-
-def back_tokens(back, grad_slots, mid, gains, valid, freight):
+    for part in parts:
+        part.wait()
+
+
+def back_tokens(back, grad_slots, mid, gains, valid, freight, splits):
     rows = (160, D)
     bits = tuple(bit for bit, _ in freight)
     goods = [array for _, array in freight]
     results = pl.pallas_call(
-        functools.partial(back_kernel, bits),
+        functools.partial(back_kernel, bits, tuple(bit for _, _, bit in splits)),
         out_shape=[like(rows, F32), like((8, D), F32), like((4, *rows))]
-        + [like(g.shape, g.dtype) for g in goods],
-        in_specs=[VMEM_SPEC] * 5 + [ANY_SPEC] * len(goods),
-        out_specs=[VMEM_SPEC] * 3 + [ANY_SPEC] * len(goods),
-        scratch_shapes=sum_scratch() + [pltpu.SemaphoreType.DMA((24,)), pltpu.SemaphoreType.DMA((24,))],
+        + [like(g.shape, g.dtype) for g in goods]
+        + split_outputs(splits),
+        in_specs=[VMEM_SPEC] * 5 + [ANY_SPEC] * (len(goods) + 2 * len(splits)),
+        out_specs=[VMEM_SPEC] * 3 + [ANY_SPEC] * (len(goods) + 2 * len(splits)),
+        scratch_shapes=split_scratch(splits)
+        + sum_scratch() + [pltpu.SemaphoreType.DMA((24,)), pltpu.SemaphoreType.DMA((24,))],
         compiler_params=pltpu.CompilerParams(
             collective_id=2, has_side_effects=True, vmem_limit_bytes=GIVEN_VMEM
         ),
         cost_estimate=cost(55),
         name="back_tokens",
-    )(back, grad_slots, mid, gains, valid, *goods)
-    return results[:3], list(results[3:])
-
-
-def attention_backward_kernel(bits, *refs):
+    )(back, grad_slots, mid, gains, valid, *goods, *[v for keep, got, _ in splits for v in (keep, got)])
+    n = 3 + len(goods)
+    return results[:3], list(results[3:n]), list(zip(results[n::2], results[n + 1 :: 2]))
+
+
+def attention_backward_kernel(bits, splits, *refs):
     refs = list(refs)
     take = lambda n: [refs.pop(0) for _ in range(n)]
     (
@@ -1375,16 +1419,23 @@
         out_ref,
     ) = take(16)
     sources = take(len(bits))
+    pairs = take(2 * len(splits))
     output_wgrad, query_wgrad, keyval_wgrad, part_ref, out_sum, out_end_a, out_end_b = take(7)
     targets = take(len(bits))
     output_got = take(1)[0]
+    ends = take(2 * len(splits))
+    rooms = take(2 * len(splits))
+    local_sems = take(1)[0]
     mix_grad, query_grad, keyval_grad, key_grad, rope_grad, wide, send_sems, recv_sems = take(8)
-    copies = Copies(send_sems, recv_sems)
+    copies = Copies(send_sems, recv_sems, local_sems)
+    parts = [Split(copies, *pairs[2 * k : 2 * k + 2], *rooms[2 * k : 2 * k + 2]) for k in range(len(splits))]
     copies.greet((0, 1, 2))
     pair = PairSum(copies, out_ref, *refs, None, None, None, None)
     pair.start()
     freight = Freight(copies, bits, sources, targets)
     freight.start()
+    for k, bit in enumerate(splits):
+        parts[k].send(bit, ends[2 * k + 1], ends[2 * k])
     places = Places()
     scale = (HD + RD) ** (-0.5)
     w_query = w_query_ref[...].reshape(D, w_query_ref.shape[2])
@@ -1467,9 +1518,11 @@
     pair.settle(out_sum, out_end_a, out_end_b)
     output_flight.wait()
     freight.wait()
-
-
-def attention_backward(grad, saved, out, freight):
+    for part in parts:
+        part.wait()
+
+
+def attention_backward(grad, saved, out, freight, splits):
     shapes = [like((8, 512, SLOT)), like((8, SLOT, 768)), like((8, 64, 1024)), like((4, 160, D + KR + 128))]
     shapes += [like((160, D), F32), like((1, 160, 1024)), like((1, 160, 1024))]
     bits = tuple(bit for bit, _ in freight)
@@ -1477,11 +1530,12 @@
     kept = (saved.output, saved.mix, saved.query_final, saved.keyval_final, saved.key_rope, saved.lse, saved.query)
     kept += (saved.w_keyval, saved.normed, saved.latent_norm, saved.col, saved.row, saved.cos, saved.sin)
     results = pl.pallas_call(
-        functools.partial(attention_backward_kernel, bits),
-        out_shape=shapes + [like(g.shape) for g in goods] + [like((4, 512, SLOT))],
-        in_specs=[VMEM_SPEC] * 16 + [ANY_SPEC] * len(goods),
-        out_specs=[VMEM_SPEC] * len(shapes) + [ANY_SPEC] * (len(goods) + 1),
-        scratch_shapes=[
+        functools.partial(attention_backward_kernel, bits, tuple(bit for _, _, bit in splits)),
+        out_shape=shapes + [like(g.shape) for g in goods] + [like((4, 512, SLOT))] + split_outputs(splits),
+        in_specs=[VMEM_SPEC] * 16 + [ANY_SPEC] * (len(goods) + 2 * len(splits)),
+        out_specs=[VMEM_SPEC] * len(shapes) + [ANY_SPEC] * (len(goods) + 1 + 2 * len(splits)),
+        scratch_shapes=split_scratch(splits)
+        + [
             pltpu.VMEM((TOK, 512), BF16),
             pltpu.VMEM((TOK, 768), BF16),
             pltpu.VMEM((TOK, 1024), BF16),
@@ -1497,8 +1551,9 @@
         ),
         cost_estimate=cost(30),
         name="attention_backward",
-    )(grad, *kept, out, *goods)
-    return results[:7], list(results[7:])
+    )(grad, *kept, out, *goods, *[v for keep, got, _ in splits for v in (keep, got)])
+    n = 8 + len(goods)
+    return results[:7], list(results[7:n]), list(zip(results[n::2], results[n + 1 :: 2]))
 
 
 class SlotSum:
@@ -1569,11 +1624,10 @@
 ):
     refs = list(refs)
     take = lambda n: [refs.pop(0) for _ in range(n)]
-    rest_refs, stay_refs = take(n_rest), take(n_rest)
-    last_refs = take(n_last)
+    rest_pairs, last_pairs = take(2 * n_rest), take(2 * n_last)
     output_owned, query_owned, keyval_owned, latent_owned, res_grad_ref, res_out_ref = take(6)
-    rest_cames, end_cames = take(n_rest), take(n_rest)
-    last_cames = take(n_last)
+    rest_owned, end_cames = take(n_rest), take(n_rest)
+    last_ends = take(2 * n_last)
     send_sems, recv_sems = take(2)
     sums = []
     copies = Copies(send_sems, recv_sems)
@@ -1593,14 +1647,14 @@
     space = take(5)
     latent_sum = SlotSum(copies, latent_values, (0, 1, 2), space[:3], space[3:])
     got_c, give_x, got_x = take(3)
-    latent_all, gain_rows, gain_c, gain_x, gain_columns, wide, end_one, end_two, end_sum, local_sems = take(10)
+    latent_all, gain_rows, gain_c, gain_x, gain_columns, wide, rest_came, end_sum, _, local_sems = take(10)
     copies.local_sems = local_sems
     copies.greet((0, 1, 2))
     last_a, last_b = take(2)
     out_ends = [copies.swapped(out_end_a, last_a, 0, 1024), copies.start(out_end_b, last_b, TENSOR, 1)]
-    rests = [copies.start(a, b, DP, 2) for a, b in zip(rest_refs, rest_cames)]
-    lasts = [copies.start(a, b, DP, 1) for a, b in zip(last_refs, last_cames)]
-    stays = [copies.local(stay_refs[g].at[1], end_one.at[g]) for g in range(n_rest)]
+    rest_rooms, last_rooms = take(2 * n_rest), take(2 * n_last)
+    rests = [Split(copies, *rest_pairs[2 * k : 2 * k + 2], *rest_rooms[2 * k : 2 * k + 2]) for k in range(n_rest)]
+    lasts = [Split(copies, *last_pairs[2 * k : 2 * k + 2], *last_rooms[2 * k : 2 * k + 2]) for k in range(n_last)]
     query_first, query_second, keyval_sum, output_sum = sums
     output_sum.got[0] = output_came
     output_sum.level = 1
@@ -1611,6 +1665,10 @@
     c_far.wait()
     give_x[0] = (part_ref[1].astype(F32) + got_c[1].astype(F32)).astype(BF16)
     x_far = copies.start(give_x, got_x, TENSOR, 1)
+    for k in range(n_rest):
+        rests[k].send(2, rest_came.at[pl.ds(2 * k, 2)])
+    for k in range(n_last):
+        lasts[k].send(1, last_ends[2 * k + 1], last_ends[2 * k])
     c_near.wait()
     query_first.wait()
     query_second.start()
@@ -1693,10 +1751,9 @@
     ends = []
     for g in range(n_rest):
         rests[g].wait()
-        stays[g].wait()
-        comes = copies.local(rest_cames[g].at[1], end_two.at[g])
-        comes.wait()
-        end_sum[g] = (end_one[g].astype(F32) + end_two[g].astype(F32)).astype(BF16)
+        own, over = rests[g].kept[0].astype(F32), rests[g].kept[1].astype(F32)
+        rest_owned[g][0] = (own + rest_came[2 * g].astype(F32)).astype(BF16)
+        end_sum[g] = (over + rest_came[2 * g + 1].astype(F32)).astype(BF16)
         ends.append(copies.start(end_sum.at[pl.ds(g, 1)], end_cames[g], DP, 1))
     keyval_sum.wait()
     output_sum.wait()
@@ -1721,7 +1778,7 @@
         copy.wait()
 
 
-def tail(part, wgrads, output_came, out_parts, saved, mid_grad, ffn_gain, rests, stays, lasts):
+def tail(part, wgrads, output_came, out_parts, saved, mid_grad, ffn_gain, rests, lasts):
     output_wgrad, query_wgrad, keyval_wgrad = wgrads
     rows = (160, D)
     latent = (64, KR + 128)
@@ -1734,14 +1791,14 @@
         like(rows),
     ]
     part_row = (160, D + KR + 128)
-    unit = rests[0].shape[1:]
+    unit = rests[0][0].shape[1:]
     rows_spec = pl.BlockSpec((160, 128), lambda i: (0, 0))
     results = pl.pallas_call(
         functools.partial(tail_kernel, len(rests), len(lasts)),
-        out_shape=shapes + [like((2, *unit))] * len(rests) + [like((1, *unit))] * (len(rests) + len(lasts)),
+        out_shape=shapes + [like((1, *unit))] * (2 * len(rests) + 2 * len(lasts)),
         grid=(1,),
-        in_specs=[VMEM_SPEC] * 18 + [rows_spec] * 2 + [ANY_SPEC] * (2 * len(rests) + len(lasts)),
-        out_specs=[VMEM_SPEC] * len(shapes) + [ANY_SPEC] * (2 * len(rests) + len(lasts)),
+        in_specs=[VMEM_SPEC] * 18 + [rows_spec] * 2 + [ANY_SPEC] * (2 * len(rests) + 2 * len(lasts)),
+        out_specs=[VMEM_SPEC] * (len(shapes) + len(rests)) + [ANY_SPEC] * (len(rests) + 2 * len(lasts)),
         scratch_shapes=[
             pltpu.SemaphoreType.DMA((40,)),
             pltpu.SemaphoreType.DMA((40,)),
@@ -1759,12 +1816,14 @@
             pltpu.VMEM((1, 8, D), F32),
             pltpu.VMEM((D, 128), F32),
             pltpu.VMEM((SLOT, KR + 128), F32),
-            pltpu.VMEM((3, *unit), BF16),
-            pltpu.VMEM((3, *unit), BF16),
-            pltpu.VMEM((3, *unit), BF16),
-            pltpu.SemaphoreType.DMA((8,)),
+            pltpu.VMEM((2 * len(rests), *unit), BF16),
+            pltpu.VMEM((len(rests), *unit), BF16),
+            pltpu.SemaphoreType.DMA((1,)),
+            pltpu.SemaphoreType.DMA((32,)),
             pltpu.VMEM((1, 160, 1024), BF16),
             pltpu.VMEM((1, 160, 1024), BF16),
+            *split_scratch(rests)[:-1],
+            *split_scratch(lasts)[:-1],
         ],
         compiler_params=pltpu.CompilerParams(
             collective_id=3, has_side_effects=True, vmem_limit_bytes=GIVEN_VMEM
@@ -1790,12 +1849,10 @@
         *out_parts,
         saved.cos,
         saved.sin,
-        *rests,
-        *stays,
-        *lasts,
+        *[v for keep, got, _ in rests + lasts for v in (keep, got)],
     )
     n = len(rests)
-    return results[:6], results[6 : 6 + n], results[6 + n : 6 + 2 * n], results[6 + 2 * n :]
+    return results[:6], results[6 : 6 + n], results[6 + n : 6 + 2 * n], list(zip(results[6 + 2 * n :: 2], results[7 + 2 * n :: 2]))
 
 
 def finish_kernel(
@@ -1955,32 +2012,27 @@
         [Cut(give0[2], 0), Cut(give1[0], 0), Cut(h0a, 2), Cut(h0b, 2)],
         7,
     )
-    (k0c, h0c), (k1a, h1a), (s0a, m0a), (s0b, m0b) = halve(
-        [(keep0[2], y0c), (keep1[0], y1a), (k0a, z0a), (k0b, z0b)]
-    )
     back = back.reshape(8, rows, D)
     out = out.reshape(8, rows, D)
-    (mid_grad, ffn_gain_part, attn_grad), (y1b, y1c, y2a, y2b, z0c, z1a, o0a, o0b) = back_tokens(
+    (mid_grad, ffn_gain_part, attn_grad), (y1b, y1c, y2a, y2b), split = back_tokens(
         back,
         saved.grad,
         saved.mid,
         saved.gains,
         saved.valid,
-        [(0, give1[1]), (0, give1[2]), (0, give2[0]), (0, give2[1]), (2, h0c), (2, h1a), (1, m0a), (1, m0b)],
-    )
-    (k1b, h1b), (k1c, h1c), (k2a, h2a), (k2b, h2b), (s0c, m0c), (s1a, m1a) = halve(
-        [(keep1[1], y1b), (keep1[2], y1c), (keep2[0], y2a), (keep2[1], y2b), (k0c, z0c), (k1a, z1a)]
-    )
-    (*wgrads, back_part, out_sum, out_a, out_b), (y2c, z1b, z1c, z2a, o0c, o1a, output_came) = attention_backward(
+        [(0, give1[1]), (0, give1[2]), (0, give2[0]), (0, give2[1])],
+        [(keep0[2], y0c, 2), (keep1[0], y1a, 2), (k0a, z0a, 1), (k0b, z0b, 1)],
+    )
+    (k0c, z0c), (k1a, z1a), over0a, over0b = split
+    (*wgrads, back_part, out_sum, out_a, out_b), (y2c, output_came), split = attention_backward(
         attn_grad,
         saved,
         out,
-        [(0, give2[2]), (2, h1b), (2, h1c), (2, h2a), (1, m0c), (1, m1a)],
-    )
-    (k2c, h2c), (s1b, m1b), (s1c, m1c), (s2a, m2a) = halve(
-        [(keep2[2], y2c), (k1b, z1b), (k1c, z1c), (k2a, z2a)]
-    )
-    (output_owned, query_owned, keyval_owned, latent_owned, res_grad, res_out), cames, ends, (o1b, o1c, o2a) = tail(
+        [(0, give2[2])],
+        [(keep1[1], y1b, 2), (keep1[2], y1c, 2), (keep2[0], y2a, 2), (k0c, z0c, 1), (k1a, z1a, 1)],
+    )
+    (k1b, z1b), (k1c, z1c), (k2a, z2a), over0c, over1a = split
+    (output_owned, query_owned, keyval_owned, latent_owned, res_grad, res_out), own2, over2, late = tail(
         back_part,
         wgrads,
         output_came,
@@ -1988,19 +2040,19 @@
         saved,
         mid_grad,
         ffn_gain_part,
-        [h2b, h2c],
-        [k2b, k2c],
-        [m1b, m1c, m2a],
-    )
+        [(keep2[1], y2b, 2), (keep2[2], y2c, 2)],
+        [(k1b, z1b, 1), (k1c, z1c, 1), (k2a, z2a, 1)],
+    )
+    ready = [over0a, over0b, over0c, over1a, *late]
     places = jnp.concatenate([dp ^ jnp.array(COLUMNS, jnp.int32), ((dp >> 1) & 1)[None]])
     res_out, res_grad, latent_owned, gains, expert_in, expert_out, shared_in, shared_out = finish(
         places,
         res_out,
         res_grad,
         latent_owned,
-        [s0a, s0b, s0c, s1a, s1b, s1c, s2a, k2b, k2c],
-        cames,
-        [o0a, o0b, o0c, o1a, o1b, o1c, o2a, *ends],
+        [mine for mine, _ in ready] + list(own2),
+        [],
+        [other for _, other in ready] + list(over2),
         width,
     )
     return (

time: 642 us -> 616 us (0.960)
  Pallas kernels: 625 us -> 600 us
    pallas_call x1, Pallas kernels: 234 us -> 220 us  [front(): pl.pallas_call(functools.partial(front_kernel, width), out_shape=shapes,...]
    pallas_call x4 -> x1, Pallas kernels: 14.9 us -> 2.94 us  [halve(): pl.pallas_call(functools.partial(halve_kernel, count), out_shape=shapes *...]
where the time goes in v4:
time: 616 us; the launch traced here: 613 us
  Pallas kernels  600 us (97%)
  local copies, waits for them, and re-layouts  11 us (2%)
    pallas_call x1, Pallas kernels, front(): pl.pallas_call(functools.partial(front_kernel, width), out_shape=shapes,...  220 us
    pallas_call x3, Pallas kernels, experts_step(): pl.pallas_call(functools.partial(experts_kernel, width, sums is not None,...  118 us
    pallas_call x1, Pallas kernels, tail(): pl.pallas_call(functools.partial(tail_kernel, len(rests), len(lasts)), ou...  114 us
    pallas_call x1, Pallas kernels, back_tokens(): pl.pallas_call(functools.partial(back_kernel, bits, tuple((bit for _, _,...  74.4 us
    pallas_call x1, Pallas kernels, attention_backward(): pl.pallas_call(functools.partial(attention_backward_kernel, bits, tuple((...  65 us

profile of v4, /device:TPU:0, one launch (start us, length us, event | category | flops | bytes accessed | tf_op | source)
XLA Modules:
  0.0 613.2 jit_solution(5278914100717974002)
XLA Ops:
  0.6 0.7 pad_bitcast_fusion
  1.3 0.1 copy.34
  1.4 0.8 copy.32
  2.2 0.8 copy.33
  2.9 1.6 concatenate.10
  5.2 220.0 %front.1 = (bf16[8,160,2048]{2,1,0:T(8,128)(2,1)}, f32[8,640]{1,0:T(8,128)}, bf16[4,1056,256]{2,1,0:T(8,128)(2,1)}, bf16[4,1056,256]{2,1,0:T(8,128)(2,1)}, bf16[...) custom-call(s32[1]{0:T(128)S(6)} %copy.38.count_ref, ...), custom_call_target="tpu_custom_call" | custom-call | flops 219999993856 | bytes 220000000 | tf_op jit(solution)/shard_map/front/pallas_call | solution.py:1050
  225.2 0.9 fusion
  226.1 0.1 concatenate.11
  226.2 0.6 fusion.2
  226.8 38.6 %experts_step.3 = (f32[1280,2048]{1,0:T(8,128)}, f32[1280,2048]{1,0:T(8,128)}, bf16[4,352,256]{2,1,0:T(8,128)(2,1)}, bf16[4,352,256]{2,1,0:T(8,128)(2,1)}, bf16[...) custom-call(bf16[1280,2048]{1,0:T(8,128)(2,1)} %bitcast.38, ...), custom_call_target="tpu_custom_call" | custom-call | flops 35000000512 | bytes 35000000 | tf_op jit(solution)/shard_map/experts_step/pallas_call | solution.py:1224
  265.5 40.1 %experts_step.4 = (f32[1280,2048]{1,0:T(8,128)}, f32[1280,2048]{1,0:T(8,128)}, bf16[4,352,256]{2,1,0:T(8,128)(2,1)}, bf16[4,352,256]{2,1,0:T(8,128)(2,1)}, bf16[...) custom-call(bf16[1280,2048]{1,0:T(8,128)(2,1)} %bitcast.39, ...), custom_call_target="tpu_custom_call" | custom-call | flops 35000000512 | bytes 35000000 | tf_op jit(solution)/shard_map/experts_step/pallas_call | solution.py:1224
  305.6 2.9 halve.1
  308.6 0.6 broadcast_in_dim_broadcast_in_dim.3.refs_2_
  309.1 39.1 %experts_step.5 = (bf16[1280,2048]{1,0:T(8,128)(2,1)}, bf16[1280,2048]{1,0:T(8,128)(2,1)}, bf16[4,352,256]{2,1,0:T(8,128)(2,1)}, bf16[4,352,256]{2,1,0:T(8,128)(...) custom-call(bf16[1280,2048]{1,0:T(8,128)(2,1)} %bitcast.40, ...), custom_call_target="tpu_custom_call" | custom-call | flops 35000000512 | bytes 35000000 | tf_op jit(solution)/shard_map/experts_step/pallas_call | solution.py:1224
  348.3 74.4 %back_tokens.1 = (f32[160,2048]{1,0:T(8,128)}, f32[8,2048]{1,0:T(8,128)}, bf16[4,160,2048]{2,1,0:T(8,128)(2,1)}, bf16[4,352,256]{2,1,0:T(8,128)(2,1)}, bf16[4,35...) custom-call(bf16[8,160,2048]{2,1,0:T(8,128)(2,1)} %bitcast.42, ...), custom_call_target="tpu_custom_call" | custom-call | flops 54999998464 | bytes 55000000 | tf_op jit(solution)/shard_map/back_tokens/pallas_call | solution.py:1381
  422.7 65.0 %attention_backward.1 = (bf16[8,512,256]{2,1,0:T(8,128)(2,1)}, bf16[8,256,768]{2,1,0:T(8,128)(2,1)}, bf16[8,64,1024]{2,1,0:T(8,128)(2,1)}, bf16[4,160,2688]{2,1,...) custom-call(bf16[4,160,2048]{2,1,0:T(8,128)(2,1)} %get-tuple-element, ...), custom_call_target="tpu_custom_call" | custom-call | flops 30000001024 | bytes 30000000 | tf_op jit(solution)/shard_map/attention_backward/pallas_call | solution.py:1532
  487.7 113.8 %tail.1 = (f32[512,256]{1,0:T(8,128)}, f32[256,768]{1,0:T(8,128)}, f32[64,1024]{1,0:T(8,128)}, f32[64,640]{1,0:T(8,128)}, f32[160,2048]{1,0:T(8,128)}, /*index=5...) custom-call(bf16[4,160,2688]{2,1,0:T(8,128)(2,1)} %get-tuple-element, ...), custom_call_target="tpu_custom_call" | custom-call | flops 109999996928 | bytes 110000000 | tf_op jit(solution)/shard_map/tail/pallas_call | solution.py:1796
  601.5 0.6 pad_add_fusion.places
  602.1 6.1 finish.1
  608.2 1.3 slice_bitcast_fusion
  609.5 1.2 slice_bitcast_fusion.1
  610.7 0.9 copy.39
  611.6 0.7 copy.40
  612.3 0.8 copy.41
  (11 shorter events, 0.0 us)
Async XLA Ops:
  487.6 113.8 %copy-start.3 = (s32[8]{0:T(128)S(1)}, s32[8]{0:T(128)}, u32[]{:S(2)}) copy-start(s32[8]{0:T(128)} %constant.20.clone) | copy-start | bytes 100
  602.1 8.6 %copy-start = (f32[256,768]{1,0:T(8,128)S(1)}, f32[256,768]{1,0:T(8,128)}, u32[]{:S(2)}) copy-start(f32[256,768]{1,0:T(8,128)} %get-tuple-element.298) | copy-start | bytes 2359300
  602.1 9.5 %copy-start.2 = (f32[64,1024]{1,0:T(8,128)S(1)}, f32[64,1024]{1,0:T(8,128)}, u32[]{:S(2)}) copy-start(f32[64,1024]{1,0:T(8,128)} %get-tuple-element.299) | copy-start | bytes 786436
  608.2 4.1 copy-start.1

commit v5 on v4

--- a/solution.py
+++ b/solution.py
@@ -703,6 +703,7 @@
     got_x = ((1, 160, D), BF16)
     gain_rows = ((KR, 128), BF16)
     masked = ((1, 160, D), BF16)
+    own_pack = ((1, 64, KR + 128), BF16)
     own_query = ((1, SLOT, 768), BF16)
 
 
@@ -730,7 +731,6 @@
 def front_kernel(
     width,
     count_ref,
-    pack_ref,
     keyval_ref,
     output_ref,
     expert_in,
@@ -744,6 +744,10 @@
     table_ref,
     slot_gates,
     frequency_ref,
+    latent_ref,
+    attn_gain_ref,
+    ffn_gain_ref,
+    latent_gain_ref,
     grad_pair,
     gates_over,
     *rest,
@@ -758,14 +762,25 @@
     send_sems, recv_sems, local_sems = rest[len(names) :]
     copies = Copies(send_sems, recv_sems, local_sems)
     places = Places()
-    copies.greet((0, 1, 2))
     saved = []
 
     def save(pick):
         for source, target in zip(pick(at), pick(outs)):
             saved.append(copies.local(source, target))
 
-    pack = SlotGather(copies, pack_ref, at.pack.at[0], FAR_FIRST)
+    at.own_pack[0] = jnp.zeros((64, KR + 128), BF16)
+    at.own_pack[0, :, : KR + RD] = latent_ref[...]
+    lane = lax.broadcasted_iota(jnp.int32, (64, 128), 1)
+    ends = at.own_pack[0, :, KR:].astype(F32)
+    for k, gain_ref in ((64, attn_gain_ref), (65, ffn_gain_ref)):
+        column = jnp.broadcast_to(gain_ref[...].astype(F32), (8, 64)).T[:, 0:1]
+        ends = jnp.where(lane == k, column, ends)
+    at.own_pack[0, :, KR:] = ends.astype(BF16)
+    column = jnp.broadcast_to(latent_gain_ref[...].astype(F32), (8, 16)).T[:, 0:1]
+    lane = lax.broadcasted_iota(jnp.int32, (16, 128), 1)
+    at.own_pack[0, 0:16, KR:] = jnp.where(lane == 66, column, ends[0:16]).astype(BF16)
+    pack = SlotGather(copies, at.own_pack, at.pack.at[0], FAR_FIRST)
+    copies.greet((0, 1, 2))
     keyval = SlotGather(copies, keyval_ref, at.keyval, FAR_FIRST)
     part = query_ref.shape[0] // 4
     queries = [
@@ -1023,14 +1038,13 @@
         copy.wait()
 
 
-def front(counts, pack, keyval, output, expert_in, expert_out, shared_in, shared_out, res, grad, query, segment, table, gates):
+def front(counts, latent, gains, keyval, output, expert_in, expert_out, shared_in, shared_out, res, grad, query, segment, table, gates):
     n_units, width = 3, expert_out.shape[1]
     half = (4, 3 * width, SLOT)
     frequency = ROPE_BASE ** (-np.arange(RD // 2, dtype=np.float32) / np.float32(RD // 2))
     frequency = jnp.asarray(np.tile(frequency.astype(np.float32), 4)[None])
     operands = [
         counts,
-        pack[None],
         keyval[None],
         output[None],
         expert_in.transpose(0, 1, 3, 2),
@@ -1044,13 +1058,15 @@
         table,
         gates,
         frequency,
+        latent,
+        *gains,
     ]
     shapes = [like((8, *res.shape)), like((8, TOK), F32)] + [like(half)] * (2 * n_units - 1) + [like((4, width, SLOT))]
     shapes += [like(*buffer) for buffer in buffers(Kept)]
     results = pl.pallas_call(
         functools.partial(front_kernel, width),
         out_shape=shapes,
-        in_specs=[SMEM_SPEC] + [ANY_SPEC] * 7 + [VMEM_SPEC] * 7,
+        in_specs=[SMEM_SPEC] + [ANY_SPEC] * 6 + [VMEM_SPEC] * 11,
         out_specs=[ANY_SPEC] * len(shapes),
         scratch_shapes=[pltpu.VMEM(*buffer) for buffer in buffers(Kept) + buffers(Landing)]
         + [
@@ -1151,6 +1167,7 @@
 
     @pl.when(step == 0)
     def _():
+        total[...] = jnp.zeros_like(total)
         copies.greet(sorted({cut.bit for cut in bits}), ())
         for flight in flights():
             flight.start()
@@ -1158,7 +1175,6 @@
             for j in range(count):
                 k = COLUMNS.index(UNIT_SLOTS[slot + j])
                 whole[start : start + size, lanes(k)] = ref[j, skip : skip + size]
-        total[...] = jnp.zeros_like(total)
 
     mid, grad = mid_ref[...], grad_ref[...]
     gate_up = nt(whole[: 2 * width], mid)
@@ -1857,7 +1873,6 @@
 
 def finish_kernel(
     n_came,
-    places,
     res_out_ref,
     res_grad_ref,
     latent_ref,
@@ -1866,14 +1881,21 @@
     refs = list(refs)
     take = lambda n: [refs.pop(0) for _ in range(n)]
     stays, cames, others = take(9), take(n_came), take(9)
-    res_out, res_grad, latent, gains, expert_in, expert_out, shared_in, shared_out = refs
+    passed = take(3)
+    res_out, res_grad, latent, attn_gain, ffn_gain, latent_gain, expert_in, expert_out, shared_in, shared_out, *out = refs
+    for source, target in zip(passed, out):
+        target[...] = source[...]
+    places = Places()
     for k in range(8):
         block = pl.ds(pl.multiple_of(places[k] * SLOT, SLOT), SLOT)
         res_out[:, block] = res_out_ref[:, lanes(k)]
         res_grad[:, block] = res_grad_ref[:, lanes(k)]
     latent[...] = latent_ref[:, : KR + RD]
-    gains[...] = latent_ref[:, KR : KR + 128].T[64:72]
-    side = places[8]
+    turned = latent_ref[:, KR : KR + 128].T
+    attn_gain[...] = turned[64:65]
+    ffn_gain[...] = turned[65:66]
+    latent_gain[...] = turned[66:67, : KR // 32]
+    side = places[12]
     n_half = expert_in.shape[0] // 2
     width = expert_out.shape[1]
     for p in range(n_half + 1):
@@ -1896,26 +1918,28 @@
                         shared_out[cut] = value
 
 
-def finish(places, res_out, res_grad, latent, stays, cames, others, width):
+def finish(res_out, res_grad, latent, stays, cames, others, passed, width):
     shapes = [
         like(res_out.shape),
         like(res_grad.shape, F32),
         like((64, KR + RD), F32),
-        like((8, 64), F32),
+        like((1, 64), F32),
+        like((1, 64), F32),
+        like((1, KR // 32), F32),
         like((EXPERTS, 2, width, SLOT), F32),
         like((EXPERTS, width, SLOT), F32),
         like((2, 2 * width, SLOT), F32),
         like((2 * width, SLOT), F32),
-    ]
+    ] + [like(array.shape, F32) for array in passed]
     return pl.pallas_call(
         functools.partial(finish_kernel, len(cames)),
         out_shape=shapes,
-        in_specs=[SMEM_SPEC] + [VMEM_SPEC] * (21 + len(cames)),
+        in_specs=[VMEM_SPEC] * (24 + len(cames)),
         out_specs=[VMEM_SPEC] * len(shapes),
         compiler_params=pltpu.CompilerParams(vmem_limit_bytes=GIVEN_VMEM),
         cost_estimate=cost(10),
         name="finish",
-    )(places, res_out, res_grad, latent, *stays, *cames, *others)
+    )(res_out, res_grad, latent, *stays, *cames, *others, *passed)
 
 
 def body(
@@ -1942,19 +1966,10 @@
     first = ((dp >> 1) & 1) == 0
     n_half = EXPERTS // 2
     width = w_expert_out.shape[1]
-    pack = jnp.concatenate(
-        [
-            w_latent,
-            attn_gain[:, None],
-            ffn_gain[:, None],
-            jnp.pad(latent_gain, (0, w_latent.shape[0] - latent_gain.shape[0]))[:, None],
-            jnp.zeros((w_latent.shape[0], 61), BF16),
-        ],
-        axis=1,
-    )
     grad_pair, over_gate, lows, highs, saved = front(
         tok_counts,
-        pack,
+        w_latent,
+        (attn_gain[None], ffn_gain[None], latent_gain[None]),
         w_keyval,
         w_output,
         w_expert_in,
@@ -2044,23 +2059,36 @@
         [(k1b, z1b, 1), (k1c, z1c, 1), (k2a, z2a, 1)],
     )
     ready = [over0a, over0b, over0c, over1a, *late]
-    places = jnp.concatenate([dp ^ jnp.array(COLUMNS, jnp.int32), ((dp >> 1) & 1)[None]])
-    res_out, res_grad, latent_owned, gains, expert_in, expert_out, shared_in, shared_out = finish(
-        places,
+    (
+        res_out,
+        res_grad,
+        latent_owned,
+        attn_gain,
+        ffn_gain,
+        latent_gain,
+        expert_in,
+        expert_out,
+        shared_in,
+        shared_out,
+        output_owned,
+        query_owned,
+        keyval_owned,
+    ) = finish(
         res_out,
         res_grad,
         latent_owned,
         [mine for mine, _ in ready] + list(own2),
         [],
         [other for _, other in ready] + list(over2),
+        [output_owned, query_owned, keyval_owned],
         width,
     )
     return (
         res_out,
         res_grad,
-        gains[0],
-        gains[2, : KR // 32],
-        gains[1],
+        attn_gain[0],
+        latent_gain[0],
+        ffn_gain[0],
         latent_owned,
         query_owned,
         keyval_owned,

time: 616 us -> 607 us (0.985)
  local copies, waits for them, and re-layouts: 11 us -> 2.22 us
where the time goes in v5:
time: 607 us; the launch traced here: 604 us
  Pallas kernels  600 us (99%)
    pallas_call x1, Pallas kernels, front(): pl.pallas_call(functools.partial(front_kernel, width), out_shape=shapes,...  220 us
    pallas_call x3, Pallas kernels, experts_step(): pl.pallas_call(functools.partial(experts_kernel, width, sums is not None,...  119 us
    pallas_call x1, Pallas kernels, tail(): pl.pallas_call(functools.partial(tail_kernel, len(rests), len(lasts)), ou...  113 us
    pallas_call x1, Pallas kernels, back_tokens(): pl.pallas_call(functools.partial(back_kernel, bits, tuple((bit for _, _,...  72.8 us
    pallas_call x1, Pallas kernels, attention_backward(): pl.pallas_call(functools.partial(attention_backward_kernel, bits, tuple((...  65.2 us

profile of v5, /device:TPU:0, one launch (start us, length us, event | category | flops | bytes accessed | tf_op | source)
XLA Modules:
  0.0 603.8 jit_solution(14096269035021107536)
XLA Ops:
  1.3 220.4 %front.1 = (bf16[8,160,2048]{2,1,0:T(8,128)(2,1)}, f32[8,640]{1,0:T(8,128)}, bf16[4,1056,256]{2,1,0:T(8,128)(2,1)}, bf16[4,1056,256]{2,1,0:T(8,128)(2,1)}, bf16[...) custom-call(s32[1]{0:T(128)S(6)} %copy.31.count_ref, ...), custom_call_target="tpu_custom_call" | custom-call | flops 219999993856 | bytes 220000000 | tf_op jit(solution)/shard_map/front/pallas_call | solution.py:1066
  221.7 0.9 fusion
  222.6 0.1 concatenate.3
  222.7 0.6 fusion.2
  223.4 39.0 %experts_step.3 = (f32[1280,2048]{1,0:T(8,128)}, f32[1280,2048]{1,0:T(8,128)}, bf16[4,352,256]{2,1,0:T(8,128)(2,1)}, bf16[4,352,256]{2,1,0:T(8,128)(2,1)}, bf16[...) custom-call(bf16[1280,2048]{1,0:T(8,128)(2,1)} %bitcast.32, ...), custom_call_target="tpu_custom_call" | custom-call | flops 35000000512 | bytes 35000000 | tf_op jit(solution)/shard_map/experts_step/pallas_call | solution.py:1240
  262.3 40.4 %experts_step.4 = (f32[1280,2048]{1,0:T(8,128)}, f32[1280,2048]{1,0:T(8,128)}, bf16[4,352,256]{2,1,0:T(8,128)(2,1)}, bf16[4,352,256]{2,1,0:T(8,128)(2,1)}, bf16[...) custom-call(bf16[1280,2048]{1,0:T(8,128)(2,1)} %bitcast.33, ...), custom_call_target="tpu_custom_call" | custom-call | flops 35000000512 | bytes 35000000 | tf_op jit(solution)/shard_map/experts_step/pallas_call | solution.py:1240
  302.8 2.9 halve.1
  305.7 0.6 broadcast_in_dim_broadcast_in_dim.3.refs_2_
  306.3 39.5 %experts_step.5 = (bf16[1280,2048]{1,0:T(8,128)(2,1)}, bf16[1280,2048]{1,0:T(8,128)(2,1)}, bf16[4,352,256]{2,1,0:T(8,128)(2,1)}, bf16[4,352,256]{2,1,0:T(8,128)(...) custom-call(bf16[1280,2048]{1,0:T(8,128)(2,1)} %bitcast.34, ...), custom_call_target="tpu_custom_call" | custom-call | flops 35000000512 | bytes 35000000 | tf_op jit(solution)/shard_map/experts_step/pallas_call | solution.py:1240
  345.8 72.8 %back_tokens.1 = (f32[160,2048]{1,0:T(8,128)}, f32[8,2048]{1,0:T(8,128)}, bf16[4,160,2048]{2,1,0:T(8,128)(2,1)}, bf16[4,352,256]{2,1,0:T(8,128)(2,1)}, bf16[4,35...) custom-call(bf16[8,160,2048]{2,1,0:T(8,128)(2,1)} %bitcast.36, ...), custom_call_target="tpu_custom_call" | custom-call | flops 54999998464 | bytes 55000000 | tf_op jit(solution)/shard_map/back_tokens/pallas_call | solution.py:1397
  418.6 65.2 %attention_backward.1 = (bf16[8,512,256]{2,1,0:T(8,128)(2,1)}, bf16[8,256,768]{2,1,0:T(8,128)(2,1)}, bf16[8,64,1024]{2,1,0:T(8,128)(2,1)}, bf16[4,160,2688]{2,1,...) custom-call(bf16[4,160,2048]{2,1,0:T(8,128)(2,1)} %get-tuple-element, ...), custom_call_target="tpu_custom_call" | custom-call | flops 30000001024 | bytes 30000000 | tf_op jit(solution)/shard_map/attention_backward/pallas_call | solution.py:1548
  483.8 112.8 %tail.1 = (f32[512,256]{1,0:T(8,128)}, f32[256,768]{1,0:T(8,128)}, f32[64,1024]{1,0:T(8,128)}, f32[64,640]{1,0:T(8,128)}, f32[160,2048]{1,0:T(8,128)}, /*index=5...) custom-call(bf16[4,160,2688]{2,1,0:T(8,128)(2,1)} %get-tuple-element, ...), custom_call_target="tpu_custom_call" | custom-call | flops 109999996928 | bytes 110000000 | tf_op jit(solution)/shard_map/tail/pallas_call | solution.py:1812
  596.6 7.0 %finish.1 = (bf16[160,2048]{1,0:T(8,128)(2,1)}, f32[160,2048]{1,0:T(8,128)}, f32[64,576]{1,0:T(8,128)}, f32[1,64]{1,0:T(1,128)}, f32[1,64]{1,0:T(1,128)}, /*inde...) custom-call(bf16[160,2048]{1,0:T(8,128)(2,1)} %get-tuple-element.236, ...), custom_call_target="tpu_custom_call" | custom-call | flops 10000000000 | bytes 10000000 | tf_op jit(solution)/shard_map/finish/pallas_call | solution.py:1934
  (1 shorter events, 0.0 us)

commit v6 on v5

--- a/solution.py
+++ b/solution.py
@@ -1137,10 +1137,11 @@
     return [like((keep.shape[0] // 2, *keep.shape[1:])) for keep, _, _ in splits for _ in range(2)]
 
 
-def experts_kernel(width, has_sum, bits, parts, *refs):
+def experts_kernel(width, has_sum, gated, bits, parts, *refs):
     refs = list(refs)
     take = lambda n: [refs.pop(0) for _ in range(n)]
-    mid_ref, grad_ref, gate_ref = take(3)
+    mid_ref, grad_ref = take(2)
+    gate_ref = take(1)[0] if gated else None
     unit_refs = take(len(parts))
     if has_sum:
         back_in, out_in = take(2)
@@ -1148,9 +1149,9 @@
     back_ref, out_ref = take(2)
     keep_refs, give_refs = take(3), take(3)
     targets = take(len(bits))
-    whole, total, send_sems, recv_sems = take(4)
+    whole, total, send_sems, recv_sems, local_sems = take(5)
     step = pl.program_id(0)
-    copies = Copies(send_sems, recv_sems)
+    copies = Copies(send_sems, recv_sems, local_sems)
 
     def flights():
         return [
@@ -1171,10 +1172,17 @@
         copies.greet(sorted({cut.bit for cut in bits}), ())
         for flight in flights():
             flight.start()
+        loads = []
         for ref, (slot, count, start, size, skip) in zip(unit_refs, parts):
             for j in range(count):
                 k = COLUMNS.index(UNIT_SLOTS[slot + j])
-                whole[start : start + size, lanes(k)] = ref[j, skip : skip + size]
+                loads.append(
+                    copies.local(
+                        ref.at[j, pl.ds(skip, size)], whole.at[pl.ds(start, size), pl.ds(k * SLOT, SLOT)]
+                    )
+                )
+        for load in loads:
+            load.wait()
 
     mid, grad = mid_ref[...], grad_ref[...]
     gate_up = nt(whole[: 2 * width], mid)
@@ -1184,9 +1192,11 @@
     sigma = 1.0 / (1.0 + jnp.exp(-gate))
     silu = gate * sigma
     slope = sigma * (1.0 + gate * (1.0 - sigma))
-    weight = gate_ref[...]
-    hidden_grad = hidden_grad * weight
-    hidden = (silu * up * weight).astype(BF16)
+    hidden = silu * up
+    if gated:
+        hidden_grad = hidden_grad * gate_ref[...]
+        hidden = hidden * gate_ref[...]
+    hidden = hidden.astype(BF16)
     pre = jnp.concatenate(
         [(hidden_grad * up * slope).astype(BF16), (hidden_grad * silu).astype(BF16)], axis=0
     )
@@ -1231,15 +1241,17 @@
     fixed = lambda *shape: pl.BlockSpec(shape, lambda i: (0,) * len(shape))
     kind = BF16 if last else F32
     part = (4, width, SLOT)
-    operands = [mid_pair, grad_pair, gate[None]] + [part[0] for part in unit]
-    specs = [rows, rows, pl.BlockSpec((1, block), lambda i: (0, i))]
-    specs += [fixed(*part[0].shape) for part in unit]
+    operands, specs = [mid_pair, grad_pair], [rows, rows]
+    if gate is not None:
+        operands, specs = operands + [gate[None]], specs + [pl.BlockSpec((1, block), lambda i: (0, i))]
+    operands += [part[0] for part in unit]
+    specs += [ANY_SPEC] * len(unit)
     if sums is not None:
         operands += list(sums)
         specs += [rows, rows]
     results = pl.pallas_call(
         functools.partial(
-            experts_kernel, width, sums is not None, tuple(freight), tuple(p[1:] for p in unit)
+            experts_kernel, width, sums is not None, gate is not None, tuple(freight), tuple(p[1:] for p in unit)
         ),
         grid=(tokens // block,),
         out_shape=[like((tokens, D), kind)] * 2
@@ -1252,6 +1264,7 @@
             pltpu.VMEM((3 * width, D), F32),
             pltpu.SemaphoreType.DMA((len(freight),)),
             pltpu.SemaphoreType.DMA((len(freight),)),
+            pltpu.SemaphoreType.DMA((24,)),
         ],
         compiler_params=pltpu.CompilerParams(
             collective_id=ident, has_side_effects=True, vmem_limit_bytes=GIVEN_VMEM
@@ -1989,7 +2002,6 @@
     pair_gate = jnp.where(first, pair_gate[:n_half], pair_gate[n_half : 2 * n_half])
     mid_pair = saved.mid_pair.reshape(-1, D)
     grad_pair = grad_pair.reshape(-1, D)
-    ones = jnp.ones_like(pair_gate[0])
     whole = 3 * width
     low, high = lows[2], highs[2]
     sums, keep0, give0, (high_far,) = experts_step(
@@ -2021,7 +2033,7 @@
             (high, 4, 4, 0, width, 0),
             (high_far, 4, 4, width, whole - width, 0),
         ],
-        ones,
+        None,
         sums,
         True,
         [Cut(give0[2], 0), Cut(give1[0], 0), Cut(h0a, 2), Cut(h0b, 2)],

time: 607 us -> 603 us (level)
  no operation moved by 1% of the time
where the time goes in v6:
time: 603 us; the launch traced here: 600 us
  Pallas kernels  597 us (99%)
    pallas_call x1, Pallas kernels, front(): pl.pallas_call(functools.partial(front_kernel, width), out_shape=shapes,...  219 us
    pallas_call x3, Pallas kernels, experts_step(): pl.pallas_call(functools.partial(experts_kernel, width, sums is not None,...  115 us
    pallas_call x1, Pallas kernels, tail(): pl.pallas_call(functools.partial(tail_kernel, len(rests), len(lasts)), ou...  114 us
    pallas_call x1, Pallas kernels, back_tokens(): pl.pallas_call(functools.partial(back_kernel, bits, tuple((bit for _, _,...  74.2 us
    pallas_call x1, Pallas kernels, attention_backward(): pl.pallas_call(functools.partial(attention_backward_kernel, bits, tuple((...  65 us

profile of v6, /device:TPU:0, one launch (start us, length us, event | category | flops | bytes accessed | tf_op | source)
XLA Modules:
  0.0 600.4 jit_solution(8174764258370023899)
XLA Ops:
  1.3 218.7 %front.1 = (bf16[8,160,2048]{2,1,0:T(8,128)(2,1)}, f32[8,640]{1,0:T(8,128)}, bf16[4,1056,256]{2,1,0:T(8,128)(2,1)}, bf16[4,1056,256]{2,1,0:T(8,128)(2,1)}, bf16[...) custom-call(s32[1]{0:T(128)S(6)} %copy.31.count_ref, ...), custom_call_target="tpu_custom_call" | custom-call | flops 219999993856 | bytes 220000000 | tf_op jit(solution)/shard_map/front/pallas_call | solution.py:1066
  220.0 0.9 fusion
  220.9 0.1 concatenate.3
  221.0 0.6 fusion.2
  221.6 38.5 %experts_step.3 = (f32[1280,2048]{1,0:T(8,128)}, f32[1280,2048]{1,0:T(8,128)}, bf16[4,352,256]{2,1,0:T(8,128)(2,1)}, bf16[4,352,256]{2,1,0:T(8,128)(2,1)}, bf16[...) custom-call(bf16[1280,2048]{1,0:T(8,128)(2,1)} %bitcast.32, ...), custom_call_target="tpu_custom_call" | custom-call | flops 35000000512 | bytes 35000000 | tf_op jit(solution)/shard_map/experts_step/pallas_call | solution.py:1252
  260.1 39.0 %experts_step.4 = (f32[1280,2048]{1,0:T(8,128)}, f32[1280,2048]{1,0:T(8,128)}, bf16[4,352,256]{2,1,0:T(8,128)(2,1)}, bf16[4,352,256]{2,1,0:T(8,128)(2,1)}, bf16[...) custom-call(bf16[1280,2048]{1,0:T(8,128)(2,1)} %bitcast.33, ...), custom_call_target="tpu_custom_call" | custom-call | flops 35000000512 | bytes 35000000 | tf_op jit(solution)/shard_map/experts_step/pallas_call | solution.py:1252
  299.2 2.9 halve.1
  302.1 37.9 %experts_step.5 = (bf16[1280,2048]{1,0:T(8,128)(2,1)}, bf16[1280,2048]{1,0:T(8,128)(2,1)}, bf16[4,352,256]{2,1,0:T(8,128)(2,1)}, bf16[4,352,256]{2,1,0:T(8,128)(...) custom-call(bf16[1280,2048]{1,0:T(8,128)(2,1)} %bitcast.34, ...), custom_call_target="tpu_custom_call" | custom-call | flops 35000000512 | bytes 35000000 | tf_op jit(solution)/shard_map/experts_step/pallas_call | solution.py:1252
  340.0 74.2 %back_tokens.1 = (f32[160,2048]{1,0:T(8,128)}, f32[8,2048]{1,0:T(8,128)}, bf16[4,160,2048]{2,1,0:T(8,128)(2,1)}, bf16[4,352,256]{2,1,0:T(8,128)(2,1)}, bf16[4,35...) custom-call(bf16[8,160,2048]{2,1,0:T(8,128)(2,1)} %bitcast.36, ...), custom_call_target="tpu_custom_call" | custom-call | flops 54999998464 | bytes 55000000 | tf_op jit(solution)/shard_map/back_tokens/pallas_call | solution.py:1410
  414.2 65.0 %attention_backward.1 = (bf16[8,512,256]{2,1,0:T(8,128)(2,1)}, bf16[8,256,768]{2,1,0:T(8,128)(2,1)}, bf16[8,64,1024]{2,1,0:T(8,128)(2,1)}, bf16[4,160,2688]{2,1,...) custom-call(bf16[4,160,2048]{2,1,0:T(8,128)(2,1)} %get-tuple-element, ...), custom_call_target="tpu_custom_call" | custom-call | flops 30000001024 | bytes 30000000 | tf_op jit(solution)/shard_map/attention_backward/pallas_call | solution.py:1561
  479.2 113.8 %tail.1 = (f32[512,256]{1,0:T(8,128)}, f32[256,768]{1,0:T(8,128)}, f32[64,1024]{1,0:T(8,128)}, f32[64,640]{1,0:T(8,128)}, f32[160,2048]{1,0:T(8,128)}, /*index=5...) custom-call(bf16[4,160,2688]{2,1,0:T(8,128)(2,1)} %get-tuple-element, ...), custom_call_target="tpu_custom_call" | custom-call | flops 109999996928 | bytes 110000000 | tf_op jit(solution)/shard_map/tail/pallas_call | solution.py:1825
  593.0 7.0 %finish.1 = (bf16[160,2048]{1,0:T(8,128)(2,1)}, f32[160,2048]{1,0:T(8,128)}, f32[64,576]{1,0:T(8,128)}, f32[1,64]{1,0:T(1,128)}, f32[1,64]{1,0:T(1,128)}, /*inde...) custom-call(bf16[160,2048]{1,0:T(8,128)(2,1)} %get-tuple-element.236, ...), custom_call_target="tpu_custom_call" | custom-call | flops 10000000000 | bytes 10000000 | tf_op jit(solution)/shard_map/finish/pallas_call | solution.py:1947
  (1 shorter events, 0.0 us)

commit v7 on v6

--- a/solution.py
+++ b/solution.py
@@ -1168,7 +1168,6 @@
 
     @pl.when(step == 0)
     def _():
-        total[...] = jnp.zeros_like(total)
         copies.greet(sorted({cut.bit for cut in bits}), ())
         for flight in flights():
             flight.start()
@@ -1181,6 +1180,7 @@
                         ref.at[j, pl.ds(skip, size)], whole.at[pl.ds(start, size), pl.ds(k * SLOT, SLOT)]
                     )
                 )
+        total[...] = jnp.zeros_like(total)
         for load in loads:
             load.wait()
 

time: 603 us -> 602 us (level)
  no operation moved by 1% of the time
where the time goes in v7:
time: 602 us; the launch traced here: 599 us
  Pallas kernels  595 us (99%)
    pallas_call x1, Pallas kernels, front(): pl.pallas_call(functools.partial(front_kernel, width), out_shape=shapes,...  219 us
    pallas_call x1, Pallas kernels, tail(): pl.pallas_call(functools.partial(tail_kernel, len(rests), len(lasts)), ou...  114 us
    pallas_call x3, Pallas kernels, experts_step(): pl.pallas_call(functools.partial(experts_kernel, width, sums is not None,...  114 us
    pallas_call x1, Pallas kernels, back_tokens(): pl.pallas_call(functools.partial(back_kernel, bits, tuple((bit for _, _,...  74.2 us
    pallas_call x1, Pallas kernels, attention_backward(): pl.pallas_call(functools.partial(attention_backward_kernel, bits, tuple((...  65 us

profile of v7, /device:TPU:0, one launch (start us, length us, event | category | flops | bytes accessed | tf_op | source)
XLA Modules:
  0.0 598.7 jit_solution(3993773333453347418)
XLA Ops:
  1.3 218.7 %front.1 = (bf16[8,160,2048]{2,1,0:T(8,128)(2,1)}, f32[8,640]{1,0:T(8,128)}, bf16[4,1056,256]{2,1,0:T(8,128)(2,1)}, bf16[4,1056,256]{2,1,0:T(8,128)(2,1)}, bf16[...) custom-call(s32[1]{0:T(128)S(6)} %copy.31.count_ref, ...), custom_call_target="tpu_custom_call" | custom-call | flops 219999993856 | bytes 220000000 | tf_op jit(solution)/shard_map/front/pallas_call | solution.py:1066
  220.0 0.9 fusion
  220.9 0.1 concatenate.3
  221.0 0.6 fusion.2
  221.6 37.9 %experts_step.3 = (f32[1280,2048]{1,0:T(8,128)}, f32[1280,2048]{1,0:T(8,128)}, bf16[4,352,256]{2,1,0:T(8,128)(2,1)}, bf16[4,352,256]{2,1,0:T(8,128)(2,1)}, bf16[...) custom-call(bf16[1280,2048]{1,0:T(8,128)(2,1)} %bitcast.32, ...), custom_call_target="tpu_custom_call" | custom-call | flops 35000000512 | bytes 35000000 | tf_op jit(solution)/shard_map/experts_step/pallas_call | solution.py:1252
  259.6 38.5 %experts_step.4 = (f32[1280,2048]{1,0:T(8,128)}, f32[1280,2048]{1,0:T(8,128)}, bf16[4,352,256]{2,1,0:T(8,128)(2,1)}, bf16[4,352,256]{2,1,0:T(8,128)(2,1)}, bf16[...) custom-call(bf16[1280,2048]{1,0:T(8,128)(2,1)} %bitcast.33, ...), custom_call_target="tpu_custom_call" | custom-call | flops 35000000512 | bytes 35000000 | tf_op jit(solution)/shard_map/experts_step/pallas_call | solution.py:1252
  298.1 2.9 halve.1
  301.0 37.3 %experts_step.5 = (bf16[1280,2048]{1,0:T(8,128)(2,1)}, bf16[1280,2048]{1,0:T(8,128)(2,1)}, bf16[4,352,256]{2,1,0:T(8,128)(2,1)}, bf16[4,352,256]{2,1,0:T(8,128)(...) custom-call(bf16[1280,2048]{1,0:T(8,128)(2,1)} %bitcast.34, ...), custom_call_target="tpu_custom_call" | custom-call | flops 35000000512 | bytes 35000000 | tf_op jit(solution)/shard_map/experts_step/pallas_call | solution.py:1252
  338.3 74.2 %back_tokens.1 = (f32[160,2048]{1,0:T(8,128)}, f32[8,2048]{1,0:T(8,128)}, bf16[4,160,2048]{2,1,0:T(8,128)(2,1)}, bf16[4,352,256]{2,1,0:T(8,128)(2,1)}, bf16[4,35...) custom-call(bf16[8,160,2048]{2,1,0:T(8,128)(2,1)} %bitcast.36, ...), custom_call_target="tpu_custom_call" | custom-call | flops 54999998464 | bytes 55000000 | tf_op jit(solution)/shard_map/back_tokens/pallas_call | solution.py:1410
  412.5 65.0 %attention_backward.1 = (bf16[8,512,256]{2,1,0:T(8,128)(2,1)}, bf16[8,256,768]{2,1,0:T(8,128)(2,1)}, bf16[8,64,1024]{2,1,0:T(8,128)(2,1)}, bf16[4,160,2688]{2,1,...) custom-call(bf16[4,160,2048]{2,1,0:T(8,128)(2,1)} %get-tuple-element, ...), custom_call_target="tpu_custom_call" | custom-call | flops 30000001024 | bytes 30000000 | tf_op jit(solution)/shard_map/attention_backward/pallas_call | solution.py:1561
  477.5 113.8 %tail.1 = (f32[512,256]{1,0:T(8,128)}, f32[256,768]{1,0:T(8,128)}, f32[64,1024]{1,0:T(8,128)}, f32[64,640]{1,0:T(8,128)}, f32[160,2048]{1,0:T(8,128)}, /*index=5...) custom-call(bf16[4,160,2688]{2,1,0:T(8,128)(2,1)} %get-tuple-element, ...), custom_call_target="tpu_custom_call" | custom-call | flops 109999996928 | bytes 110000000 | tf_op jit(solution)/shard_map/tail/pallas_call | solution.py:1825
  591.2 7.0 %finish.1 = (bf16[160,2048]{1,0:T(8,128)(2,1)}, f32[160,2048]{1,0:T(8,128)}, f32[64,576]{1,0:T(8,128)}, f32[1,64]{1,0:T(1,128)}, f32[1,64]{1,0:T(1,128)}, /*inde...) custom-call(bf16[160,2048]{1,0:T(8,128)(2,1)} %get-tuple-element.236, ...), custom_call_target="tpu_custom_call" | custom-call | flops 10000000000 | bytes 10000000 | tf_op jit(solution)/shard_map/finish/pallas_call | solution.py:1947
  (1 shorter events, 0.0 us)
